TPU v7x, 512 devices: a whole 4x8x8 slice. The times are simulated.
512 devices in a mesh: occ: 64 (over y, x, core), vir: 8 (over z).
Axes of the slice: x: 4, y: 8, z: 8, core: 2. Of those that a mesh axis runs over, the one named last changes fastest.
Arguments:
- amplitudes: bfloat16 [32768, 64, 128], P(('occ', 'vir')), may hold values from -6 to 6
- tile_list: int32 [32768, 4], P(('occ', 'vir')), may hold values from 0 to 399, as said below
- ladder_virtual_integrals: bfloat16 [32, 64, 64], P('vir'), may hold values from -0.75 to 0.75
- ladder_domain_integrals: bfloat16 [16, 128, 128], P('vir'), may hold values from -0.5 to 0.5
- cycle_virtual: bfloat16 [16, 128, 128], P('vir'), may hold values from -0.5 to 0.5
- cycle_occupied: bfloat16 [400, 128], replicated, may hold values from -5 to 5
- cycle_core: bfloat16 [128, 128], replicated, may hold values from -0.5 to 0.5
- occ_energy: float32 [400], replicated, may hold values from -1.5 to -0.5
- vir_energy: float32 [2048], replicated, may hold values from 0.25 to 2
Outputs:
- updated: bfloat16 [32768, 64, 128], P(('occ', 'vir'))
Inputs may be any that keep to these rules, and one draw needn't show every extreme that they name: `tile_list`: the tiles of device (o, v), rows (o * 8 + v) * 64 onward, have A from v * 4 to (v + 1) * 4 - 1 and g below 16; i and k lie below 400. Among one device's tiles at most 2 share the value of i modulo 64, and every device has such a value shared by exactly 2 of its tiles.
All inputs are finite; a program needn't handle non-finite values.
Results may differ from a plain program's by a relative error of at most 0.0057.
Values may be sent and summed in bfloat16 or wider, within the bound.
No kernel may reach another device: no remote copies, remote signals or barrier semaphores. Data moves between devices by JAX's collectives and lax.ppermute only.
A program may use at most 64 MiB of HBM per device.

v0:
```python
import jax
import jax.numpy as jnp
from jax import lax
from jax.sharding import PartitionSpec as P


def make_factors(cycle_virtual, cycle_occupied, second_occ, pair_domain):
    scaled = (
        cycle_virtual[pair_domain].astype(jnp.float32)
        * cycle_occupied[second_occ].astype(jnp.float32)[:, None, :]
    )
    return scaled.astype(jnp.bfloat16)


def group_sum(group_keys, values):
    slot_count = values.shape[0]
    same_group = ((group_keys[:, None] == group_keys[None, :]) & (group_keys[:, None] >= 0)).astype(
        jnp.bfloat16
    )
    summed = jnp.dot(same_group, values.reshape(slot_count, -1), preferred_element_type=jnp.float32)
    return summed.astype(jnp.bfloat16).reshape(values.shape)


def apply_core(grouped, cycle_core):
    cycle_rank = cycle_core.shape[0]
    result = jnp.dot(
        grouped.reshape(-1, cycle_rank), cycle_core, preferred_element_type=jnp.float32
    )
    return result.astype(jnp.bfloat16).reshape(grouped.shape)


def body(
    amplitudes,
    tile_list,
    ladder_virtual_integrals,
    ladder_domain_integrals,
    cycle_virtual,
    cycle_occupied,
    cycle_core,
    occ_energy,
    vir_energy,
):
    tile_count, tile_width, domain_width = amplitudes.shape
    owners = lax.axis_size("occ")
    capacity = 2 * tile_count // owners
    slot_count = owners * capacity
    vir_index = lax.axis_index("vir")
    local_tiles = ladder_virtual_integrals.shape[0]
    vir_tiles = vir_energy.shape[0] // tile_width
    first_occ = tile_list[:, 0]
    second_occ = tile_list[:, 1]
    virtual_tile = tile_list[:, 2]
    pair_domain = tile_list[:, 3]
    rightside_collected, virtual_all = (
        lax.all_gather(ladder_domain_integrals, "vir", axis=0, tiled=True),
        lax.all_gather(cycle_virtual, "vir", axis=0, tiled=True),
    )
    target = first_occ % owners
    one_hot = (target[:, None] == jnp.arange(owners, dtype=jnp.int32)[None, :]).astype(jnp.int32)
    slot_rank = jnp.sum(jnp.cumsum(one_hot, axis=0) * one_hot, axis=1) - 1
    position = target * capacity + slot_rank
    group_key = first_occ * vir_tiles + virtual_tile
    send_tiles = (
        jnp.zeros((slot_count, tile_width, domain_width), jnp.bfloat16).at[position].set(amplitudes)
    )
    tile_ids = jnp.stack([group_key, second_occ, pair_domain], axis=1)
    send_ids = jnp.full((slot_count, 3), -1, jnp.int32).at[position].set(tile_ids)
    got_tiles, got_ids = (
        lax.all_to_all(
            send_tiles.reshape(owners, capacity, tile_width, domain_width),
            "occ",
            split_axis=0,
            concat_axis=0,
            tiled=True,
        ),
        lax.all_to_all(
            send_ids.reshape(owners, capacity, 3), "occ", split_axis=0, concat_axis=0, tiled=True
        ),
    )
    slot_tiles = got_tiles.reshape(slot_count, tile_width, domain_width)
    slot_ids = got_ids.reshape(slot_count, 3)
    factors_per_slot = make_factors(
        virtual_all, cycle_occupied, jnp.maximum(slot_ids[:, 1], 0), jnp.maximum(slot_ids[:, 2], 0)
    )
    partial_value = jnp.einsum(
        "sac,scr->sar", slot_tiles, factors_per_slot, preferred_element_type=jnp.float32
    ).astype(jnp.bfloat16)
    grouped = group_sum(slot_ids[:, 0], partial_value)
    answer_messages = apply_core(grouped, cycle_core)
    slot_terms = jnp.einsum(
        "clx,cfx->clf", answer_messages, factors_per_slot, preferred_element_type=jnp.float32
    ).astype(jnp.bfloat16)
    returned = lax.all_to_all(
        slot_terms.reshape(owners, capacity, tile_width, domain_width),
        "occ",
        split_axis=0,
        concat_axis=0,
        tiled=True,
    )
    cycle_term = returned.reshape(slot_count, tile_width, domain_width)[position]
    midpoint_result = jnp.einsum(
        "fnd,fdg->fng",
        amplitudes,
        rightside_collected[pair_domain],
        preferred_element_type=jnp.float32,
    ).astype(jnp.bfloat16)
    leftside_tiles = ladder_virtual_integrals[virtual_tile - vir_index * local_tiles]
    ladder_contribution = jnp.einsum(
        "fnd,fdg->fng", leftside_tiles, midpoint_result, preferred_element_type=jnp.float32
    )
    rows_left = (
        virtual_tile[:, None] * tile_width + jnp.arange(tile_width, dtype=jnp.int32)[None, :]
    )
    rows_right = (
        pair_domain[:, None] * domain_width + jnp.arange(domain_width, dtype=jnp.int32)[None, :]
    )
    occ_sum = occ_energy[first_occ] + occ_energy[second_occ]
    denominator = (
        vir_energy[rows_left][:, :, None]
        + vir_energy[rows_right][:, None, :]
        - occ_sum[:, None, None]
    )
    result = (
        amplitudes.astype(jnp.float32)
        + (ladder_contribution + cycle_term.astype(jnp.float32)) / denominator
    )
    return result.astype(jnp.bfloat16)


def solution(mesh):
    return jax.shard_map(
        body,
        mesh=mesh,
        in_specs=(
            P(("occ", "vir"), None, None),
            P(("occ", "vir"), None),
            P("vir", None, None),
            P("vir", None, None),
            P("vir", None, None),
            P(),
            P(),
            P(),
            P(),
        ),
        out_specs=P(("occ", "vir"), None, None),
        check_vma=False,
    )
```

profile of v0, /device:TPU:2, one launch (start us, length us, event | category | flops | bytes accessed | tf_op | source)
XLA Modules:
  0.0 219.0 jit_solution(6701952026621541193)
XLA Ops:
  0.0 0.8 multiply_bitcast_fusion.1
  0.9 0.1 reduce_window_sum.11
  1.0 0.2 select_reduce_fusion
  1.2 0.1 copy.12
  1.3 1.3 scatter_custom_fusion
  2.6 10.7 %all-to-all-start = ((s32[64,2,3]{2,1,0:T(2,128)}), s32[64,2,3]{2,1,0:T(2,128)S(1)}, u32[]{:S(2)}, u32[]{:S(2)}) async-start(s32[64,2,3]{2,1,0:T(2,128)} %bitcast.5), calls=%async_computation | async-start | bytes 131072 | tf_op jit(solution)/shard_map/all_to_all | solution.py:76
  13.3 1.9 broadcast_in_dim.5
  15.2 8.1 %scatter_fusion = bf16[128,64,128]{2,1,0:T(8,128)(2,1)} fusion(bf16[128,64,128]{2,1,0:T(8,128)(2,1)} %broadcast_in_dim.5, s32[64]{0:T(128)S(1)} %fusion.20, bf16[64,64,128]{2,1,0:T(8,128)(2,1)S(1)} %copy-done.6), kind=kCustom, calls=%fused_computation.10 | custom fusion | bytes 3145984 | tf_op jit(solution)/shard_map/scatter | solution.py:64
  23.3 10.4 %all-to-all-start.1 = ((bf16[64,2,64,128]{3,2,1,0:T(8,128)(2,1)}), bf16[64,2,64,128]{3,2,1,0:T(8,128)(2,1)S(1)}, u32[]{:S(2)}, u32[]{:S(2)}) async-start(bf16[64,2,64,128]{3,2,1,0:T(8,128)(2,1)} %bitcast.9), calls=%async_computation.1 | async-start | bytes 4194304 | tf_op jit(solution)/shard_map/all_to_all | solution.py:69
  33.7 31.8 %all_gather.7 = bf16[16,128,128]{2,1,0:T(8,128)(2,1)S(1)} all-gather(bf16[2,128,128]{2,1,0:T(8,128)(2,1)S(1)} %copy-done.7), channel_id=1, replica_groups=mesh['occ'=64,'vir'=8] {'vir'}, dimensions={0}, use_global_device_ids=true | all-gather | bytes 589824 | tf_op jit(solution)/shard_map/all_gather | solution.py:56
  65.5 0.1 fusion.22
  65.7 0.1 copy.23
  65.8 0.7 gather_fusion.3
  66.6 3.1 %gather_fusion.2 = bf16[128,128,128]{2,1,0:T(8,128)(2,1)} fusion(bf16[16,128,128]{2,1,0:T(8,128)(2,1)S(1)} %all_gather.7, s32[1024]{0:T(1024)S(1)} %pad_clamp_fusion.4), kind=kCustom, calls=%fused_computation.2 | custom fusion | bytes 8389120 | tf_op jit(solution)/shard_map/gather | solution.py:9
  69.7 15.3 %all-to-all-done.1 = bf16[64,2,64,128]{3,2,1,0:T(8,128)(2,1)S(1)} async-done(((bf16[64,2,64,128]{3,2,1,0:T(8,128)(2,1)}), bf16[64,2,64,128]{3,2,1,0:T(8,128)(2,1)S(1)}, u32[]{:S(2)}, u32[]{:S(2)}) %all-to-all-start.1) | async-done | bytes 2097184 | tf_op jit(solution)/shard_map/all_to_all | solution.py:69
  85.0 3.4 %fusion.4 = bf16[128,64,128]{2,1,0:T(8,128)(2,1)S(1)} fusion(bf16[128,64,128]{2,1,0:T(8,128)(2,1)S(1)} %bitcast.51, bf16[128,128,128]{2,1,0:T(8,128)(2,1)} %gather_fusion.2, f32[128,128]{1,0:T(8,128)S(1)} %convert_element_type.46), kind=kOutput, calls=%fused_computation.19 | convolution fusion | flops 275775488 | bytes 8454144 | tf_op jit(solution)/shard_map/sac,scr->sar/dot_general | solution.py:85
  88.4 3.0 %convolution_convert_fusion.1 = bf16[128,8192]{1,0:T(8,128)(2,1)} fusion(bf16[16,8,64,128]{3,2,1,0:T(8,128)(2,1)S(1)} %bitcast.50, s32[128]{0:T(128)S(1)} %bitcast.55, pred[128]{0:T(512)(128)(4,1)S(1)} %compare_bitcast_fusion), kind=kOutput, calls=%fused_computation.12 | convolution fusion | flops 269516800 | bytes 4194944 | tf_op jit(solution)/shard_map/dot_general | solution.py:20
  91.4 2.9 %reshape_reshape.3 = bf16[8192,128]{1,0:T(8,128)(2,1)S(1)} reshape(bf16[128,8192]{1,0:T(8,128)(2,1)} %convolution_convert_fusion.1) | data formatting | bytes 4194304 | tf_op jit(solution)/shard_map/reshape;reshape | solution.py:27
  94.3 0.7 convolution_convert_fusion
  95.0 1.5 copy-done.3
  96.5 4.3 %fusion.5 = bf16[128,64,128]{2,1,0:T(8,128)(2,1)} fusion(bf16[128,64,128]{2,1,0:T(8,128)(2,1)S(1)} %bitcast.49, bf16[128,128,128]{2,1,0:T(8,128)(2,1)S(1)} %copy-done.3, f32[128,128]{1,0:T(8,128)S(1)} %convert_element_type.46), kind=kOutput, calls=%fused_computation.20 | convolution fusion | flops 275775488 | bytes 8454144 | tf_op jit(solution)/shard_map/clx,cfx->clf/dot_general | solution.py:90
  100.8 5.6 %all-to-all-start.2 = ((bf16[64,2,64,128]{3,2,1,0:T(8,128)(2,1)}), bf16[64,2,64,128]{3,2,1,0:T(8,128)(2,1)S(1)}, u32[]{:S(2)}, u32[]{:S(2)}) async-start(bf16[64,2,64,128]{3,2,1,0:T(8,128)(2,1)} %bitcast.14), calls=%async_computation.2 | async-start | bytes 4194304 | tf_op jit(solution)/shard_map/all_to_all | solution.py:93
  106.4 0.8 gather_fusion.7
  107.2 0.8 gather_fusion.8
  108.1 0.1 fusion.9
  108.2 45.5 %gather_fusion.6 = f32[8192]{0:T(1024)S(1)} fusion(f32[2048]{0:T(1024)S(1)} %copy-done.1, s32[8192]{0:T(1024)S(1)} %fusion.9), kind=kCustom, calls=%fused_computation.6 | custom fusion | bytes 98304 | tf_op jit(solution)/shard_map/gather | solution.py:120
  153.8 23.0 %gather_fusion.5 = f32[4096]{0:T(1024)S(1)} fusion(f32[2048]{0:T(1024)S(1)} %copy-done.1, s32[4096]{0:T(1024)S(1)} %broadcast_clamp_fusion), kind=kCustom, calls=%fused_computation.5 | custom fusion | bytes 49152 | tf_op jit(solution)/shard_map/gather | solution.py:119
  176.9 1.6 gather_fusion
  178.5 32.0 %all_gather.6 = bf16[16,128,128]{2,1,0:T(8,128)(2,1)S(1)} all-gather(bf16[2,128,128]{2,1,0:T(8,128)(2,1)S(1)} %copy-done.8), channel_id=1, replica_groups=mesh['occ'=64,'vir'=8] {'vir'}, dimensions={0}, use_global_device_ids=true | all-gather | bytes 589824 | tf_op jit(solution)/shard_map/all_gather | solution.py:55
  210.5 2.1 gather_fusion.1
  212.7 1.7 gather_fusion.4
  214.4 4.6 %add_convert_fusion = bf16[64,64,128]{2,1,0:T(8,128)(2,1)} fusion(bf16[64,64,128]{2,1,0:T(8,128)(2,1)} %gather_fusion.4, bf16[64,64,128]{2,1,0:T(8,128)(2,1)} %param.9, bf16[64,64,64]{2,1,0:T(8,128)(2,1)S(1)} %copy-done.5, bf16[64,128,128]{2,1,0:T(8,128)(2,1)} %gather_fusion.1, f32[64]{0:T(128)S(1)} %add.176, f32[64,128]{1,0:T(8,128)S(1)} %bitcast.54, ...), kind=kOutput, calls=%fused_computation.18 | convolution fusion | flops 206045184 | bytes 5816576 | tf_op jit(solution)/shard_map/fnd,fdg->fng/dot_general | solution.py:108
  (38 shorter events, 0.5 us)
Async XLA Ops:
  0.0 65.8 %copy-start = (bf16[400,128]{1,0:T(8,128)(2,1)S(1)}, bf16[400,128]{1,0:T(8,128)(2,1)}, u32[]{:S(2)}) copy-start(bf16[400,128]{1,0:T(8,128)(2,1)} %param.14) | copy-start | bytes 307204
  0.0 15.2 %copy-start.6 = (bf16[64,64,128]{2,1,0:T(8,128)(2,1)S(1)}, bf16[64,64,128]{2,1,0:T(8,128)(2,1)}, u32[]{:S(2)}) copy-start(bf16[64,64,128]{2,1,0:T(8,128)(2,1)} %param.9) | copy-start | bytes 3145732
  2.6 20.6 %all-to-all-start = ((s32[64,2,3]{2,1,0:T(2,128)}), s32[64,2,3]{2,1,0:T(2,128)S(1)}, u32[]{:S(2)}, u32[]{:S(2)}) async-start(s32[64,2,3]{2,1,0:T(2,128)} %bitcast.5), calls=%async_computation | async-start | bytes 131072 | tf_op jit(solution)/shard_map/all_to_all | solution.py:76
  23.3 10.4 %copy-start.7 = (bf16[2,128,128]{2,1,0:T(8,128)(2,1)S(1)}, bf16[2,128,128]{2,1,0:T(8,128)(2,1)}, u32[]{:S(2)}) copy-start(bf16[2,128,128]{2,1,0:T(8,128)(2,1)} %param.13) | copy-start | bytes 196612
  23.3 61.7 %all-to-all-start.1 = ((bf16[64,2,64,128]{3,2,1,0:T(8,128)(2,1)}), bf16[64,2,64,128]{3,2,1,0:T(8,128)(2,1)S(1)}, u32[]{:S(2)}, u32[]{:S(2)}) async-start(bf16[64,2,64,128]{3,2,1,0:T(8,128)(2,1)} %bitcast.9), calls=%async_computation.1 | async-start | bytes 4194304 | tf_op jit(solution)/shard_map/all_to_all | solution.py:69
  91.4 2.9 %copy-start.9 = (bf16[128,128]{1,0:T(8,128)(2,1)S(1)}, bf16[128,128]{1,0:T(8,128)(2,1)}, u32[]{:S(2)}) copy-start(bf16[128,128]{1,0:T(8,128)(2,1)} %param.15) | copy-start | bytes 98308
  94.3 2.2 copy-start.3
  100.8 5.6 %copy-start.2 = (f32[400]{0:T(512)S(1)}, f32[400]{0:T(512)}, u32[]{:S(2)}) copy-start(f32[400]{0:T(512)} %param.16) | copy-start | bytes 4804
  100.8 7.4 %copy-start.1 = (f32[2048]{0:T(1024)S(1)}, f32[2048]{0:T(1024)}, u32[]{:S(2)}) copy-start(f32[2048]{0:T(1024)} %param.17) | copy-start | bytes 24580
  100.8 111.9 %all-to-all-start.2 = ((bf16[64,2,64,128]{3,2,1,0:T(8,128)(2,1)}), bf16[64,2,64,128]{3,2,1,0:T(8,128)(2,1)S(1)}, u32[]{:S(2)}, u32[]{:S(2)}) async-start(bf16[64,2,64,128]{3,2,1,0:T(8,128)(2,1)} %bitcast.14), calls=%async_computation.2 | async-start | bytes 4194304 | tf_op jit(solution)/shard_map/all_to_all | solution.py:93
  153.8 23.1 %copy-start.4 = (bf16[4,64,64]{2,1,0:T(8,128)(2,1)S(1)}, bf16[4,64,64]{2,1,0:T(8,128)(2,1)}, u32[]{:S(2)}) copy-start(bf16[4,64,64]{2,1,0:T(8,128)(2,1)} %param.11) | copy-start | bytes 98308
  176.8 1.7 copy-start.8
  212.7 1.7 copy-start.5
where the time goes:
time: 220 us; the launch traced here: 219 us
  local copies, waits for them, and re-layouts  95.5 us (43%)
  blocking collectives  63.8 us (29%)
  starting transfers between devices  26.6 us (12%)
  matrix products  16 us (7%)
  waiting for transfers between devices  15.3 us (7%)
    gather x1, local copies, waits for them, and re-layouts, body(): vir_energy[rows_right][:, None, :]  45.5 us
    all_gather x1, blocking collectives, body(): lax.all_gather(ladder_domain_integrals, 'vir', axis=0, tiled=True)  32 us
    all_gather x1, blocking collectives, body(): lax.all_gather(cycle_virtual, 'vir', axis=0, tiled=True)  31.8 us
    gather x2, local copies, waits for them, and re-layouts, body(): vir_energy[rows_left][:, :, None] + vir_energy[rows_right][:, None, :]  23.1 us
    all_to_all x1, waiting for transfers between devices, body(): lax.all_to_all(send_tiles.reshape(owners, capacity, tile_width, domain_wi...  15.3 us
    all_to_all x1, starting transfers between devices, body(): lax.all_to_all(send_ids.reshape(owners, capacity, 3), 'occ', split_axis=0...  10.7 us
    all_to_all x1, starting transfers between devices, body(): lax.all_to_all(send_tiles.reshape(owners, capacity, tile_width, domain_wi...  10.4 us
    scatter x1, local copies, waits for them, and re-layouts, body(): jnp.zeros((slot_count, tile_width, domain_width), jnp.bfloat16).at[position]  8.11 us
  transfers between devices with their start and end apart: 3, of which 1 were waited for; matrix products, arithmetic and copies ran while one was open for 40% of the time, Pallas kernels for 0%

commit v1 on v0

v1 whole, which is shorter than its diff:
```python
import jax
import jax.numpy as jnp
from jax import lax
from jax.experimental import pallas as pl
from jax.experimental.pallas import tpu as pltpu
from jax.sharding import PartitionSpec as P

CAP = 2
META = 8
SMEM = pltpu.SMEM
VMEM = pltpu.VMEM


def sds(shape, dtype):
    return jax.ShapeDtypeStruct(shape, dtype)


def spec(space=VMEM):
    return pl.BlockSpec(memory_space=space)


def pack(amplitudes, tile_list, owners, local_tiles, empty_key):
    tiles, width, domain = amplitudes.shape
    rows = CAP * width

    def kernel(list_ref, amp_ref, out_ref, pos_ref, count, meta):
        out_ref[...] = jnp.zeros_like(out_ref)
        lane = lax.broadcasted_iota(jnp.int32, (1, domain), 1)
        empty = jnp.where(lax.broadcasted_iota(jnp.int32, meta.shape, 1) % 4 == 0, empty_key, 0)
        meta[...] = empty.astype(jnp.float32)

        def clear(o, carry):
            count[o] = 0
            return carry

        lax.fori_loop(0, owners, clear, 0, unroll=8)

        def place(t, carry):
            i = list_ref[t, 0]
            k = list_ref[t, 1]
            owner = lax.rem(i, owners)
            rank = count[owner]
            count[owner] = rank + 1
            pos_ref[t] = owner * CAP + rank
            key = lax.div(i, owners) * local_tiles + lax.rem(list_ref[t, 2], local_tiles)
            row = meta[pl.ds(owner * META, 1), :]
            field = lane - 4 * rank
            row = jnp.where(field == 0, key.astype(jnp.float32), row)
            row = jnp.where(field == 1, lax.div(k, 16).astype(jnp.float32), row)
            row = jnp.where(field == 2, lax.rem(k, 16).astype(jnp.float32), row)
            row = jnp.where(field == 3, list_ref[t, 3].astype(jnp.float32), row)
            meta[pl.ds(owner * META, 1), :] = row
            out_ref[owner, pl.ds(pl.multiple_of(rank * width, width), width), :] = amp_ref[t]
            return carry

        lax.fori_loop(0, tiles, place, 0, unroll=4)
        out_ref[:, rows:, :] = meta[...].reshape(owners, META, domain).astype(jnp.bfloat16)

    return pl.pallas_call(
        kernel,
        out_shape=(sds((owners, rows + META, domain), jnp.bfloat16), sds((tiles,), jnp.int32)),
        in_specs=[spec(SMEM), spec()],
        out_specs=(spec(), spec(SMEM)),
        scratch_shapes=[SMEM((owners,), jnp.int32), VMEM((owners * META, domain), jnp.float32)],
        name="pack",
    )(tile_list, amplitudes)


def owner_core(received, cycle_virtual, cycle_occupied, cycle_core, width, groups):
    sources, message, domain = received.shape
    rank = cycle_core.shape[0]
    rows = CAP * width

    def kernel(got_ref, cv_ref, co_ref, core_ref, out_ref, meta, ids_v, ids, sums, cores, sem):
        got_meta = got_ref[:, rows:, :].astype(jnp.float32)
        meta[...] = got_meta.reshape(meta.shape)
        ids_v[...] = meta[pl.ds(0, sources, stride=META), :].astype(jnp.int32)
        copy = pltpu.make_async_copy(ids_v, ids, sem)
        copy.start()
        sums[...] = jnp.zeros_like(sums)
        copy.wait()

        def add(s, carry):
            for c in range(CAP):
                key = ids[s, 4 * c]
                k = ids[s, 4 * c + 1] * 16 + ids[s, 4 * c + 2]
                g = ids[s, 4 * c + 3]
                tile = got_ref[s, c * width : (c + 1) * width, :]
                part = jnp.dot(tile, cv_ref[g], preferred_element_type=jnp.float32)
                part = part * co_ref[pl.ds(k, 1), :]
                sums[key] += part.astype(jnp.bfloat16).astype(jnp.float32)
            return carry

        lax.fori_loop(0, sources, add, 0, unroll=4)
        grouped = sums[...].astype(jnp.bfloat16).reshape((groups + 1) * width, rank)
        core = jnp.dot(grouped, core_ref[...], preferred_element_type=jnp.float32)
        cores[...] = core.astype(jnp.bfloat16).reshape(cores.shape)

        def answer(s, carry):
            for c in range(CAP):
                out_ref[s, c * width : (c + 1) * width, :] = cores[ids[s, 4 * c]]
            return carry

        lax.fori_loop(0, sources, answer, 0, unroll=4)

    return pl.pallas_call(
        kernel,
        out_shape=sds((sources, rows, rank), jnp.bfloat16),
        in_specs=[spec()] * 4,
        out_specs=spec(),
        scratch_shapes=[
            VMEM((sources * META, domain), jnp.float32),
            VMEM((sources, domain), jnp.int32),
            SMEM((sources, domain), jnp.int32),
            VMEM((groups + 1, width, rank), jnp.float32),
            VMEM((groups + 1, width, rank), jnp.bfloat16),
            pltpu.SemaphoreType.DMA,
        ],
        name="owner_core",
    )(received, cycle_virtual, cycle_occupied.astype(jnp.float32), cycle_core)


def ladder_part(tile_list, occ_energy, amplitudes, ladder_virtual, ladder_domain, row_energy, column_energy):
    tiles, width, domain = amplitudes.shape
    local_tiles = ladder_virtual.shape[0]

    def kernel(list_ref, occ_ref, amp_ref, lv_ref, ld_ref, re_ref, ce_ref, base_ref, inv_ref):
        def one(t, carry):
            a = lax.rem(list_ref[t, 2], local_tiles)
            g = list_ref[t, 3]
            amp = amp_ref[t]
            half = jnp.dot(amp, ld_ref[g], preferred_element_type=jnp.float32).astype(jnp.bfloat16)
            ladder = jnp.dot(lv_ref[a], half, preferred_element_type=jnp.float32)
            occ = occ_ref[list_ref[t, 0]] + occ_ref[list_ref[t, 1]]
            inverse = 1.0 / (re_ref[a] + ce_ref[pl.ds(g, 1), :] - occ)
            base_ref[t] = amp.astype(jnp.float32) + ladder * inverse
            inv_ref[t] = inverse
            return carry

        lax.fori_loop(0, tiles, one, 0, unroll=4)

    return pl.pallas_call(
        kernel,
        out_shape=(sds(amplitudes.shape, jnp.float32), sds(amplitudes.shape, jnp.float32)),
        in_specs=[spec(SMEM), spec(SMEM)] + [spec()] * 5,
        out_specs=(spec(), spec()),
        name="ladder",
    )(tile_list, occ_energy, amplitudes, ladder_virtual, ladder_domain, row_energy, column_energy)


def finish(tile_list, position, returned, cycle_virtual, cycle_occupied, base, inverse):
    tiles, width, domain = base.shape

    def kernel(list_ref, pos_ref, ret_ref, cv_ref, co_ref, base_ref, inv_ref, out_ref):
        def one(t, carry):
            slot = pos_ref[t]
            core = ret_ref[slot].astype(jnp.float32) * co_ref[pl.ds(list_ref[t, 1], 1), :]
            term = lax.dot_general(
                core.astype(jnp.bfloat16),
                cv_ref[list_ref[t, 3]],
                (((1,), (1,)), ((), ())),
                preferred_element_type=jnp.float32,
            )
            out_ref[t] = (base_ref[t] + term * inv_ref[t]).astype(jnp.bfloat16)
            return carry

        lax.fori_loop(0, tiles, one, 0, unroll=4)

    return pl.pallas_call(
        kernel,
        out_shape=sds(base.shape, jnp.bfloat16),
        in_specs=[spec(SMEM), spec(SMEM)] + [spec()] * 5,
        out_specs=spec(),
        name="finish",
    )(tile_list, position, returned, cycle_virtual, cycle_occupied.astype(jnp.float32), base, inverse)


def body(
    amplitudes,
    tile_list,
    ladder_virtual_integrals,
    ladder_domain_integrals,
    cycle_virtual,
    cycle_occupied,
    cycle_core,
    occ_energy,
    vir_energy,
):
    tiles, width, domain = amplitudes.shape
    owners = lax.axis_size("occ")
    local_tiles = ladder_virtual_integrals.shape[0]
    groups = -(-occ_energy.shape[0] // owners) * local_tiles
    vir_index = lax.axis_index("vir")
    local_energy = lax.dynamic_slice_in_dim(vir_energy, vir_index * local_tiles * width, local_tiles * width)
    row_energy = jnp.broadcast_to(local_energy.reshape(local_tiles, width, 1), (local_tiles, width, domain))
    column_energy = vir_energy.reshape(-1, domain)

    send, position = pack(amplitudes, tile_list, owners, local_tiles, groups)
    received = lax.all_to_all(send, "occ", split_axis=0, concat_axis=0, tiled=True)
    virtual_all = lax.all_gather(cycle_virtual, "vir", axis=0, tiled=True)
    answers = owner_core(received, virtual_all, cycle_occupied, cycle_core, width, groups)
    returned = lax.all_to_all(answers, "occ", split_axis=0, concat_axis=0, tiled=True)
    domain_own, _ = lax.optimization_barrier((ladder_domain_integrals, virtual_all))
    domain_all = lax.all_gather(domain_own, "vir", axis=0, tiled=True)
    base, inverse = ladder_part(
        tile_list, occ_energy, amplitudes, ladder_virtual_integrals, domain_all, row_energy, column_energy
    )
    return finish(
        tile_list,
        position,
        returned.reshape(owners * CAP, width, domain),
        virtual_all,
        cycle_occupied,
        base,
        inverse,
    )


def solution(mesh):
    tile_spec = P(("occ", "vir"), None, None)
    return jax.shard_map(
        body,
        mesh=mesh,
        in_specs=(tile_spec, P(("occ", "vir"), None), P("vir"), P("vir"), P("vir"), P(), P(), P(), P()),
        out_specs=tile_spec,
        check_vma=False,
    )
```

time: 220 us -> 146 us (0.66)
  the two profiles are of different devices: /device:TPU:2 before, /device:TPU:448 now
where the time goes in v1:
time: 146 us
  blocking collectives  54.7 us (37%)
  waiting for transfers between devices  34.2 us (23%)
  Pallas kernels  34 us (23%)
  starting transfers between devices  16.2 us (11%)
  local copies, waits for them, and re-layouts  5.7 us (4%)
    all_gather x1, blocking collectives, body(): virtual_all = lax.all_gather(cycle_virtual, 'vir', axis=0, tiled=True)  27.4 us
    all_gather x1, blocking collectives, body(): domain_all = lax.all_gather(domain_own, 'vir', axis=0, tiled=True)  27.3 us
    all_to_all x1, waiting for transfers between devices, body(): lax.all_to_all(send, 'occ', split_axis=0, concat_axis=0, tiled=True)  26.1 us
    pallas_call x1, Pallas kernels, ladder_part(): pl.pallas_call(kernel, out_shape=(sds(amplitudes.shape, jnp.float32), sds...  14.3 us
    all_to_all x1, starting transfers between devices, body(): lax.all_to_all(send, 'occ', split_axis=0, concat_axis=0, tiled=True)  10.7 us
    pallas_call x1, Pallas kernels, owner_core(): pl.pallas_call(kernel, out_shape=sds((sources, rows, rank), jnp.bfloat16)...  8.29 us
    all_to_all x1, waiting for transfers between devices, body(): lax.all_to_all(answers, 'occ', split_axis=0, concat_axis=0, tiled=True)  8.08 us
    pallas_call x1, Pallas kernels, finish(): pl.pallas_call(kernel, out_shape=sds(base.shape, jnp.bfloat16), in_specs=...  7.33 us
  transfers between devices with their start and end apart: 2, of which 2 were waited for; matrix products, arithmetic and copies ran while one was open for 2% of the time, Pallas kernels for 10%

profile of v1, /device:TPU:448, one launch (start us, length us, event | category | flops | bytes accessed | tf_op | source)
XLA Modules:
  0.0 145.5 jit_solution(9943120679938037981)
XLA Ops:
  0.0 1.4 copy.15.list_ref
  1.4 4.0 %pack.1 = (bf16[64,136,128]{2,1,0:T(8,128)(2,1)}, s32[64]{0:T(128)}) custom-call(s32[64,4]{1,0:T(8,128)} %copy.15.list_ref, bf16[64,64,128]{2,1,0:T(8,128)(2,1)} %amp_ref.3), custom_call_target="tpu_custom_call" | custom-call | tf_op jit(solution)/shard_map/pack/pallas_call | solution.py:59
  5.4 0.0 copy-start.2
  5.4 0.0 copy-start.3
  5.4 10.7 %all-to-all-start = ((bf16[64,136,128]{2,1,0:T(8,128)(2,1)}), bf16[64,136,128]{2,1,0:T(8,128)(2,1)S(1)}, u32[]{:S(2)}, u32[]{:S(2)}) async-start(bf16[64,136,128]{2,1,0:T(8,128)(2,1)} %get-tuple-element.11), calls=%async_computation | async-start | bytes 4456448 | tf_op jit(solution)/shard_map/all_to_all | solution.py:199
  16.2 0.0 copy-done.2
  16.2 0.7 convert_element_type.4.co_ref
  16.9 0.0 copy-done.3
  16.9 27.4 %all_gather.6.cv_ref = bf16[16,128,128]{2,1,0:T(8,128)(2,1)} all-gather(bf16[2,128,128]{2,1,0:T(8,128)(2,1)S(1)} %copy-done.3), channel_id=1, replica_groups=mesh['occ'=64,'vir'=8] {'vir'}, dimensions={0}, use_global_device_ids=true | all-gather | bytes 589824 | tf_op jit(solution)/shard_map/all_gather | solution.py:200
  44.2 26.1 %all-to-all-done.got_ref = bf16[64,136,128]{2,1,0:T(8,128)(2,1)S(1)} async-done(((bf16[64,136,128]{2,1,0:T(8,128)(2,1)}), bf16[64,136,128]{2,1,0:T(8,128)(2,1)S(1)}, u32[]{:S(2)}, u32[]{:S(2)}) %all-to-all-start) | async-done | bytes 2228256 | tf_op jit(solution)/shard_map/all_to_all | solution.py:199
  70.3 0.0 copy-start
  70.3 1.4 copy-done
  71.7 8.3 %owner_core.1 = bf16[64,128,128]{2,1,0:T(8,128)(2,1)} custom-call(bf16[64,136,128]{2,1,0:T(8,128)(2,1)} %copy-done, bf16[16,128,128]{2,1,0:T(8,128)(2,1)} %all_gather.6.cv_ref, f32[400,128]{1,0:T(8,128)} %convert_element_type.4.co_ref, bf16[128,128]{1,0:T(8,128)(2,1)} %core_ref.1), custom_call_target="tpu_custom_call" | custom-call | tf_op jit(solution)/shard_map/owner_core/pallas_call | solution.py:106
  80.0 0.0 copy-start.4
  80.0 5.5 %all-to-all-start.1 = ((bf16[64,128,128]{2,1,0:T(8,128)(2,1)}), bf16[64,128,128]{2,1,0:T(8,128)(2,1)S(1)}, u32[]{:S(2)}, u32[]{:S(2)}) async-start(bf16[64,128,128]{2,1,0:T(8,128)(2,1)} %owner_core.1), calls=%async_computation.1 | async-start | bytes 4194304 | tf_op jit(solution)/shard_map/all_to_all | solution.py:202
  85.5 0.8 dynamic_slice.3
  86.3 0.1 broadcast_in_dim.7
  86.4 0.0 copy-done.4
  86.4 27.3 %all_gather.7.ld_ref = bf16[16,128,128]{2,1,0:T(8,128)(2,1)} all-gather(bf16[2,128,128]{2,1,0:T(8,128)(2,1)S(1)} %copy-done.4), channel_id=1, replica_groups=mesh['occ'=64,'vir'=8] {'vir'}, dimensions={0}, use_global_device_ids=true | all-gather | bytes 589824 | tf_op jit(solution)/shard_map/all_gather | solution.py:204
  113.7 0.8 broadcast_in_dim.8.re_ref
  114.5 14.3 %ladder.1 = (f32[64,64,128]{2,1,0:T(8,128)}, f32[64,64,128]{2,1,0:T(8,128)}) custom-call(s32[64,4]{1,0:T(8,128)} %copy.15.list_ref, f32[400]{0:T(512)} %occ_ref.1, bf16[64,64,128]{2,1,0:T(8,128)(2,1)} %amp_ref.3, bf16[4,64,64]{2,1,0:T(8,128)(2,1)} %lv_ref.1, bf16[16,128,128]{2,1,0:T(8,128)(2,1)} %all_gather.7.ld_ref, f32[4,64,128]{2,1,0:T(8,128)} %broadcast_in_dim.8.re_ref, ...), custom_call_target="tpu_custom_call" | custom-call | tf_op jit(solution)/shard_map/ladder/pallas_call | solution.py:142
  128.8 8.1 %all-to-all-done.1 = bf16[64,128,128]{2,1,0:T(8,128)(2,1)S(1)} async-done(((bf16[64,128,128]{2,1,0:T(8,128)(2,1)}), bf16[64,128,128]{2,1,0:T(8,128)(2,1)S(1)}, u32[]{:S(2)}, u32[]{:S(2)}) %all-to-all-start.1) | async-done | bytes 2097184 | tf_op jit(solution)/shard_map/all_to_all | solution.py:202
  136.9 0.0 copy-start.1
  136.9 1.3 copy-done.1
  138.2 7.3 %finish.1 = bf16[64,64,128]{2,1,0:T(8,128)(2,1)} custom-call(s32[64,4]{1,0:T(8,128)} %copy.15.list_ref, s32[64]{0:T(128)} %get-tuple-element.10.pos_ref, bf16[128,64,128]{2,1,0:T(8,128)(2,1)} %bitcast.2, bf16[16,128,128]{2,1,0:T(8,128)(2,1)} %all_gather.6.cv_ref, f32[400,128]{1,0:T(8,128)} %convert_element_type.4.co_ref, ...), custom_call_target="tpu_custom_call" | custom-call | tf_op jit(solution)/shard_map/finish/pallas_call | solution.py:169
Async XLA Ops:
  5.4 10.7 %copy-start.2 = (bf16[400,128]{1,0:T(8,128)(2,1)S(1)}, bf16[400,128]{1,0:T(8,128)(2,1)}, u32[]{:S(2)}) copy-start(bf16[400,128]{1,0:T(8,128)(2,1)} %param.14) | copy-start | bytes 307204
  5.4 11.4 %copy-start.3 = (bf16[2,128,128]{2,1,0:T(8,128)(2,1)S(1)}, bf16[2,128,128]{2,1,0:T(8,128)(2,1)}, u32[]{:S(2)}) copy-start(bf16[2,128,128]{2,1,0:T(8,128)(2,1)} %param.13) | copy-start | bytes 196612
  5.4 64.9 %all-to-all-start = ((bf16[64,136,128]{2,1,0:T(8,128)(2,1)}), bf16[64,136,128]{2,1,0:T(8,128)(2,1)S(1)}, u32[]{:S(2)}, u32[]{:S(2)}) async-start(bf16[64,136,128]{2,1,0:T(8,128)(2,1)} %get-tuple-element.11), calls=%async_computation | async-start | bytes 4456448 | tf_op jit(solution)/shard_map/all_to_all | solution.py:199
  70.3 1.4 copy-start
  80.0 6.3 %copy-start.4 = (bf16[2,128,128]{2,1,0:T(8,128)(2,1)S(1)}, bf16[2,128,128]{2,1,0:T(8,128)(2,1)}, u32[]{:S(2)}) copy-start(bf16[2,128,128]{2,1,0:T(8,128)(2,1)} %param.12) | copy-start | bytes 196612
  80.0 56.8 %all-to-all-start.1 = ((bf16[64,128,128]{2,1,0:T(8,128)(2,1)}), bf16[64,128,128]{2,1,0:T(8,128)(2,1)S(1)}, u32[]{:S(2)}, u32[]{:S(2)}) async-start(bf16[64,128,128]{2,1,0:T(8,128)(2,1)} %owner_core.1), calls=%async_computation.1 | async-start | bytes 4194304 | tf_op jit(solution)/shard_map/all_to_all | solution.py:202
  136.9 1.3 copy-start.1

commit v2 on v1

v2 whole, which is shorter than its diff:
```python
import jax
import jax.numpy as jnp
from jax import lax
from jax.experimental import pallas as pl
from jax.experimental.pallas import tpu as pltpu
from jax.sharding import PartitionSpec as P

CAP = 2
META = 8
CHUNKS = 4
SMEM = pltpu.SMEM
VMEM = pltpu.VMEM


def sds(shape, dtype):
    return jax.ShapeDtypeStruct(shape, dtype)


def spec(space=VMEM):
    return pl.BlockSpec(memory_space=space)


def pack(amplitudes, tile_list, owners, local_tiles):
    tiles, width, domain = amplitudes.shape
    rows = CAP * width

    def kernel(list_ref, ids_ref, amp_ref, out_ref, pos_ref, count, meta, tile_sem, meta_sem):
        def clear(o, carry):
            count[o] = 0
            return carry

        lax.fori_loop(0, owners, clear, 0, unroll=8)

        def place(t, carry):
            owner = lax.rem(list_ref[0, t], owners)
            rank = count[owner]
            count[owner] = rank + 1
            pos_ref[t] = owner * CAP + rank
            slot = out_ref.at[owner, pl.ds(pl.multiple_of(rank * width, width), width)]
            pltpu.make_async_copy(amp_ref.at[t], slot, tile_sem).start()
            return carry

        lax.fori_loop(0, tiles, place, 0, unroll=4)
        ids = ids_ref[...]
        i, k = ids[0:1], ids[1:2]
        owner = jnp.broadcast_to(lax.rem(i, owners).astype(jnp.float32), (tiles, tiles))
        earlier = lax.broadcasted_iota(jnp.int32, (tiles, tiles), 0) < lax.broadcasted_iota(
            jnp.int32, (tiles, tiles), 1
        )
        same = jnp.where((owner == owner.T) & earlier, 1.0, 0.0)
        rank = jnp.sum(same, axis=0, keepdims=True)
        key = lax.div(i, owners) * local_tiles + lax.rem(ids[2:3], local_tiles) + 1
        fields = [v.astype(jnp.float32) for v in (key, lax.div(k, 16), lax.rem(k, 16), ids[3:4])]
        lane = lax.broadcasted_iota(jnp.int32, (domain, tiles), 0)
        row_owner = lax.broadcasted_iota(jnp.int32, (owners * META, tiles), 0) // META
        total = jnp.zeros((owners * META, domain), jnp.float32)
        for c in range(CAP):
            mine = (row_owner.astype(jnp.float32) == owner[0:1]) & (rank == float(c))
            table = jnp.zeros((domain, tiles), jnp.float32)
            for f, value in enumerate(fields):
                table = jnp.where(lane == 4 * c + f, value, table)
            total += lax.dot_general(
                jnp.where(mine, 1.0, 0.0).astype(jnp.bfloat16),
                table.astype(jnp.bfloat16),
                (((1,), (1,)), ((), ())),
                preferred_element_type=jnp.float32,
            )
        meta[...] = total.reshape(owners, META, domain).astype(jnp.bfloat16)
        meta_copy = pltpu.make_async_copy(meta, out_ref.at[:, pl.ds(rows, META)], meta_sem)
        meta_copy.start()
        meta_copy.wait()
        pltpu.make_async_copy(amp_ref, amp_ref, tile_sem).wait()

    return pl.pallas_call(
        kernel,
        out_shape=(sds((owners, rows + META, domain), jnp.bfloat16), sds((tiles,), jnp.int32)),
        in_specs=[spec(SMEM), spec(), spec(pl.ANY)],
        out_specs=(spec(pl.ANY), spec(SMEM)),
        scratch_shapes=[
            SMEM((owners,), jnp.int32),
            VMEM((owners, META, domain), jnp.bfloat16),
            pltpu.SemaphoreType.DMA,
            pltpu.SemaphoreType.DMA,
        ],
        name="pack",
    )(tile_list, tile_list, amplitudes)


def owner_core(received, cycle_virtual, cycle_occupied, cycle_core, width, groups):
    sources, message, domain = received.shape
    rank = cycle_core.shape[0]
    rows = CAP * width
    part = sources // CHUNKS

    def kernel(
        got_ref, cv_ref, co_ref, core_ref, out_ref, got, meta_b, meta, ids_v, ids, sums, cores, sem, meta_sem, out_sem
    ):
        meta_copy = pltpu.make_async_copy(got_ref.at[:, pl.ds(rows, META)], meta_b, meta_sem)
        meta_copy.start()
        copies = [
            pltpu.make_async_copy(
                got_ref.at[pl.ds(j * part, part), pl.ds(0, rows)], got.at[pl.ds(j * part, part)], sem.at[j]
            )
            for j in range(CHUNKS)
        ]
        for copy in copies:
            copy.start()
        sums[...] = jnp.zeros_like(sums)
        meta_copy.wait()
        meta[...] = meta_b[...].astype(jnp.float32).reshape(meta.shape)
        ids_v[...] = meta[pl.ds(0, sources, stride=META), :].astype(jnp.int32)
        ids_copy = pltpu.make_async_copy(ids_v, ids, meta_sem)
        ids_copy.start()
        ids_copy.wait()

        def add(s, carry):
            for c in range(CAP):
                key = ids[s, 4 * c]
                k = ids[s, 4 * c + 1] * 16 + ids[s, 4 * c + 2]
                g = ids[s, 4 * c + 3]
                tile = got[s, c * width : (c + 1) * width, :]
                one = jnp.dot(tile, cv_ref[g], preferred_element_type=jnp.float32)
                one = one * co_ref[pl.ds(k, 1), :]
                sums[key] += one.astype(jnp.bfloat16).astype(jnp.float32)
            return carry

        for j, copy in enumerate(copies):
            copy.wait()
            lax.fori_loop(j * part, (j + 1) * part, add, 0, unroll=4)
        grouped = sums[...].astype(jnp.bfloat16).reshape((groups + 1) * width, rank)
        core = jnp.dot(grouped, core_ref[...], preferred_element_type=jnp.float32)
        cores[...] = core.astype(jnp.bfloat16).reshape(cores.shape)

        def answer(s, carry):
            for c in range(CAP):
                slot = out_ref.at[s, pl.ds(c * width, width)]
                pltpu.make_async_copy(cores.at[ids[s, 4 * c]], slot, out_sem).start()
            return carry

        lax.fori_loop(0, sources, answer, 0, unroll=4)
        pltpu.make_async_copy(out_ref, out_ref, out_sem).wait()

    return pl.pallas_call(
        kernel,
        out_shape=sds((sources, rows, rank), jnp.bfloat16),
        in_specs=[spec(pl.ANY)] + [spec()] * 3,
        out_specs=spec(pl.ANY),
        scratch_shapes=[
            VMEM((sources, rows, domain), jnp.bfloat16),
            VMEM((sources, META, domain), jnp.bfloat16),
            VMEM((sources * META, domain), jnp.float32),
            VMEM((sources, domain), jnp.int32),
            SMEM((sources, domain), jnp.int32),
            VMEM((groups + 1, width, rank), jnp.float32),
            VMEM((groups + 1, width, rank), jnp.bfloat16),
            pltpu.SemaphoreType.DMA((CHUNKS,)),
            pltpu.SemaphoreType.DMA,
            pltpu.SemaphoreType.DMA,
        ],
        name="owner_core",
    )(received, cycle_virtual, cycle_occupied.astype(jnp.float32), cycle_core)


def ladder_part(tile_list, occ_energy, amplitudes, ladder_virtual, ladder_domain, row_energy, column_energy):
    tiles, width, domain = amplitudes.shape
    local_tiles = ladder_virtual.shape[0]

    def kernel(list_ref, occ_ref, amp_ref, lv_ref, ld_ref, re_ref, ce_ref, base_ref, inv_ref):
        def one(t, carry):
            a = lax.rem(list_ref[2, t], local_tiles)
            g = list_ref[3, t]
            amp = amp_ref[t]
            half = jnp.dot(amp, ld_ref[g], preferred_element_type=jnp.float32).astype(jnp.bfloat16)
            ladder = jnp.dot(lv_ref[a], half, preferred_element_type=jnp.float32)
            occ = occ_ref[list_ref[0, t]] + occ_ref[list_ref[1, t]]
            inverse = 1.0 / (re_ref[a] + ce_ref[pl.ds(g, 1), :] - occ)
            base_ref[t] = amp.astype(jnp.float32) + ladder * inverse
            inv_ref[t] = inverse
            return carry

        lax.fori_loop(0, tiles, one, 0, unroll=4)

    return pl.pallas_call(
        kernel,
        out_shape=(sds(amplitudes.shape, jnp.float32), sds(amplitudes.shape, jnp.float32)),
        in_specs=[spec(SMEM), spec(SMEM)] + [spec()] * 5,
        out_specs=(spec(), spec()),
        name="ladder",
    )(tile_list, occ_energy, amplitudes, ladder_virtual, ladder_domain, row_energy, column_energy)


def finish(tile_list, position, returned, cycle_virtual, cycle_occupied, base, inverse):
    tiles, width, domain = base.shape
    part = tiles // CHUNKS

    def kernel(
        list_ref, pos_ref, ret_ref, cv_ref, co_ref, base_ref, inv_ref, out_ref, core, base, inv, out, core_sem, sem, out_sem
    ):
        loads, stores = [], []
        for j in range(CHUNKS):
            piece = pl.ds(j * part, part)
            loads.append(
                (
                    pltpu.make_async_copy(base_ref.at[piece], base.at[piece], sem.at[j, 0]),
                    pltpu.make_async_copy(inv_ref.at[piece], inv.at[piece], sem.at[j, 1]),
                    pltpu.make_async_copy(ret_ref.at[piece], core.at[piece], core_sem.at[j]),
                )
            )
            stores.append(pltpu.make_async_copy(out.at[piece], out_ref.at[piece], out_sem.at[j]))

        for j in range(CHUNKS):

            def fetch(t, carry):
                pltpu.make_async_copy(ret_ref.at[pos_ref[t]], core.at[t], core_sem.at[j]).start()
                return carry

            lax.fori_loop(j * part, (j + 1) * part, fetch, 0, unroll=4)
            loads[j][0].start()
            loads[j][1].start()

        def one(t, carry):
            scaled = core[t].astype(jnp.float32) * co_ref[pl.ds(list_ref[1, t], 1), :]
            term = lax.dot_general(
                scaled.astype(jnp.bfloat16),
                cv_ref[list_ref[3, t]],
                (((1,), (1,)), ((), ())),
                preferred_element_type=jnp.float32,
            )
            out[t] = (base[t] + term * inv[t]).astype(jnp.bfloat16)
            return carry

        for j in range(CHUNKS):
            for copy in loads[j]:
                copy.wait()
            lax.fori_loop(j * part, (j + 1) * part, one, 0, unroll=4)
            stores[j].start()
        for copy in stores:
            copy.wait()

    return pl.pallas_call(
        kernel,
        out_shape=sds(base.shape, jnp.bfloat16),
        in_specs=[spec(SMEM), spec(SMEM), spec(pl.ANY), spec(), spec(), spec(pl.ANY), spec(pl.ANY)],
        out_specs=spec(pl.ANY),
        scratch_shapes=[
            VMEM((tiles, width, domain), jnp.bfloat16),
            VMEM((tiles, width, domain), jnp.float32),
            VMEM((tiles, width, domain), jnp.float32),
            VMEM((tiles, width, domain), jnp.bfloat16),
            pltpu.SemaphoreType.DMA((CHUNKS,)),
            pltpu.SemaphoreType.DMA((CHUNKS, 2)),
            pltpu.SemaphoreType.DMA((CHUNKS,)),
        ],
        name="finish",
    )(tile_list, position, returned, cycle_virtual, cycle_occupied.astype(jnp.float32), base, inverse)


def body(
    amplitudes,
    tile_list,
    ladder_virtual_integrals,
    ladder_domain_integrals,
    cycle_virtual,
    cycle_occupied,
    cycle_core,
    occ_energy,
    vir_energy,
):
    tiles, width, domain = amplitudes.shape
    owners = lax.axis_size("occ")
    local_tiles = ladder_virtual_integrals.shape[0]
    groups = -(-occ_energy.shape[0] // owners) * local_tiles
    vir_index = lax.axis_index("vir")
    local_energy = lax.dynamic_slice_in_dim(vir_energy, vir_index * local_tiles * width, local_tiles * width)
    row_energy = jnp.broadcast_to(local_energy.reshape(local_tiles, width, 1), (local_tiles, width, domain))
    column_energy = vir_energy.reshape(-1, domain)

    tile_list = tile_list.T
    send, position = pack(amplitudes, tile_list, owners, local_tiles)
    received = lax.all_to_all(send, "occ", split_axis=0, concat_axis=0, tiled=True)
    virtual_all = lax.all_gather(cycle_virtual, "vir", axis=0, tiled=True)
    answers = owner_core(received, virtual_all, cycle_occupied, cycle_core, width, groups)
    returned = lax.all_to_all(answers, "occ", split_axis=0, concat_axis=0, tiled=True)
    domain_own, _ = lax.optimization_barrier((ladder_domain_integrals, virtual_all))
    domain_all = lax.all_gather(domain_own, "vir", axis=0, tiled=True)
    base, inverse = ladder_part(
        tile_list, occ_energy, amplitudes, ladder_virtual_integrals, domain_all, row_energy, column_energy
    )
    return finish(
        tile_list,
        position,
        returned.reshape(owners * CAP, width, domain),
        virtual_all,
        cycle_occupied,
        base,
        inverse,
    )


def solution(mesh):
    tile_spec = P(("occ", "vir"), None, None)
    return jax.shard_map(
        body,
        mesh=mesh,
        in_specs=(tile_spec, P(("occ", "vir"), None), P("vir"), P("vir"), P("vir"), P(), P(), P(), P()),
        out_specs=tile_spec,
        check_vma=False,
    )
```

time: 146 us -> 175 us (1.20)
  Pallas kernels: 34 us -> 63.9 us
    pallas_call x1, Pallas kernels: 4.04 us -> 34.2 us  [pack(): pl.pallas_call(kernel, out_shape=(sds((owners, rows + META, domain), jnp....]
    unnamed x11 -> x10, local copies, waits for them, and re-layouts: 4.09 us -> 2.73 us
  transfers between devices with their start and end apart: 2 -> 2, of which waited for: 2 -> 2; matrix products, arithmetic and copies ran while one was open for 2% -> 1% of each run, Pallas kernels for 10% -> 8%
where the time goes in v2:
time: 175 us; the launch traced here: 174 us
  Pallas kernels  63.9 us (37%)
  blocking collectives  54.7 us (31%)
  waiting for transfers between devices  34.2 us (20%)
  starting transfers between devices  16.2 us (9%)
  local copies, waits for them, and re-layouts  4.33 us (2%)
    pallas_call x1, Pallas kernels, pack(): pl.pallas_call(kernel, out_shape=(sds((owners, rows + META, domain), jnp....  34.2 us
    all_gather x1, blocking collectives, body(): virtual_all = lax.all_gather(cycle_virtual, 'vir', axis=0, tiled=True)  27.4 us
    all_gather x1, blocking collectives, body(): domain_all = lax.all_gather(domain_own, 'vir', axis=0, tiled=True)  27.4 us
    all_to_all x1, waiting for transfers between devices, body(): lax.all_to_all(send, 'occ', split_axis=0, concat_axis=0, tiled=True)  26.1 us
    pallas_call x1, Pallas kernels, ladder_part(): pl.pallas_call(kernel, out_shape=(sds(amplitudes.shape, jnp.float32), sds...  14.3 us
    all_to_all x1, starting transfers between devices, body(): lax.all_to_all(send, 'occ', split_axis=0, concat_axis=0, tiled=True)  10.7 us
    pallas_call x1, Pallas kernels, owner_core(): pl.pallas_call(kernel, out_shape=sds((sources, rows, rank), jnp.bfloat16)...  8.75 us
    all_to_all x1, waiting for transfers between devices, body(): lax.all_to_all(answers, 'occ', split_axis=0, concat_axis=0, tiled=True)  8.07 us
  transfers between devices with their start and end apart: 2, of which 2 were waited for; matrix products, arithmetic and copies ran while one was open for 1% of the time, Pallas kernels for 8%

profile of v2, /device:TPU:448, one launch (start us, length us, event | category | flops | bytes accessed | tf_op | source)
XLA Modules:
  0.0 174.1 jit_solution(6441731394811890641)
XLA Ops:
  0.0 34.2 %pack.1 = (bf16[64,136,128]{2,1,0:T(8,128)(2,1)}, s32[64]{0:T(128)}) custom-call(s32[4,64]{1,0:T(4,128)} %bitcast.4, s32[4,64]{1,0:T(4,128)} %bitcast.5, bf16[64,64,128]{2,1,0:T(8,128)(2,1)} %amp_ref.3), custom_call_target="tpu_custom_call" | custom-call | tf_op jit(solution)/shard_map/pack/pallas_call | solution.py:74
  34.2 0.0 copy-start.2
  34.2 0.0 copy-start.3
  34.2 10.7 %all-to-all-start = ((bf16[64,136,128]{2,1,0:T(8,128)(2,1)}), bf16[64,136,128]{2,1,0:T(8,128)(2,1)S(1)}, u32[]{:S(2)}, u32[]{:S(2)}) async-start(bf16[64,136,128]{2,1,0:T(8,128)(2,1)} %get-tuple-element.11), calls=%async_computation | async-start | bytes 4456448 | tf_op jit(solution)/shard_map/all_to_all | solution.py:280
  45.0 0.0 copy-done.2
  45.0 0.7 convert_element_type.4.co_ref
  45.7 0.0 copy-done.3
  45.7 27.4 %all_gather.6.cv_ref = bf16[16,128,128]{2,1,0:T(8,128)(2,1)} all-gather(bf16[2,128,128]{2,1,0:T(8,128)(2,1)S(1)} %copy-done.3), channel_id=1, replica_groups=mesh['occ'=64,'vir'=8] {'vir'}, dimensions={0}, use_global_device_ids=true | all-gather | bytes 589824 | tf_op jit(solution)/shard_map/all_gather | solution.py:281
  73.0 26.1 %all-to-all-done.got_ref = bf16[64,136,128]{2,1,0:T(8,128)(2,1)S(1)} async-done(((bf16[64,136,128]{2,1,0:T(8,128)(2,1)}), bf16[64,136,128]{2,1,0:T(8,128)(2,1)S(1)}, u32[]{:S(2)}, u32[]{:S(2)}) %all-to-all-start) | async-done | bytes 2228256 | tf_op jit(solution)/shard_map/all_to_all | solution.py:280
  99.1 0.0 copy-start
  99.1 1.4 copy-done
  100.5 8.7 %owner_core.1 = bf16[64,128,128]{2,1,0:T(8,128)(2,1)} custom-call(bf16[64,136,128]{2,1,0:T(8,128)(2,1)} %copy-done, bf16[16,128,128]{2,1,0:T(8,128)(2,1)} %all_gather.6.cv_ref, f32[400,128]{1,0:T(8,128)} %convert_element_type.4.co_ref, bf16[128,128]{1,0:T(8,128)(2,1)} %core_ref.1), custom_call_target="tpu_custom_call" | custom-call | tf_op jit(solution)/shard_map/owner_core/pallas_call | solution.py:143
  109.3 0.0 copy-start.4
  109.3 5.5 %all-to-all-start.1 = ((bf16[64,128,128]{2,1,0:T(8,128)(2,1)}), bf16[64,128,128]{2,1,0:T(8,128)(2,1)S(1)}, u32[]{:S(2)}, u32[]{:S(2)}) async-start(bf16[64,128,128]{2,1,0:T(8,128)(2,1)} %owner_core.1), calls=%async_computation.1 | async-start | bytes 4194304 | tf_op jit(solution)/shard_map/all_to_all | solution.py:283
  114.8 0.8 dynamic_slice.3
  115.5 0.1 broadcast_in_dim.7
  115.6 0.0 copy-done.4
  115.6 27.4 %all_gather.7.ld_ref = bf16[16,128,128]{2,1,0:T(8,128)(2,1)} all-gather(bf16[2,128,128]{2,1,0:T(8,128)(2,1)S(1)} %copy-done.4), channel_id=1, replica_groups=mesh['occ'=64,'vir'=8] {'vir'}, dimensions={0}, use_global_device_ids=true | all-gather | bytes 589824 | tf_op jit(solution)/shard_map/all_gather | solution.py:285
  143.0 0.8 broadcast_in_dim.8.re_ref
  143.7 14.3 %ladder.1 = (f32[64,64,128]{2,1,0:T(8,128)}, f32[64,64,128]{2,1,0:T(8,128)}) custom-call(s32[4,64]{1,0:T(4,128)} %bitcast.6, f32[400]{0:T(512)} %occ_ref.1, bf16[64,64,128]{2,1,0:T(8,128)(2,1)} %amp_ref.3, bf16[4,64,64]{2,1,0:T(8,128)(2,1)} %lv_ref.1, bf16[16,128,128]{2,1,0:T(8,128)(2,1)} %all_gather.7.ld_ref, f32[4,64,128]{2,1,0:T(8,128)} %broadcast_in_dim.8.re_ref, ...), custom_call_target="tpu_custom_call" | custom-call | tf_op jit(solution)/shard_map/ladder/pallas_call | solution.py:183
  158.0 8.1 %all-to-all-done.1 = bf16[64,128,128]{2,1,0:T(8,128)(2,1)S(1)} async-done(((bf16[64,128,128]{2,1,0:T(8,128)(2,1)}), bf16[64,128,128]{2,1,0:T(8,128)(2,1)S(1)}, u32[]{:S(2)}, u32[]{:S(2)}) %all-to-all-start.1) | async-done | bytes 2097184 | tf_op jit(solution)/shard_map/all_to_all | solution.py:283
  166.1 0.0 copy-start.1
  166.1 1.3 copy-done.1
  167.4 6.6 %finish.1 = bf16[64,64,128]{2,1,0:T(8,128)(2,1)} custom-call(s32[4,64]{1,0:T(4,128)} %bitcast.7, s32[64]{0:T(128)} %get-tuple-element.10.pos_ref, bf16[128,64,128]{2,1,0:T(8,128)(2,1)} %bitcast.3, bf16[16,128,128]{2,1,0:T(8,128)(2,1)} %all_gather.6.cv_ref, f32[400,128]{1,0:T(8,128)} %convert_element_type.4.co_ref, ...), custom_call_target="tpu_custom_call" | custom-call | tf_op jit(solution)/shard_map/finish/pallas_call | solution.py:240
Async XLA Ops:
  34.2 10.7 %copy-start.2 = (bf16[400,128]{1,0:T(8,128)(2,1)S(1)}, bf16[400,128]{1,0:T(8,128)(2,1)}, u32[]{:S(2)}) copy-start(bf16[400,128]{1,0:T(8,128)(2,1)} %param.14) | copy-start | bytes 307204
  34.2 11.4 %copy-start.3 = (bf16[2,128,128]{2,1,0:T(8,128)(2,1)S(1)}, bf16[2,128,128]{2,1,0:T(8,128)(2,1)}, u32[]{:S(2)}) copy-start(bf16[2,128,128]{2,1,0:T(8,128)(2,1)} %param.13) | copy-start | bytes 196612
  34.2 64.9 %all-to-all-start = ((bf16[64,136,128]{2,1,0:T(8,128)(2,1)}), bf16[64,136,128]{2,1,0:T(8,128)(2,1)S(1)}, u32[]{:S(2)}, u32[]{:S(2)}) async-start(bf16[64,136,128]{2,1,0:T(8,128)(2,1)} %get-tuple-element.11), calls=%async_computation | async-start | bytes 4456448 | tf_op jit(solution)/shard_map/all_to_all | solution.py:280
  99.1 1.4 copy-start
  109.3 6.3 %copy-start.4 = (bf16[2,128,128]{2,1,0:T(8,128)(2,1)S(1)}, bf16[2,128,128]{2,1,0:T(8,128)(2,1)}, u32[]{:S(2)}) copy-start(bf16[2,128,128]{2,1,0:T(8,128)(2,1)} %param.12) | copy-start | bytes 196612
  109.3 56.8 %all-to-all-start.1 = ((bf16[64,128,128]{2,1,0:T(8,128)(2,1)}), bf16[64,128,128]{2,1,0:T(8,128)(2,1)S(1)}, u32[]{:S(2)}, u32[]{:S(2)}) async-start(bf16[64,128,128]{2,1,0:T(8,128)(2,1)} %owner_core.1), calls=%async_computation.1 | async-start | bytes 4194304 | tf_op jit(solution)/shard_map/all_to_all | solution.py:283
  166.1 1.3 copy-start.1

commit v3 on v2

v3 whole, which is shorter than its diff:
```python
import jax
import jax.numpy as jnp
from jax import lax
from jax.experimental import pallas as pl
from jax.experimental.pallas import tpu as pltpu
from jax.sharding import PartitionSpec as P

CAP = 2
META = 8
VMEM_LIMIT = 20 * 2**20
CHUNKS = 4
SMEM = pltpu.SMEM
VMEM = pltpu.VMEM


def sds(shape, dtype):
    return jax.ShapeDtypeStruct(shape, dtype)


def spec(space=VMEM):
    return pl.BlockSpec(memory_space=space)


def near(x):
    return pltpu.with_memory_space_constraint(x, pltpu.VMEM)


def far(x):
    return pltpu.with_memory_space_constraint(x, pltpu.HBM)


def params():
    return pltpu.CompilerParams(vmem_limit_bytes=VMEM_LIMIT)


def pack(amplitudes, tile_list, owners, local_tiles):
    tiles, width, domain = amplitudes.shape
    rows = CAP * width

    def kernel(list_ref, ids_ref, amp_ref, out_ref, pos_ref, count, amp, meta, load_sem, tile_sem, meta_sem):
        part = tiles // CHUNKS
        loads = []
        for j in range(CHUNKS):
            piece = pl.ds(j * part, part)
            loads.append(pltpu.make_async_copy(amp_ref.at[piece], amp.at[piece], load_sem.at[j]))
            loads[j].start()

        def clear(o, carry):
            count[o] = 0
            return carry

        lax.fori_loop(0, owners, clear, 0, unroll=8)

        def place(t, carry):
            owner = lax.rem(list_ref[0, t], owners)
            rank = count[owner]
            count[owner] = rank + 1
            pos_ref[t] = owner * CAP + rank
            slot = out_ref.at[owner, pl.ds(pl.multiple_of(rank * width, width), width)]
            pltpu.make_async_copy(amp.at[t], slot, tile_sem).start()
            return carry

        ids = ids_ref[...]
        i, k = ids[0:1], ids[1:2]
        owner = jnp.broadcast_to(lax.rem(i, owners).astype(jnp.float32), (tiles, tiles))
        earlier = lax.broadcasted_iota(jnp.int32, (tiles, tiles), 0) < lax.broadcasted_iota(
            jnp.int32, (tiles, tiles), 1
        )
        same = jnp.where((owner == owner.T) & earlier, 1.0, 0.0)
        rank = jnp.sum(same, axis=0, keepdims=True)
        key = lax.div(i, owners) * local_tiles + lax.rem(ids[2:3], local_tiles) + 1
        fields = [v.astype(jnp.float32) for v in (key, lax.div(k, 16), lax.rem(k, 16), ids[3:4])]
        lane = lax.broadcasted_iota(jnp.int32, (domain, tiles), 0)
        row_owner = lax.broadcasted_iota(jnp.int32, (owners * META, tiles), 0) // META
        total = jnp.zeros((owners * META, domain), jnp.float32)
        for c in range(CAP):
            mine = (row_owner.astype(jnp.float32) == owner[0:1]) & (rank == float(c))
            table = jnp.zeros((domain, tiles), jnp.float32)
            for f, value in enumerate(fields):
                table = jnp.where(lane == 4 * c + f, value, table)
            total += lax.dot_general(
                jnp.where(mine, 1.0, 0.0).astype(jnp.bfloat16),
                table.astype(jnp.bfloat16),
                (((1,), (1,)), ((), ())),
                preferred_element_type=jnp.float32,
            )
        meta[...] = total.reshape(owners, META, domain).astype(jnp.bfloat16)
        meta_copy = pltpu.make_async_copy(meta, out_ref.at[:, pl.ds(rows, META)], meta_sem)
        meta_copy.start()
        for j, load in enumerate(loads):
            load.wait()
            lax.fori_loop(j * part, (j + 1) * part, place, 0, unroll=4)
        meta_copy.wait()
        pltpu.make_async_copy(amp, amp_ref, tile_sem).wait()

    return pl.pallas_call(
        kernel,
        out_shape=(pltpu.HBM((owners, rows + META, domain), jnp.bfloat16), sds((tiles,), jnp.int32)),
        in_specs=[spec(SMEM), spec(), spec(pltpu.HBM)],
        out_specs=(spec(pltpu.HBM), spec(SMEM)),
        scratch_shapes=[
            SMEM((owners,), jnp.int32),
            VMEM((tiles, width, domain), jnp.bfloat16),
            VMEM((owners, META, domain), jnp.bfloat16),
            pltpu.SemaphoreType.DMA((CHUNKS,)),
            pltpu.SemaphoreType.DMA,
            pltpu.SemaphoreType.DMA,
        ],
        compiler_params=params(),
        name="pack",
    )(tile_list, tile_list, far(amplitudes))


def owner_core(received, cycle_virtual, cycle_occupied, cycle_core, width, groups):
    sources, message, domain = received.shape
    rank = cycle_core.shape[0]
    rows = CAP * width

    def kernel(got_ref, cv_ref, co_ref, core_ref, out_ref, meta, ids_v, ids, sums, cores, sem, out_sem):
        meta[...] = got_ref[:, rows:, :].astype(jnp.float32).reshape(meta.shape)
        ids_v[...] = meta[pl.ds(0, sources, stride=META), :].astype(jnp.int32)
        ids_copy = pltpu.make_async_copy(ids_v, ids, sem)
        ids_copy.start()
        sums[...] = jnp.zeros_like(sums)
        ids_copy.wait()

        def add(s, carry):
            for c in range(CAP):
                key = ids[s, 4 * c]
                k = ids[s, 4 * c + 1] * 16 + ids[s, 4 * c + 2]
                g = ids[s, 4 * c + 3]
                tile = got_ref[s, c * width : (c + 1) * width, :]
                one = jnp.dot(tile, cv_ref[g], preferred_element_type=jnp.float32)
                sums[key] += one * co_ref[pl.ds(k, 1), :]
            return carry

        lax.fori_loop(0, sources, add, 0, unroll=8)
        grouped = sums[...].astype(jnp.bfloat16).reshape((groups + 1) * width, rank)
        core = jnp.dot(grouped, core_ref[...], preferred_element_type=jnp.float32)
        cores[...] = core.astype(jnp.bfloat16).reshape(cores.shape)

        def answer(s, carry):
            for c in range(CAP):
                slot = out_ref.at[s, pl.ds(c * width, width)]
                pltpu.make_async_copy(cores.at[ids[s, 4 * c]], slot, out_sem).start()
            return carry

        lax.fori_loop(0, sources, answer, 0, unroll=4)
        pltpu.make_async_copy(out_ref, out_ref, out_sem).wait()

    return pl.pallas_call(
        kernel,
        out_shape=pltpu.HBM((sources, rows, rank), jnp.bfloat16),
        in_specs=[spec()] * 4,
        out_specs=spec(pltpu.HBM),
        scratch_shapes=[
            VMEM((sources * META, domain), jnp.float32),
            VMEM((sources, domain), jnp.int32),
            SMEM((sources, domain), jnp.int32),
            VMEM((groups + 1, width, rank), jnp.float32),
            VMEM((groups + 1, width, rank), jnp.bfloat16),
            pltpu.SemaphoreType.DMA,
            pltpu.SemaphoreType.DMA,
        ],
        compiler_params=params(),
        name="owner_core",
    )(near(received), near(cycle_virtual), near(cycle_occupied), near(cycle_core))


def inverse_denominator(tile_list, occ_energy, row_energy, column_energy):
    tiles = tile_list.shape[1]
    local_tiles, width, domain = row_energy.shape

    def kernel(list_ref, occ_ref, re_ref, ce_ref, inv_ref):
        def one(t, carry):
            a = lax.rem(list_ref[2, t], local_tiles)
            occ = occ_ref[list_ref[0, t]] + occ_ref[list_ref[1, t]]
            inv_ref[t] = 1.0 / (re_ref[a] + ce_ref[pl.ds(list_ref[3, t], 1), :] - occ)
            return carry

        lax.fori_loop(0, tiles, one, 0, unroll=4)

    return pl.pallas_call(
        kernel,
        out_shape=sds((tiles, width, domain), jnp.float32),
        in_specs=[spec(SMEM), spec(SMEM)] + [spec()] * 2,
        out_specs=spec(),
        compiler_params=params(),
        name="inverse",
    )(tile_list, occ_energy, row_energy, column_energy)


def ladder_part(tile_list, amplitudes, ladder_virtual, ladder_domain, inverse, cycle_virtual):
    tiles, width, domain = amplitudes.shape
    local_tiles = ladder_virtual.shape[0]
    domains = cycle_virtual.shape[0]

    def kernel(list_ref, amp_ref, lv_ref, ld_ref, inv_ref, cv_ref, base_ref, turned_ref, half):
        def first(t, carry):
            part = jnp.dot(amp_ref[t], ld_ref[list_ref[3, t]], preferred_element_type=jnp.float32)
            half[t] = part.astype(jnp.bfloat16)
            return carry

        lax.fori_loop(0, tiles, first, 0, unroll=8)

        def second(t, carry):
            a = lax.rem(list_ref[2, t], local_tiles)
            ladder = jnp.dot(lv_ref[a], half[t], preferred_element_type=jnp.float32)
            base_ref[t] = amp_ref[t].astype(jnp.float32) + ladder * inv_ref[t]
            return carry

        lax.fori_loop(0, tiles, second, 0, unroll=8)

        def turn(g, carry):
            turned_ref[g] = cv_ref[g].astype(jnp.float32).T.astype(jnp.bfloat16)
            return carry

        lax.fori_loop(0, domains, turn, 0, unroll=2)

    return pl.pallas_call(
        kernel,
        out_shape=(sds(amplitudes.shape, jnp.float32), sds(cycle_virtual.shape, jnp.bfloat16)),
        in_specs=[spec(SMEM)] + [spec()] * 5,
        out_specs=(spec(), spec()),
        scratch_shapes=[VMEM(amplitudes.shape, jnp.bfloat16)],
        compiler_params=params(),
        name="ladder",
    )(tile_list, amplitudes, ladder_virtual, ladder_domain, inverse, cycle_virtual)


def finish(tile_list, position, returned, cycle_turned, cycle_occupied, base, inverse):
    tiles, width, domain = base.shape
    part = tiles // CHUNKS

    def kernel(
        list_ref, pos_ref, ret_ref, cv_ref, co_ref, base_ref, inv_ref, out_ref, base, inv, out, sem, out_sem
    ):
        loads, stores = [], []
        for j in range(CHUNKS):
            piece = pl.ds(j * part, part)
            loads.append(
                (
                    pltpu.make_async_copy(base_ref.at[piece], base.at[piece], sem.at[j, 0]),
                    pltpu.make_async_copy(inv_ref.at[piece], inv.at[piece], sem.at[j, 1]),
                )
            )
            stores.append(pltpu.make_async_copy(out.at[piece], out_ref.at[piece], out_sem.at[j]))

        for pair in loads:
            for copy in pair:
                copy.start()

        def one(t, carry):
            row = pl.multiple_of(lax.rem(pos_ref[t], CAP) * width, width)
            scaled = ret_ref[lax.div(pos_ref[t], CAP), pl.ds(row, width), :].astype(jnp.float32) * co_ref[pl.ds(list_ref[1, t], 1), :]
            term = jnp.dot(scaled.astype(jnp.bfloat16), cv_ref[list_ref[3, t]], preferred_element_type=jnp.float32)
            out[t] = (base[t] + term * inv[t]).astype(jnp.bfloat16)
            return carry

        for j in range(CHUNKS):
            for copy in loads[j]:
                copy.wait()
            lax.fori_loop(j * part, (j + 1) * part, one, 0, unroll=4)
            stores[j].start()
        for copy in stores:
            copy.wait()

    return pl.pallas_call(
        kernel,
        out_shape=sds(base.shape, jnp.bfloat16),
        in_specs=[spec(SMEM), spec(SMEM), spec(), spec(), spec(), spec(pltpu.HBM), spec(pltpu.HBM)],
        out_specs=spec(pltpu.HBM),
        scratch_shapes=[
            VMEM((tiles, width, domain), jnp.float32),
            VMEM((tiles, width, domain), jnp.float32),
            VMEM((tiles, width, domain), jnp.bfloat16),
            pltpu.SemaphoreType.DMA((CHUNKS, 2)),
            pltpu.SemaphoreType.DMA((CHUNKS,)),
        ],
        compiler_params=params(),
        name="finish",
    )(tile_list, position, near(returned), cycle_turned, cycle_occupied, far(base), far(inverse))


def body(
    amplitudes,
    tile_list,
    ladder_virtual_integrals,
    ladder_domain_integrals,
    cycle_virtual,
    cycle_occupied,
    cycle_core,
    occ_energy,
    vir_energy,
):
    tiles, width, domain = amplitudes.shape
    owners = lax.axis_size("occ")
    local_tiles = ladder_virtual_integrals.shape[0]
    groups = -(-occ_energy.shape[0] // owners) * local_tiles
    vir_index = lax.axis_index("vir")
    local_energy = lax.dynamic_slice_in_dim(vir_energy, vir_index * local_tiles * width, local_tiles * width)
    row_energy = jnp.broadcast_to(local_energy.reshape(local_tiles, width, 1), (local_tiles, width, domain))
    column_energy = vir_energy.reshape(-1, domain)

    tile_list = tile_list.T
    cycle_occupied = cycle_occupied.astype(jnp.float32)
    send, position = pack(amplitudes, tile_list, owners, local_tiles)
    received = lax.all_to_all(send, "occ", split_axis=0, concat_axis=0, tiled=True)
    virtual_all = lax.all_gather(cycle_virtual, "vir", axis=0, tiled=True)
    row_energy, _ = lax.optimization_barrier((row_energy, virtual_all))
    inverse = inverse_denominator(tile_list, occ_energy, row_energy, column_energy)
    inverse, virtual_all = lax.optimization_barrier((inverse, virtual_all))
    answers = owner_core(received, virtual_all, cycle_occupied, cycle_core, width, groups)
    returned = lax.all_to_all(answers, "occ", split_axis=0, concat_axis=0, tiled=True)
    domain_own, _ = lax.optimization_barrier((ladder_domain_integrals, virtual_all))
    domain_all = lax.all_gather(domain_own, "vir", axis=0, tiled=True)
    base, turned = ladder_part(
        tile_list, amplitudes, ladder_virtual_integrals, domain_all, inverse, virtual_all
    )
    return finish(tile_list, position, returned, turned, cycle_occupied, base, inverse)


def solution(mesh):
    tile_spec = P(("occ", "vir"), None, None)
    return jax.shard_map(
        body,
        mesh=mesh,
        in_specs=(tile_spec, P(("occ", "vir"), None), P("vir"), P("vir"), P("vir"), P(), P(), P(), P()),
        out_specs=tile_spec,
        check_vma=False,
    )
```

time: 175 us -> 140 us (0.80)
  Pallas kernels: 63.9 us -> 21.9 us
  waiting for transfers between devices: 34.2 us -> 45.7 us
  blocking collectives: 54.7 us -> 50.9 us
    pallas_call x2 -> x3, Pallas kernels: 43 us -> 11.1 us  [the longest x1 6.68 us: owner_core(): pl.pallas_call(kernel, out_shape=pltpu.HBM((sources, rows, rank), jnp.bfl...]
    all_to_all x1, waiting for transfers between devices: 8.07 us -> 18.7 us  [body(): lax.all_to_all(answers, 'occ', split_axis=0, concat_axis=0, tiled=True)]
    pallas_call x1, Pallas kernels: 14.3 us -> 4.4 us  [ladder_part(): pl.pallas_call(kernel, out_shape=(sds(amplitudes.shape, jnp.float32), sds...]
    all_gather x1, blocking collectives: 27.4 us -> 25.5 us  [body(): virtual_all = lax.all_gather(cycle_virtual, 'vir', axis=0, tiled=True)]
    all_gather x1, blocking collectives: 27.4 us -> 25.5 us  [body(): domain_all = lax.all_gather(domain_own, 'vir', axis=0, tiled=True)]
  transfers between devices with their start and end apart: 2 -> 2, of which waited for: 2 -> 2; matrix products, arithmetic and copies ran while one was open for 1% -> 0% of each run, Pallas kernels for 8% -> 4%
where the time goes in v3:
time: 140 us; the launch traced here: 139 us
  blocking collectives  50.9 us (36%)
  waiting for transfers between devices  45.7 us (33%)
  Pallas kernels  21.9 us (16%)
  starting transfers between devices  16.6 us (12%)
  local copies, waits for them, and re-layouts  3.59 us (3%)
    all_to_all x1, waiting for transfers between devices, body(): lax.all_to_all(send, 'occ', split_axis=0, concat_axis=0, tiled=True)  27 us
    all_gather x1, blocking collectives, body(): domain_all = lax.all_gather(domain_own, 'vir', axis=0, tiled=True)  25.5 us
    all_gather x1, blocking collectives, body(): virtual_all = lax.all_gather(cycle_virtual, 'vir', axis=0, tiled=True)  25.5 us
    all_to_all x1, waiting for transfers between devices, body(): lax.all_to_all(answers, 'occ', split_axis=0, concat_axis=0, tiled=True)  18.7 us
    all_to_all x1, starting transfers between devices, body(): lax.all_to_all(send, 'occ', split_axis=0, concat_axis=0, tiled=True)  10.9 us
    pallas_call x1, Pallas kernels, owner_core(): pl.pallas_call(kernel, out_shape=pltpu.HBM((sources, rows, rank), jnp.bfl...  6.68 us
    pallas_call x1, Pallas kernels, finish(): pl.pallas_call(kernel, out_shape=sds(base.shape, jnp.bfloat16), in_specs=...  6.35 us
    all_to_all x1, starting transfers between devices, body(): lax.all_to_all(answers, 'occ', split_axis=0, concat_axis=0, tiled=True)  5.72 us
  transfers between devices with their start and end apart: 2, of which 2 were waited for; matrix products, arithmetic and copies ran while one was open for 0% of the time, Pallas kernels for 4%

profile of v3, /device:TPU:448, one launch (start us, length us, event | category | flops | bytes accessed | tf_op | source)
XLA Modules:
  0.0 138.9 jit_solution(12659477795094738475)
XLA Ops:
  0.0 0.7 copy-done.4
  0.7 3.2 %pack.1 = (bf16[64,136,128]{2,1,0:T(8,128)(2,1)}, s32[64]{0:T(128)S(1)}) custom-call(s32[4,64]{1,0:T(4,128)S(1)} %bitcast.2, s32[4,64]{1,0:T(4,128)S(1)} %bitcast.3, bf16[64,64,128]{2,1,0:T(8,128)(2,1)} %amp_ref.3), custom_call_target="tpu_custom_call" | custom-call | tf_op jit(solution)/shard_map/pack/pallas_call | solution.py:96
  3.9 0.0 copy-start.7
  3.9 0.0 copy-start.10
  3.9 0.0 copy-start.5
  3.9 0.0 copy-start.8
  3.9 10.9 %all-to-all-start = ((bf16[64,136,128]{2,1,0:T(8,128)(2,1)}), bf16[64,136,128]{2,1,0:T(8,128)(2,1)}, u32[]{:S(2)}, u32[]{:S(2)}) async-start(bf16[64,136,128]{2,1,0:T(8,128)(2,1)} %get-tuple-element.14), calls=%async_computation | async-start | bytes 4456448 | tf_op jit(solution)/shard_map/all_to_all | solution.py:308
  14.9 0.0 copy-start.9
  14.9 0.0 copy-start.6
  14.9 0.0 copy-done.7
  14.9 0.1 dynamic_slice.3
  15.0 0.1 broadcast_in_dim.7
  15.1 0.0 copy-done.10
  15.1 25.5 %all_gather.6.cv_ref = bf16[16,128,128]{2,1,0:T(8,128)(2,1)S(1)} all-gather(bf16[2,128,128]{2,1,0:T(8,128)(2,1)S(1)} %copy-done.10), channel_id=1, replica_groups=mesh['occ'=64,'vir'=8] {'vir'}, dimensions={0}, use_global_device_ids=true | all-gather | bytes 589824 | tf_op jit(solution)/shard_map/all_gather | solution.py:309
  40.5 0.1 broadcast_in_dim.8.re_ref
  40.6 0.0 copy-done.5
  40.6 0.0 copy-done.8
  40.6 1.3 inverse.1.inv_ref
  41.9 0.0 copy-done.9
  41.9 0.0 copy-start
  41.9 27.0 %all-to-all-done.got_ref = bf16[64,136,128]{2,1,0:T(8,128)(2,1)} async-done(((bf16[64,136,128]{2,1,0:T(8,128)(2,1)}), bf16[64,136,128]{2,1,0:T(8,128)(2,1)}, u32[]{:S(2)}, u32[]{:S(2)}) %all-to-all-start) | async-done | bytes 2228256 | tf_op jit(solution)/shard_map/all_to_all | solution.py:308
  68.9 6.7 %owner_core.1 = bf16[64,128,128]{2,1,0:T(8,128)(2,1)} custom-call(bf16[64,136,128]{2,1,0:T(8,128)(2,1)} %all-to-all-done.got_ref, bf16[16,128,128]{2,1,0:T(8,128)(2,1)S(1)} %all_gather.6.cv_ref, f32[400,128]{1,0:T(8,128)S(1)} %convert_element_type.3.co_ref, bf16[128,128]{1,0:T(8,128)(2,1)S(1)} %copy-done.6), custom_call_target="tpu_custom_call" | custom-call | tf_op jit(solution)/shard_map/owner_core/pallas_call | solution.py:151
  75.6 0.0 copy-start.11
  75.6 0.0 copy-start.3
  75.6 5.7 %all-to-all-start.1 = ((bf16[64,128,128]{2,1,0:T(8,128)(2,1)}), bf16[64,128,128]{2,1,0:T(8,128)(2,1)}, u32[]{:S(2)}, u32[]{:S(2)}) async-start(bf16[64,128,128]{2,1,0:T(8,128)(2,1)} %owner_core.1), calls=%async_computation.1 | async-start | bytes 4194304 | tf_op jit(solution)/shard_map/all_to_all | solution.py:314
  81.3 0.0 copy-done.11
  81.4 25.5 %all_gather.7.ld_ref = bf16[16,128,128]{2,1,0:T(8,128)(2,1)S(1)} all-gather(bf16[2,128,128]{2,1,0:T(8,128)(2,1)S(1)} %copy-done.11), channel_id=1, replica_groups=mesh['occ'=64,'vir'=8] {'vir'}, dimensions={0}, use_global_device_ids=true | all-gather | bytes 589824 | tf_op jit(solution)/shard_map/all_gather | solution.py:316
  106.8 1.2 copy-done.1
  108.0 4.4 %ladder.1 = (f32[64,64,128]{2,1,0:T(8,128)S(1)}, bf16[16,128,128]{2,1,0:T(8,128)(2,1)S(1)}) custom-call(s32[4,64]{1,0:T(4,128)S(1)} %bitcast.5, bf16[64,64,128]{2,1,0:T(8,128)(2,1)S(1)} %copy-done.1, bf16[4,64,64]{2,1,0:T(8,128)(2,1)S(1)} %copy-done.3, bf16[16,128,128]{2,1,0:T(8,128)(2,1)S(1)} %all_gather.7.ld_ref, f32[64,64,128]{2,1,0:T(8,128)S(1)} %inverse.1.inv_ref, ...), custom_call_target="tpu_custom_call" | custom-call | tf_op jit(solution)/shard_map/ladder/pallas_call | solution.py:220
  112.5 1.4 copy-done.2
  113.8 18.7 %all-to-all-done.1.ret_ref = bf16[64,128,128]{2,1,0:T(8,128)(2,1)} async-done(((bf16[64,128,128]{2,1,0:T(8,128)(2,1)}), bf16[64,128,128]{2,1,0:T(8,128)(2,1)}, u32[]{:S(2)}, u32[]{:S(2)}) %all-to-all-start.1) | async-done | bytes 2097184 | tf_op jit(solution)/shard_map/all_to_all | solution.py:314
  132.5 6.3 %finish.1 = bf16[64,64,128]{2,1,0:T(8,128)(2,1)} custom-call(s32[4,64]{1,0:T(4,128)S(1)} %bitcast.6, s32[64]{0:T(128)S(1)} %get-tuple-element.13.pos_ref, bf16[64,128,128]{2,1,0:T(8,128)(2,1)} %all-to-all-done.1.ret_ref, bf16[16,128,128]{2,1,0:T(8,128)(2,1)S(1)} %get-tuple-element.19.cv_ref, f32[400,128]{1,0:T(8,128)S(1)} %convert_element_type.3.co_ref, ...), custom_call_target="tpu_custom_call" | custom-call | tf_op jit(solution)/shard_map/finish/pallas_call | solution.py:268
  (7 shorter events, 0.0 us)
Async XLA Ops:
  0.0 0.7 copy-start.4
  3.9 11.0 %copy-start.7 = (f32[2048]{0:T(1024)S(1)}, f32[2048]{0:T(1024)}, u32[]{:S(2)}) copy-start(f32[2048]{0:T(1024)} %param.17) | copy-start | bytes 24580
  3.9 11.2 %copy-start.10 = (bf16[2,128,128]{2,1,0:T(8,128)(2,1)S(1)}, bf16[2,128,128]{2,1,0:T(8,128)(2,1)}, u32[]{:S(2)}) copy-start(bf16[2,128,128]{2,1,0:T(8,128)(2,1)} %param.13) | copy-start | bytes 196612
  3.9 36.7 %copy-start.5 = (s32[64,4]{0,1:T(4,128)S(1)}, s32[64,4]{0,1:T(4,128)}, u32[]{:S(2)}) copy-start(s32[64,4]{0,1:T(4,128)} %param.10) | copy-start | bytes 3076
  3.9 36.7 %copy-start.8 = (f32[400]{0:T(512)S(1)}, f32[400]{0:T(512)}, u32[]{:S(2)}) copy-start(f32[400]{0:T(512)} %occ_ref.1) | copy-start | bytes 4804
  3.9 65.0 %all-to-all-start = ((bf16[64,136,128]{2,1,0:T(8,128)(2,1)}), bf16[64,136,128]{2,1,0:T(8,128)(2,1)}, u32[]{:S(2)}, u32[]{:S(2)}) async-start(bf16[64,136,128]{2,1,0:T(8,128)(2,1)} %get-tuple-element.14), calls=%async_computation | async-start | bytes 4456448 | tf_op jit(solution)/shard_map/all_to_all | solution.py:308
  14.9 27.0 %copy-start.9 = (bf16[400,128]{1,0:T(8,128)(2,1)S(1)}, bf16[400,128]{1,0:T(8,128)(2,1)}, u32[]{:S(2)}) copy-start(bf16[400,128]{1,0:T(8,128)(2,1)} %param.14) | copy-start | bytes 307204
  14.9 54.0 %copy-start.6 = (bf16[128,128]{1,0:T(8,128)(2,1)S(1)}, bf16[128,128]{1,0:T(8,128)(2,1)}, u32[]{:S(2)}) copy-start(bf16[128,128]{1,0:T(8,128)(2,1)} %core_ref.1) | copy-start | bytes 98308
  41.9 64.9 %copy-start = (f32[64,64,128]{2,1,0:T(8,128)}, f32[64,64,128]{2,1,0:T(8,128)S(1)}, u32[]{:S(2)}) copy-start(f32[64,64,128]{2,1,0:T(8,128)S(1)} %inverse.1.inv_ref) | copy-start | bytes 6291460
  75.6 5.8 %copy-start.11 = (bf16[2,128,128]{2,1,0:T(8,128)(2,1)S(1)}, bf16[2,128,128]{2,1,0:T(8,128)(2,1)}, u32[]{:S(2)}) copy-start(bf16[2,128,128]{2,1,0:T(8,128)(2,1)} %param.12) | copy-start | bytes 196612
  75.6 31.2 %copy-start.3 = (bf16[4,64,64]{2,1,0:T(8,128)(2,1)S(1)}, bf16[4,64,64]{2,1,0:T(8,128)(2,1)}, u32[]{:S(2)}) copy-start(bf16[4,64,64]{2,1,0:T(8,128)(2,1)} %lv_ref.1) | copy-start | bytes 98308
  75.6 56.9 %all-to-all-start.1 = ((bf16[64,128,128]{2,1,0:T(8,128)(2,1)}), bf16[64,128,128]{2,1,0:T(8,128)(2,1)}, u32[]{:S(2)}, u32[]{:S(2)}) async-start(bf16[64,128,128]{2,1,0:T(8,128)(2,1)} %owner_core.1), calls=%async_computation.1 | async-start | bytes 4194304 | tf_op jit(solution)/shard_map/all_to_all | solution.py:314
  106.8 1.2 copy-start.1
  112.5 1.4 copy-start.2

commit v4 on v3

--- a/solution.py
+++ b/solution.py
@@ -9,6 +9,7 @@
 META = 8
 VMEM_LIMIT = 20 * 2**20
 CHUNKS = 4
+PARTS = 2
 SMEM = pltpu.SMEM
 VMEM = pltpu.VMEM
 
@@ -37,7 +38,11 @@
     tiles, width, domain = amplitudes.shape
     rows = CAP * width
 
-    def kernel(list_ref, ids_ref, amp_ref, out_ref, pos_ref, count, amp, meta, load_sem, tile_sem, meta_sem):
+    def kernel(list_hbm, amp_ref, out_ref, pos_ref, count, list_ref, ids_ref, amp, meta, list_sem, load_sem, tile_sem, meta_sem):
+        list_copy = pltpu.make_async_copy(list_hbm, list_ref, list_sem.at[0])
+        list_copy.start()
+        ids_copy = pltpu.make_async_copy(list_hbm, ids_ref, list_sem.at[1])
+        ids_copy.start()
         part = tiles // CHUNKS
         loads = []
         for j in range(CHUNKS):
@@ -60,6 +65,11 @@
             pltpu.make_async_copy(amp.at[t], slot, tile_sem).start()
             return carry
 
+        list_copy.wait()
+        for j, load in enumerate(loads):
+            load.wait()
+            lax.fori_loop(j * part, (j + 1) * part, place, 0, unroll=16)
+        ids_copy.wait()
         ids = ids_ref[...]
         i, k = ids[0:1], ids[1:2]
         owner = jnp.broadcast_to(lax.rem(i, owners).astype(jnp.float32), (tiles, tiles))
@@ -87,28 +97,28 @@
         meta[...] = total.reshape(owners, META, domain).astype(jnp.bfloat16)
         meta_copy = pltpu.make_async_copy(meta, out_ref.at[:, pl.ds(rows, META)], meta_sem)
         meta_copy.start()
-        for j, load in enumerate(loads):
-            load.wait()
-            lax.fori_loop(j * part, (j + 1) * part, place, 0, unroll=4)
         meta_copy.wait()
         pltpu.make_async_copy(amp, amp_ref, tile_sem).wait()
 
     return pl.pallas_call(
         kernel,
         out_shape=(pltpu.HBM((owners, rows + META, domain), jnp.bfloat16), sds((tiles,), jnp.int32)),
-        in_specs=[spec(SMEM), spec(), spec(pltpu.HBM)],
+        in_specs=[spec(pltpu.HBM), spec(pltpu.HBM)],
         out_specs=(spec(pltpu.HBM), spec(SMEM)),
         scratch_shapes=[
             SMEM((owners,), jnp.int32),
+            SMEM(tile_list.shape, jnp.int32),
+            VMEM(tile_list.shape, jnp.int32),
             VMEM((tiles, width, domain), jnp.bfloat16),
             VMEM((owners, META, domain), jnp.bfloat16),
+            pltpu.SemaphoreType.DMA((2,)),
             pltpu.SemaphoreType.DMA((CHUNKS,)),
             pltpu.SemaphoreType.DMA,
             pltpu.SemaphoreType.DMA,
         ],
         compiler_params=params(),
         name="pack",
-    )(tile_list, tile_list, far(amplitudes))
+    )(far(tile_list), far(amplitudes))
 
 
 def owner_core(received, cycle_virtual, cycle_occupied, cycle_core, width, groups):
@@ -116,8 +126,20 @@
     rank = cycle_core.shape[0]
     rows = CAP * width
 
-    def kernel(got_ref, cv_ref, co_ref, core_ref, out_ref, meta, ids_v, ids, sums, cores, sem, out_sem):
-        meta[...] = got_ref[:, rows:, :].astype(jnp.float32).reshape(meta.shape)
+    part = sources // PARTS
+
+    def kernel(
+        got_ref, cv_ref, co_ref, core_ref, out_ref, got, meta_b, meta, ids_v, ids, sums, cores, sem, part_sem, out_sem
+    ):
+        meta_copy = pltpu.make_async_copy(got_ref.at[:, pl.ds(rows, META)], meta_b, sem)
+        meta_copy.start()
+        copies = []
+        for j in range(PARTS):
+            piece = pl.ds(j * part, part)
+            copies.append(pltpu.make_async_copy(got_ref.at[piece, pl.ds(0, rows)], got.at[piece], part_sem.at[j]))
+            copies[j].start()
+        meta_copy.wait()
+        meta[...] = meta_b[...].astype(jnp.float32).reshape(meta.shape)
         ids_v[...] = meta[pl.ds(0, sources, stride=META), :].astype(jnp.int32)
         ids_copy = pltpu.make_async_copy(ids_v, ids, sem)
         ids_copy.start()
@@ -129,12 +151,14 @@
                 key = ids[s, 4 * c]
                 k = ids[s, 4 * c + 1] * 16 + ids[s, 4 * c + 2]
                 g = ids[s, 4 * c + 3]
-                tile = got_ref[s, c * width : (c + 1) * width, :]
+                tile = got[s, c * width : (c + 1) * width, :]
                 one = jnp.dot(tile, cv_ref[g], preferred_element_type=jnp.float32)
                 sums[key] += one * co_ref[pl.ds(k, 1), :]
             return carry
 
-        lax.fori_loop(0, sources, add, 0, unroll=8)
+        for j, copy in enumerate(copies):
+            copy.wait()
+            lax.fori_loop(j * part, (j + 1) * part, add, 0, unroll=32)
         grouped = sums[...].astype(jnp.bfloat16).reshape((groups + 1) * width, rank)
         core = jnp.dot(grouped, core_ref[...], preferred_element_type=jnp.float32)
         cores[...] = core.astype(jnp.bfloat16).reshape(cores.shape)
@@ -151,51 +175,37 @@
     return pl.pallas_call(
         kernel,
         out_shape=pltpu.HBM((sources, rows, rank), jnp.bfloat16),
-        in_specs=[spec()] * 4,
+        in_specs=[spec(pltpu.HBM)] + [spec()] * 3,
         out_specs=spec(pltpu.HBM),
         scratch_shapes=[
+            VMEM((sources, rows, domain), jnp.bfloat16),
+            VMEM((sources, META, domain), jnp.bfloat16),
             VMEM((sources * META, domain), jnp.float32),
             VMEM((sources, domain), jnp.int32),
             SMEM((sources, domain), jnp.int32),
             VMEM((groups + 1, width, rank), jnp.float32),
             VMEM((groups + 1, width, rank), jnp.bfloat16),
             pltpu.SemaphoreType.DMA,
+            pltpu.SemaphoreType.DMA((PARTS,)),
             pltpu.SemaphoreType.DMA,
         ],
         compiler_params=params(),
         name="owner_core",
-    )(near(received), near(cycle_virtual), near(cycle_occupied), near(cycle_core))
-
-
-def inverse_denominator(tile_list, occ_energy, row_energy, column_energy):
-    tiles = tile_list.shape[1]
-    local_tiles, width, domain = row_energy.shape
-
-    def kernel(list_ref, occ_ref, re_ref, ce_ref, inv_ref):
-        def one(t, carry):
-            a = lax.rem(list_ref[2, t], local_tiles)
-            occ = occ_ref[list_ref[0, t]] + occ_ref[list_ref[1, t]]
-            inv_ref[t] = 1.0 / (re_ref[a] + ce_ref[pl.ds(list_ref[3, t], 1), :] - occ)
-            return carry
-
-        lax.fori_loop(0, tiles, one, 0, unroll=4)
-
-    return pl.pallas_call(
-        kernel,
-        out_shape=sds((tiles, width, domain), jnp.float32),
-        in_specs=[spec(SMEM), spec(SMEM)] + [spec()] * 2,
-        out_specs=spec(),
-        compiler_params=params(),
-        name="inverse",
-    )(tile_list, occ_energy, row_energy, column_energy)
-
-
-def ladder_part(tile_list, amplitudes, ladder_virtual, ladder_domain, inverse, cycle_virtual):
+    )(far(received), near(cycle_virtual), near(cycle_occupied), near(cycle_core))
+
+
+def inverse_at(t, list_ref, occ_ref, row_ref, column_ref):
+    a = lax.rem(list_ref[2, t], row_ref.shape[0])
+    occ = occ_ref[list_ref[0, t]] + occ_ref[list_ref[1, t]]
+    return 1.0 / (row_ref[a] + column_ref[pl.ds(list_ref[3, t], 1), :] - occ)
+
+
+def ladder_part(tile_list, amplitudes, ladder_virtual, ladder_domain, energies, cycle_virtual):
     tiles, width, domain = amplitudes.shape
     local_tiles = ladder_virtual.shape[0]
     domains = cycle_virtual.shape[0]
 
-    def kernel(list_ref, amp_ref, lv_ref, ld_ref, inv_ref, cv_ref, base_ref, turned_ref, half):
+    def kernel(list_ref, occ_ref, amp_ref, lv_ref, ld_ref, row_ref, column_ref, cv_ref, base_ref, turned_ref, half):
         def first(t, carry):
             part = jnp.dot(amp_ref[t], ld_ref[list_ref[3, t]], preferred_element_type=jnp.float32)
             half[t] = part.astype(jnp.bfloat16)
@@ -206,7 +216,8 @@
         def second(t, carry):
             a = lax.rem(list_ref[2, t], local_tiles)
             ladder = jnp.dot(lv_ref[a], half[t], preferred_element_type=jnp.float32)
-            base_ref[t] = amp_ref[t].astype(jnp.float32) + ladder * inv_ref[t]
+            inverse = inverse_at(t, list_ref, occ_ref, row_ref, column_ref)
+            base_ref[t] = amp_ref[t].astype(jnp.float32) + ladder * inverse
             return carry
 
         lax.fori_loop(0, tiles, second, 0, unroll=8)
@@ -220,47 +231,65 @@
     return pl.pallas_call(
         kernel,
         out_shape=(sds(amplitudes.shape, jnp.float32), sds(cycle_virtual.shape, jnp.bfloat16)),
-        in_specs=[spec(SMEM)] + [spec()] * 5,
+        in_specs=[spec(SMEM)] * 2 + [spec()] * 6,
         out_specs=(spec(), spec()),
         scratch_shapes=[VMEM(amplitudes.shape, jnp.bfloat16)],
         compiler_params=params(),
         name="ladder",
-    )(tile_list, amplitudes, ladder_virtual, ladder_domain, inverse, cycle_virtual)
-
-
-def finish(tile_list, position, returned, cycle_turned, cycle_occupied, base, inverse):
+    )(tile_list, energies[0], amplitudes, ladder_virtual, ladder_domain, energies[1], energies[2], cycle_virtual)
+
+
+def finish(tile_list, position, returned, cycle_turned, cycle_occupied, base, energies):
     tiles, width, domain = base.shape
     part = tiles // CHUNKS
 
     def kernel(
-        list_ref, pos_ref, ret_ref, cv_ref, co_ref, base_ref, inv_ref, out_ref, base, inv, out, sem, out_sem
+        list_ref,
+        pos_ref,
+        occ_ref,
+        row_ref,
+        column_ref,
+        ret_ref,
+        cv_ref,
+        co_ref,
+        base_ref,
+        out_ref,
+        core,
+        base,
+        out,
+        sem,
+        out_sem,
     ):
         loads, stores = [], []
         for j in range(CHUNKS):
             piece = pl.ds(j * part, part)
-            loads.append(
-                (
-                    pltpu.make_async_copy(base_ref.at[piece], base.at[piece], sem.at[j, 0]),
-                    pltpu.make_async_copy(inv_ref.at[piece], inv.at[piece], sem.at[j, 1]),
-                )
-            )
+            loads.append(pltpu.make_async_copy(base_ref.at[piece], base.at[piece], sem.at[j, 0]))
             stores.append(pltpu.make_async_copy(out.at[piece], out_ref.at[piece], out_sem.at[j]))
 
-        for pair in loads:
-            for copy in pair:
-                copy.start()
+        for j in range(CHUNKS):
+
+            def fetch(t, carry):
+                slot = pos_ref[t]
+                row = pl.multiple_of(lax.rem(slot, CAP) * width, width)
+                tile = ret_ref.at[lax.div(slot, CAP), pl.ds(row, width)]
+                pltpu.make_async_copy(tile, core.at[t], sem.at[j, 1]).start()
+                return carry
+
+            lax.fori_loop(j * part, (j + 1) * part, fetch, 0, unroll=8)
+            loads[j].start()
 
         def one(t, carry):
-            row = pl.multiple_of(lax.rem(pos_ref[t], CAP) * width, width)
-            scaled = ret_ref[lax.div(pos_ref[t], CAP), pl.ds(row, width), :].astype(jnp.float32) * co_ref[pl.ds(list_ref[1, t], 1), :]
+            scaled = core[t].astype(jnp.float32) * co_ref[pl.ds(list_ref[1, t], 1), :]
             term = jnp.dot(scaled.astype(jnp.bfloat16), cv_ref[list_ref[3, t]], preferred_element_type=jnp.float32)
-            out[t] = (base[t] + term * inv[t]).astype(jnp.bfloat16)
+            inverse = inverse_at(t, list_ref, occ_ref, row_ref, column_ref)
+            out[t] = (base[t] + term * inverse).astype(jnp.bfloat16)
             return carry
 
         for j in range(CHUNKS):
-            for copy in loads[j]:
-                copy.wait()
-            lax.fori_loop(j * part, (j + 1) * part, one, 0, unroll=4)
+            piece = pl.ds(j * part, part)
+            pltpu.make_async_copy(core.at[piece], core.at[piece], sem.at[j, 1]).wait()
+            loads[j].wait()
+            lax.fori_loop(j * part, (j + 1) * part, one, 0, unroll=16)
             stores[j].start()
         for copy in stores:
             copy.wait()
@@ -268,10 +297,10 @@
     return pl.pallas_call(
         kernel,
         out_shape=sds(base.shape, jnp.bfloat16),
-        in_specs=[spec(SMEM), spec(SMEM), spec(), spec(), spec(), spec(pltpu.HBM), spec(pltpu.HBM)],
+        in_specs=[spec(SMEM)] * 3 + [spec()] * 2 + [spec(pltpu.HBM)] + [spec()] * 2 + [spec(pltpu.HBM)],
         out_specs=spec(pltpu.HBM),
         scratch_shapes=[
-            VMEM((tiles, width, domain), jnp.float32),
+            VMEM((tiles, width, domain), jnp.bfloat16),
             VMEM((tiles, width, domain), jnp.float32),
             VMEM((tiles, width, domain), jnp.bfloat16),
             pltpu.SemaphoreType.DMA((CHUNKS, 2)),
@@ -279,7 +308,7 @@
         ],
         compiler_params=params(),
         name="finish",
-    )(tile_list, position, near(returned), cycle_turned, cycle_occupied, far(base), far(inverse))
+    )(tile_list, position, *energies, far(returned), cycle_turned, cycle_occupied, far(base))
 
 
 def body(
@@ -307,17 +336,15 @@
     send, position = pack(amplitudes, tile_list, owners, local_tiles)
     received = lax.all_to_all(send, "occ", split_axis=0, concat_axis=0, tiled=True)
     virtual_all = lax.all_gather(cycle_virtual, "vir", axis=0, tiled=True)
-    row_energy, _ = lax.optimization_barrier((row_energy, virtual_all))
-    inverse = inverse_denominator(tile_list, occ_energy, row_energy, column_energy)
-    inverse, virtual_all = lax.optimization_barrier((inverse, virtual_all))
+    energies = (occ_energy, row_energy, column_energy)
     answers = owner_core(received, virtual_all, cycle_occupied, cycle_core, width, groups)
     returned = lax.all_to_all(answers, "occ", split_axis=0, concat_axis=0, tiled=True)
     domain_own, _ = lax.optimization_barrier((ladder_domain_integrals, virtual_all))
     domain_all = lax.all_gather(domain_own, "vir", axis=0, tiled=True)
     base, turned = ladder_part(
-        tile_list, amplitudes, ladder_virtual_integrals, domain_all, inverse, virtual_all
+        tile_list, amplitudes, ladder_virtual_integrals, domain_all, energies, virtual_all
     )
-    return finish(tile_list, position, returned, turned, cycle_occupied, base, inverse)
+    return finish(tile_list, position, returned, turned, cycle_occupied, base, energies)
 
 
 def solution(mesh):

time: 140 us -> 135 us (0.964)
  Pallas kernels: 21.9 us -> 16.7 us
  waiting for transfers between devices: 45.7 us -> 48.1 us
  local copies, waits for them, and re-layouts: 3.59 us -> 1.64 us
    pallas_call x1, Pallas kernels: 6.35 us -> 3.85 us  [finish(): pl.pallas_call(kernel, out_shape=sds(base.shape, jnp.bfloat16), in_specs=...]
    unnamed x24 -> x20, local copies, waits for them, and re-layouts: 3.34 us -> 1.39 us
    all_to_all x1, waiting for transfers between devices: 27 us -> 28.5 us  [body(): lax.all_to_all(send, 'occ', split_axis=0, concat_axis=0, tiled=True)]
  transfers between devices with their start and end apart: 2 -> 2, of which waited for: 2 -> 2; matrix products, arithmetic and copies ran while one was open for 0% -> 0% of each run, Pallas kernels for 4% -> 3%
where the time goes in v4:
time: 135 us; the launch traced here: 134 us
  blocking collectives  50.9 us (38%)
  waiting for transfers between devices  48.1 us (36%)
  Pallas kernels  16.7 us (12%)
  starting transfers between devices  16.7 us (12%)
  local copies, waits for them, and re-layouts  1.64 us (1%)
    all_to_all x1, waiting for transfers between devices, body(): lax.all_to_all(send, 'occ', split_axis=0, concat_axis=0, tiled=True)  28.5 us
    all_gather x1, blocking collectives, body(): virtual_all = lax.all_gather(cycle_virtual, 'vir', axis=0, tiled=True)  25.5 us
    all_gather x1, blocking collectives, body(): domain_all = lax.all_gather(domain_own, 'vir', axis=0, tiled=True)  25.5 us
    all_to_all x1, waiting for transfers between devices, body(): lax.all_to_all(answers, 'occ', split_axis=0, concat_axis=0, tiled=True)  19.6 us
    all_to_all x1, starting transfers between devices, body(): lax.all_to_all(send, 'occ', split_axis=0, concat_axis=0, tiled=True)  10.9 us
    all_to_all x1, starting transfers between devices, body(): lax.all_to_all(answers, 'occ', split_axis=0, concat_axis=0, tiled=True)  5.76 us
    pallas_call x1, Pallas kernels, owner_core(): pl.pallas_call(kernel, out_shape=pltpu.HBM((sources, rows, rank), jnp.bfl...  5.4 us
    pallas_call x1, Pallas kernels, ladder_part(): pl.pallas_call(kernel, out_shape=(sds(amplitudes.shape, jnp.float32), sds...  4.5 us
  transfers between devices with their start and end apart: 2, of which 2 were waited for; matrix products, arithmetic and copies ran while one was open for 0% of the time, Pallas kernels for 3%

profile of v4, /device:TPU:448, one launch (start us, length us, event | category | flops | bytes accessed | tf_op | source)
XLA Modules:
  0.0 134.2 jit_solution(2713594314751411137)
XLA Ops:
  0.0 2.9 %pack.1 = (bf16[64,136,128]{2,1,0:T(8,128)(2,1)}, s32[64]{0:T(128)S(1)}) custom-call(s32[4,64]{1,0:T(4,128)} %bitcast.4, bf16[64,64,128]{2,1,0:T(8,128)(2,1)} %amp_ref.3), custom_call_target="tpu_custom_call" | custom-call | tf_op jit(solution)/shard_map/pack/pallas_call | solution.py:103
  2.9 0.0 copy-start.7
  2.9 0.0 copy-start.8
  2.9 0.0 copy-start.4
  3.0 10.9 %all-to-all-start = ((bf16[64,136,128]{2,1,0:T(8,128)(2,1)}), bf16[64,136,128]{2,1,0:T(8,128)(2,1)}, u32[]{:S(2)}, u32[]{:S(2)}) async-start(bf16[64,136,128]{2,1,0:T(8,128)(2,1)} %get-tuple-element.11), calls=%async_computation | async-start | bytes 4456448 | tf_op jit(solution)/shard_map/all_to_all | solution.py:337
  13.9 0.0 copy-done.7
  13.9 0.0 copy-done.8
  14.0 25.5 %all_gather.6.cv_ref = bf16[16,128,128]{2,1,0:T(8,128)(2,1)S(1)} all-gather(bf16[2,128,128]{2,1,0:T(8,128)(2,1)S(1)} %copy-done.8), channel_id=1, replica_groups=mesh['occ'=64,'vir'=8] {'vir'}, dimensions={0}, use_global_device_ids=true | all-gather | bytes 589824 | tf_op jit(solution)/shard_map/all_gather | solution.py:338
  39.4 28.5 %all-to-all-done.got_ref = bf16[64,136,128]{2,1,0:T(8,128)(2,1)} async-done(((bf16[64,136,128]{2,1,0:T(8,128)(2,1)}), bf16[64,136,128]{2,1,0:T(8,128)(2,1)}, u32[]{:S(2)}, u32[]{:S(2)}) %all-to-all-start) | async-done | bytes 2228256 | tf_op jit(solution)/shard_map/all_to_all | solution.py:337
  67.9 0.0 copy-done.4
  68.0 5.4 %owner_core.1 = bf16[64,128,128]{2,1,0:T(8,128)(2,1)} custom-call(bf16[64,136,128]{2,1,0:T(8,128)(2,1)} %all-to-all-done.got_ref, bf16[16,128,128]{2,1,0:T(8,128)(2,1)S(1)} %all_gather.6.cv_ref, f32[400,128]{1,0:T(8,128)S(1)} %convert_element_type.3.co_ref, bf16[128,128]{1,0:T(8,128)(2,1)S(1)} %copy-done.4), custom_call_target="tpu_custom_call" | custom-call | tf_op jit(solution)/shard_map/owner_core/pallas_call | solution.py:175
  73.4 0.0 copy-start.3
  73.4 0.0 copy-start.9
  73.4 0.0 copy-start
  73.4 0.0 copy-start.2
  73.4 0.0 copy-start.5
  73.4 0.0 copy-start.6
  73.4 5.8 %all-to-all-start.1 = ((bf16[64,128,128]{2,1,0:T(8,128)(2,1)}), bf16[64,128,128]{2,1,0:T(8,128)(2,1)}, u32[]{:S(2)}, u32[]{:S(2)}) async-start(bf16[64,128,128]{2,1,0:T(8,128)(2,1)} %owner_core.1), calls=%async_computation.1 | async-start | bytes 4194304 | tf_op jit(solution)/shard_map/all_to_all | solution.py:341
  79.2 0.0 copy-done.3
  79.2 0.1 dynamic_slice.3
  79.3 0.1 broadcast_in_dim.7
  79.4 0.0 copy-done.9
  79.4 25.5 %all_gather.7.ld_ref = bf16[16,128,128]{2,1,0:T(8,128)(2,1)S(1)} all-gather(bf16[2,128,128]{2,1,0:T(8,128)(2,1)S(1)} %copy-done.9), channel_id=1, replica_groups=mesh['occ'=64,'vir'=8] {'vir'}, dimensions={0}, use_global_device_ids=true | all-gather | bytes 589824 | tf_op jit(solution)/shard_map/all_gather | solution.py:343
  104.8 0.1 broadcast_in_dim.8.row_ref
  104.9 0.0 copy-done
  104.9 0.0 copy-done.2
  104.9 0.0 copy-done.5
  105.0 0.0 copy-done.6
  105.0 4.5 %ladder.1 = (f32[64,64,128]{2,1,0:T(8,128)S(1)}, bf16[16,128,128]{2,1,0:T(8,128)(2,1)S(1)}) custom-call(s32[4,64]{1,0:T(4,128)S(1)} %bitcast.5, f32[400]{0:T(512)S(1)} %copy-done.6, bf16[64,64,128]{2,1,0:T(8,128)(2,1)S(1)} %copy-done, bf16[4,64,64]{2,1,0:T(8,128)(2,1)S(1)} %copy-done.2, bf16[16,128,128]{2,1,0:T(8,128)(2,1)S(1)} %all_gather.7.ld_ref, ...), custom_call_target="tpu_custom_call" | custom-call | tf_op jit(solution)/shard_map/ladder/pallas_call | solution.py:231
  109.5 1.3 copy-done.1
  110.8 19.6 %all-to-all-done.1.ret_ref = bf16[64,128,128]{2,1,0:T(8,128)(2,1)} async-done(((bf16[64,128,128]{2,1,0:T(8,128)(2,1)}), bf16[64,128,128]{2,1,0:T(8,128)(2,1)}, u32[]{:S(2)}, u32[]{:S(2)}) %all-to-all-start.1) | async-done | bytes 2097184 | tf_op jit(solution)/shard_map/all_to_all | solution.py:341
  130.4 3.9 %finish.1 = bf16[64,64,128]{2,1,0:T(8,128)(2,1)} custom-call(s32[4,64]{1,0:T(4,128)S(1)} %bitcast.6, s32[64]{0:T(128)S(1)} %get-tuple-element.10.pos_ref, f32[400]{0:T(512)S(1)} %copy-done.6, f32[4,64,128]{2,1,0:T(8,128)S(1)} %broadcast_in_dim.8.row_ref, f32[16,128]{1,0:T(8,128)S(1)} %bitcast.3, bf16[64,128,128]{2,1,0:T(8,128)(2,1)} %all-to-all-done.1.ret_ref, ...), custom_call_target="tpu_custom_call" | custom-call | tf_op jit(solution)/shard_map/finish/pallas_call | solution.py:297
  (2 shorter events, 0.0 us)
Async XLA Ops:
  2.9 11.0 %copy-start.7 = (bf16[400,128]{1,0:T(8,128)(2,1)S(1)}, bf16[400,128]{1,0:T(8,128)(2,1)}, u32[]{:S(2)}) copy-start(bf16[400,128]{1,0:T(8,128)(2,1)} %param.14) | copy-start | bytes 307204
  2.9 11.0 %copy-start.8 = (bf16[2,128,128]{2,1,0:T(8,128)(2,1)S(1)}, bf16[2,128,128]{2,1,0:T(8,128)(2,1)}, u32[]{:S(2)}) copy-start(bf16[2,128,128]{2,1,0:T(8,128)(2,1)} %param.13) | copy-start | bytes 196612
  2.9 65.0 %copy-start.4 = (bf16[128,128]{1,0:T(8,128)(2,1)S(1)}, bf16[128,128]{1,0:T(8,128)(2,1)}, u32[]{:S(2)}) copy-start(bf16[128,128]{1,0:T(8,128)(2,1)} %core_ref.1) | copy-start | bytes 98308
  3.0 65.0 %all-to-all-start = ((bf16[64,136,128]{2,1,0:T(8,128)(2,1)}), bf16[64,136,128]{2,1,0:T(8,128)(2,1)}, u32[]{:S(2)}, u32[]{:S(2)}) async-start(bf16[64,136,128]{2,1,0:T(8,128)(2,1)} %get-tuple-element.11), calls=%async_computation | async-start | bytes 4456448 | tf_op jit(solution)/shard_map/all_to_all | solution.py:337
  73.4 5.8 %copy-start.3 = (f32[2048]{0:T(1024)S(1)}, f32[2048]{0:T(1024)}, u32[]{:S(2)}) copy-start(f32[2048]{0:T(1024)} %param.17) | copy-start | bytes 24580
  73.4 6.0 %copy-start.9 = (bf16[2,128,128]{2,1,0:T(8,128)(2,1)S(1)}, bf16[2,128,128]{2,1,0:T(8,128)(2,1)}, u32[]{:S(2)}) copy-start(bf16[2,128,128]{2,1,0:T(8,128)(2,1)} %param.12) | copy-start | bytes 196612
  73.4 31.5 %copy-start = (bf16[64,64,128]{2,1,0:T(8,128)(2,1)S(1)}, bf16[64,64,128]{2,1,0:T(8,128)(2,1)}, u32[]{:S(2)}) copy-start(bf16[64,64,128]{2,1,0:T(8,128)(2,1)} %amp_ref.3) | copy-start | bytes 3145732
  73.4 31.5 %copy-start.2 = (bf16[4,64,64]{2,1,0:T(8,128)(2,1)S(1)}, bf16[4,64,64]{2,1,0:T(8,128)(2,1)}, u32[]{:S(2)}) copy-start(bf16[4,64,64]{2,1,0:T(8,128)(2,1)} %lv_ref.1) | copy-start | bytes 98308
  73.4 31.5 %copy-start.5 = (s32[64,4]{0,1:T(4,128)S(1)}, s32[64,4]{0,1:T(4,128)}, u32[]{:S(2)}) copy-start(s32[64,4]{0,1:T(4,128)} %param.10) | copy-start | bytes 3076
  73.4 31.5 %copy-start.6 = (f32[400]{0:T(512)S(1)}, f32[400]{0:T(512)}, u32[]{:S(2)}) copy-start(f32[400]{0:T(512)} %occ_ref.3) | copy-start | bytes 4804
  73.4 57.0 %all-to-all-start.1 = ((bf16[64,128,128]{2,1,0:T(8,128)(2,1)}), bf16[64,128,128]{2,1,0:T(8,128)(2,1)}, u32[]{:S(2)}, u32[]{:S(2)}) async-start(bf16[64,128,128]{2,1,0:T(8,128)(2,1)} %owner_core.1), calls=%async_computation.1 | async-start | bytes 4194304 | tf_op jit(solution)/shard_map/all_to_all | solution.py:341
  109.5 1.3 copy-start.1

commit v5 on v4

--- a/solution.py
+++ b/solution.py
@@ -7,9 +7,10 @@
 
 CAP = 2
 META = 8
+FIELDS = 4 * CAP
 VMEM_LIMIT = 20 * 2**20
 CHUNKS = 4
-PARTS = 2
+PARTS = 1
 SMEM = pltpu.SMEM
 VMEM = pltpu.VMEM
 
@@ -140,7 +141,8 @@
             copies[j].start()
         meta_copy.wait()
         meta[...] = meta_b[...].astype(jnp.float32).reshape(meta.shape)
-        ids_v[...] = meta[pl.ds(0, sources, stride=META), :].astype(jnp.int32)
+        turned = meta[pl.ds(0, sources, stride=META), :].T
+        ids_v[...] = turned[0:FIELDS].astype(jnp.int32)
         ids_copy = pltpu.make_async_copy(ids_v, ids, sem)
         ids_copy.start()
         sums[...] = jnp.zeros_like(sums)
@@ -148,9 +150,9 @@
 
         def add(s, carry):
             for c in range(CAP):
-                key = ids[s, 4 * c]
-                k = ids[s, 4 * c + 1] * 16 + ids[s, 4 * c + 2]
-                g = ids[s, 4 * c + 3]
+                key = ids[4 * c, s]
+                k = ids[4 * c + 1, s] * 16 + ids[4 * c + 2, s]
+                g = ids[4 * c + 3, s]
                 tile = got[s, c * width : (c + 1) * width, :]
                 one = jnp.dot(tile, cv_ref[g], preferred_element_type=jnp.float32)
                 sums[key] += one * co_ref[pl.ds(k, 1), :]
@@ -158,7 +160,7 @@
 
         for j, copy in enumerate(copies):
             copy.wait()
-            lax.fori_loop(j * part, (j + 1) * part, add, 0, unroll=32)
+            lax.fori_loop(j * part, (j + 1) * part, add, 0, unroll=64)
         grouped = sums[...].astype(jnp.bfloat16).reshape((groups + 1) * width, rank)
         core = jnp.dot(grouped, core_ref[...], preferred_element_type=jnp.float32)
         cores[...] = core.astype(jnp.bfloat16).reshape(cores.shape)
@@ -166,7 +168,7 @@
         def answer(s, carry):
             for c in range(CAP):
                 slot = out_ref.at[s, pl.ds(c * width, width)]
-                pltpu.make_async_copy(cores.at[ids[s, 4 * c]], slot, out_sem).start()
+                pltpu.make_async_copy(cores.at[ids[4 * c, s]], slot, out_sem).start()
             return carry
 
         lax.fori_loop(0, sources, answer, 0, unroll=4)
@@ -181,8 +183,8 @@
             VMEM((sources, rows, domain), jnp.bfloat16),
             VMEM((sources, META, domain), jnp.bfloat16),
             VMEM((sources * META, domain), jnp.float32),
-            VMEM((sources, domain), jnp.int32),
-            SMEM((sources, domain), jnp.int32),
+            VMEM((FIELDS, sources), jnp.int32),
+            SMEM((FIELDS, sources), jnp.int32),
             VMEM((groups + 1, width, rank), jnp.float32),
             VMEM((groups + 1, width, rank), jnp.bfloat16),
             pltpu.SemaphoreType.DMA,
@@ -241,7 +243,8 @@
 
 def finish(tile_list, position, returned, cycle_turned, cycle_occupied, base, energies):
     tiles, width, domain = base.shape
-    part = tiles // CHUNKS
+    bounds = [tiles * j // CHUNKS for j in range(CHUNKS + 1)]
+    pieces = list(zip(bounds[:-1], bounds[1:]))
 
     def kernel(
         list_ref,
@@ -261,12 +264,12 @@
         out_sem,
     ):
         loads, stores = [], []
-        for j in range(CHUNKS):
-            piece = pl.ds(j * part, part)
+        for j, (low, high) in enumerate(pieces):
+            piece = pl.ds(low, high - low)
             loads.append(pltpu.make_async_copy(base_ref.at[piece], base.at[piece], sem.at[j, 0]))
             stores.append(pltpu.make_async_copy(out.at[piece], out_ref.at[piece], out_sem.at[j]))
 
-        for j in range(CHUNKS):
+        for j, (low, high) in enumerate(pieces):
 
             def fetch(t, carry):
                 slot = pos_ref[t]
@@ -275,8 +278,8 @@
                 pltpu.make_async_copy(tile, core.at[t], sem.at[j, 1]).start()
                 return carry
 
-            lax.fori_loop(j * part, (j + 1) * part, fetch, 0, unroll=8)
             loads[j].start()
+            lax.fori_loop(low, high, fetch, 0, unroll=8)
 
         def one(t, carry):
             scaled = core[t].astype(jnp.float32) * co_ref[pl.ds(list_ref[1, t], 1), :]
@@ -285,11 +288,11 @@
             out[t] = (base[t] + term * inverse).astype(jnp.bfloat16)
             return carry
 
-        for j in range(CHUNKS):
-            piece = pl.ds(j * part, part)
+        for j, (low, high) in enumerate(pieces):
+            piece = pl.ds(low, high - low)
             pltpu.make_async_copy(core.at[piece], core.at[piece], sem.at[j, 1]).wait()
             loads[j].wait()
-            lax.fori_loop(j * part, (j + 1) * part, one, 0, unroll=16)
+            lax.fori_loop(low, high, one, 0, unroll=high - low)
             stores[j].start()
         for copy in stores:
             copy.wait()
@@ -303,8 +306,8 @@
             VMEM((tiles, width, domain), jnp.bfloat16),
             VMEM((tiles, width, domain), jnp.float32),
             VMEM((tiles, width, domain), jnp.bfloat16),
-            pltpu.SemaphoreType.DMA((CHUNKS, 2)),
-            pltpu.SemaphoreType.DMA((CHUNKS,)),
+            pltpu.SemaphoreType.DMA((len(pieces), 2)),
+            pltpu.SemaphoreType.DMA((len(pieces),)),
         ],
         compiler_params=params(),
         name="finish",

time: 135 us -> 134 us (level)
  no operation moved by 1% of the time
where the time goes in v5:
time: 134 us; the launch traced here: 133 us
  blocking collectives  50.9 us (38%)
  waiting for transfers between devices  48.1 us (36%)
  starting transfers between devices  16.7 us (12%)
  Pallas kernels  15.7 us (12%)
  local copies, waits for them, and re-layouts  1.64 us (1%)
    all_to_all x1, waiting for transfers between devices, body(): lax.all_to_all(send, 'occ', split_axis=0, concat_axis=0, tiled=True)  28.5 us
    all_gather x1, blocking collectives, body(): virtual_all = lax.all_gather(cycle_virtual, 'vir', axis=0, tiled=True)  25.5 us
    all_gather x1, blocking collectives, body(): domain_all = lax.all_gather(domain_own, 'vir', axis=0, tiled=True)  25.5 us
    all_to_all x1, waiting for transfers between devices, body(): lax.all_to_all(answers, 'occ', split_axis=0, concat_axis=0, tiled=True)  19.6 us
    all_to_all x1, starting transfers between devices, body(): lax.all_to_all(send, 'occ', split_axis=0, concat_axis=0, tiled=True)  10.9 us
    all_to_all x1, starting transfers between devices, body(): lax.all_to_all(answers, 'occ', split_axis=0, concat_axis=0, tiled=True)  5.74 us
    pallas_call x1, Pallas kernels, owner_core(): pl.pallas_call(kernel, out_shape=pltpu.HBM((sources, rows, rank), jnp.bfl...  4.61 us
    pallas_call x1, Pallas kernels, ladder_part(): pl.pallas_call(kernel, out_shape=(sds(amplitudes.shape, jnp.float32), sds...  4.5 us
  transfers between devices with their start and end apart: 2, of which 2 were waited for; matrix products, arithmetic and copies ran while one was open for 0% of the time, Pallas kernels for 3%

profile of v5, /device:TPU:448, one launch (start us, length us, event | category | flops | bytes accessed | tf_op | source)
XLA Modules:
  0.0 133.3 jit_solution(15886026272152483638)
XLA Ops:
  0.0 2.9 %pack.1 = (bf16[64,136,128]{2,1,0:T(8,128)(2,1)}, s32[64]{0:T(128)S(1)}) custom-call(s32[4,64]{1,0:T(4,128)} %bitcast.4, bf16[64,64,128]{2,1,0:T(8,128)(2,1)} %amp_ref.3), custom_call_target="tpu_custom_call" | custom-call | tf_op jit(solution)/shard_map/pack/pallas_call | solution.py:104
  2.9 0.0 copy-start.7
  2.9 0.0 copy-start.8
  2.9 0.0 copy-start.4
  3.0 10.9 %all-to-all-start = ((bf16[64,136,128]{2,1,0:T(8,128)(2,1)}), bf16[64,136,128]{2,1,0:T(8,128)(2,1)}, u32[]{:S(2)}, u32[]{:S(2)}) async-start(bf16[64,136,128]{2,1,0:T(8,128)(2,1)} %get-tuple-element.11), calls=%async_computation | async-start | bytes 4456448 | tf_op jit(solution)/shard_map/all_to_all | solution.py:340
  13.9 0.0 copy-done.7
  13.9 0.0 copy-done.8
  14.0 25.5 %all_gather.6.cv_ref = bf16[16,128,128]{2,1,0:T(8,128)(2,1)S(1)} all-gather(bf16[2,128,128]{2,1,0:T(8,128)(2,1)S(1)} %copy-done.8), channel_id=1, replica_groups=mesh['occ'=64,'vir'=8] {'vir'}, dimensions={0}, use_global_device_ids=true | all-gather | bytes 589824 | tf_op jit(solution)/shard_map/all_gather | solution.py:341
  39.4 28.5 %all-to-all-done.got_ref = bf16[64,136,128]{2,1,0:T(8,128)(2,1)} async-done(((bf16[64,136,128]{2,1,0:T(8,128)(2,1)}), bf16[64,136,128]{2,1,0:T(8,128)(2,1)}, u32[]{:S(2)}, u32[]{:S(2)}) %all-to-all-start) | async-done | bytes 2228256 | tf_op jit(solution)/shard_map/all_to_all | solution.py:340
  67.9 0.0 copy-done.4
  68.0 4.6 %owner_core.1 = bf16[64,128,128]{2,1,0:T(8,128)(2,1)} custom-call(bf16[64,136,128]{2,1,0:T(8,128)(2,1)} %all-to-all-done.got_ref, bf16[16,128,128]{2,1,0:T(8,128)(2,1)S(1)} %all_gather.6.cv_ref, f32[400,128]{1,0:T(8,128)S(1)} %convert_element_type.3.co_ref, bf16[128,128]{1,0:T(8,128)(2,1)S(1)} %copy-done.4), custom_call_target="tpu_custom_call" | custom-call | tf_op jit(solution)/shard_map/owner_core/pallas_call | solution.py:177
  72.6 0.0 copy-start.3
  72.6 0.0 copy-start.9
  72.6 0.0 copy-start
  72.6 0.0 copy-start.2
  72.6 0.0 copy-start.5
  72.6 0.0 copy-start.6
  72.6 5.7 %all-to-all-start.1 = ((bf16[64,128,128]{2,1,0:T(8,128)(2,1)}), bf16[64,128,128]{2,1,0:T(8,128)(2,1)}, u32[]{:S(2)}, u32[]{:S(2)}) async-start(bf16[64,128,128]{2,1,0:T(8,128)(2,1)} %owner_core.1), calls=%async_computation.1 | async-start | bytes 4194304 | tf_op jit(solution)/shard_map/all_to_all | solution.py:344
  78.4 0.0 copy-done.3
  78.4 0.1 dynamic_slice.3
  78.5 0.1 broadcast_in_dim.7
  78.6 0.0 copy-done.9
  78.6 25.5 %all_gather.7.ld_ref = bf16[16,128,128]{2,1,0:T(8,128)(2,1)S(1)} all-gather(bf16[2,128,128]{2,1,0:T(8,128)(2,1)S(1)} %copy-done.9), channel_id=1, replica_groups=mesh['occ'=64,'vir'=8] {'vir'}, dimensions={0}, use_global_device_ids=true | all-gather | bytes 589824 | tf_op jit(solution)/shard_map/all_gather | solution.py:346
  104.0 0.1 broadcast_in_dim.8.row_ref
  104.1 0.0 copy-done
  104.1 0.0 copy-done.2
  104.1 0.0 copy-done.5
  104.1 0.0 copy-done.6
  104.2 4.5 %ladder.1 = (f32[64,64,128]{2,1,0:T(8,128)S(1)}, bf16[16,128,128]{2,1,0:T(8,128)(2,1)S(1)}) custom-call(s32[4,64]{1,0:T(4,128)S(1)} %bitcast.5, f32[400]{0:T(512)S(1)} %copy-done.6, bf16[64,64,128]{2,1,0:T(8,128)(2,1)S(1)} %copy-done, bf16[4,64,64]{2,1,0:T(8,128)(2,1)S(1)} %copy-done.2, bf16[16,128,128]{2,1,0:T(8,128)(2,1)S(1)} %all_gather.7.ld_ref, ...), custom_call_target="tpu_custom_call" | custom-call | tf_op jit(solution)/shard_map/ladder/pallas_call | solution.py:233
  108.7 1.3 copy-done.1
  110.0 19.6 %all-to-all-done.1.ret_ref = bf16[64,128,128]{2,1,0:T(8,128)(2,1)} async-done(((bf16[64,128,128]{2,1,0:T(8,128)(2,1)}), bf16[64,128,128]{2,1,0:T(8,128)(2,1)}, u32[]{:S(2)}, u32[]{:S(2)}) %all-to-all-start.1) | async-done | bytes 2097184 | tf_op jit(solution)/shard_map/all_to_all | solution.py:344
  129.6 3.7 %finish.1 = bf16[64,64,128]{2,1,0:T(8,128)(2,1)} custom-call(s32[4,64]{1,0:T(4,128)S(1)} %bitcast.6, s32[64]{0:T(128)S(1)} %get-tuple-element.10.pos_ref, f32[400]{0:T(512)S(1)} %copy-done.6, f32[4,64,128]{2,1,0:T(8,128)S(1)} %broadcast_in_dim.8.row_ref, f32[16,128]{1,0:T(8,128)S(1)} %bitcast.3, bf16[64,128,128]{2,1,0:T(8,128)(2,1)} %all-to-all-done.1.ret_ref, ...), custom_call_target="tpu_custom_call" | custom-call | tf_op jit(solution)/shard_map/finish/pallas_call | solution.py:300
  (2 shorter events, 0.0 us)
Async XLA Ops:
  2.9 11.0 %copy-start.7 = (bf16[400,128]{1,0:T(8,128)(2,1)S(1)}, bf16[400,128]{1,0:T(8,128)(2,1)}, u32[]{:S(2)}) copy-start(bf16[400,128]{1,0:T(8,128)(2,1)} %param.14) | copy-start | bytes 307204
  2.9 11.0 %copy-start.8 = (bf16[2,128,128]{2,1,0:T(8,128)(2,1)S(1)}, bf16[2,128,128]{2,1,0:T(8,128)(2,1)}, u32[]{:S(2)}) copy-start(bf16[2,128,128]{2,1,0:T(8,128)(2,1)} %param.13) | copy-start | bytes 196612
  2.9 65.0 %copy-start.4 = (bf16[128,128]{1,0:T(8,128)(2,1)S(1)}, bf16[128,128]{1,0:T(8,128)(2,1)}, u32[]{:S(2)}) copy-start(bf16[128,128]{1,0:T(8,128)(2,1)} %core_ref.1) | copy-start | bytes 98308
  3.0 65.0 %all-to-all-start = ((bf16[64,136,128]{2,1,0:T(8,128)(2,1)}), bf16[64,136,128]{2,1,0:T(8,128)(2,1)}, u32[]{:S(2)}, u32[]{:S(2)}) async-start(bf16[64,136,128]{2,1,0:T(8,128)(2,1)} %get-tuple-element.11), calls=%async_computation | async-start | bytes 4456448 | tf_op jit(solution)/shard_map/all_to_all | solution.py:340
  72.6 5.8 %copy-start.3 = (f32[2048]{0:T(1024)S(1)}, f32[2048]{0:T(1024)}, u32[]{:S(2)}) copy-start(f32[2048]{0:T(1024)} %param.17) | copy-start | bytes 24580
  72.6 6.0 %copy-start.9 = (bf16[2,128,128]{2,1,0:T(8,128)(2,1)S(1)}, bf16[2,128,128]{2,1,0:T(8,128)(2,1)}, u32[]{:S(2)}) copy-start(bf16[2,128,128]{2,1,0:T(8,128)(2,1)} %param.12) | copy-start | bytes 196612
  72.6 31.5 %copy-start = (bf16[64,64,128]{2,1,0:T(8,128)(2,1)S(1)}, bf16[64,64,128]{2,1,0:T(8,128)(2,1)}, u32[]{:S(2)}) copy-start(bf16[64,64,128]{2,1,0:T(8,128)(2,1)} %amp_ref.3) | copy-start | bytes 3145732
  72.6 31.5 %copy-start.2 = (bf16[4,64,64]{2,1,0:T(8,128)(2,1)S(1)}, bf16[4,64,64]{2,1,0:T(8,128)(2,1)}, u32[]{:S(2)}) copy-start(bf16[4,64,64]{2,1,0:T(8,128)(2,1)} %lv_ref.1) | copy-start | bytes 98308
  72.6 31.5 %copy-start.5 = (s32[64,4]{0,1:T(4,128)S(1)}, s32[64,4]{0,1:T(4,128)}, u32[]{:S(2)}) copy-start(s32[64,4]{0,1:T(4,128)} %param.10) | copy-start | bytes 3076
  72.6 31.5 %copy-start.6 = (f32[400]{0:T(512)S(1)}, f32[400]{0:T(512)}, u32[]{:S(2)}) copy-start(f32[400]{0:T(512)} %occ_ref.3) | copy-start | bytes 4804
  72.6 56.9 %all-to-all-start.1 = ((bf16[64,128,128]{2,1,0:T(8,128)(2,1)}), bf16[64,128,128]{2,1,0:T(8,128)(2,1)}, u32[]{:S(2)}, u32[]{:S(2)}) async-start(bf16[64,128,128]{2,1,0:T(8,128)(2,1)} %owner_core.1), calls=%async_computation.1 | async-start | bytes 4194304 | tf_op jit(solution)/shard_map/all_to_all | solution.py:344
  108.7 1.3 %copy-start.1 = (f32[64,64,128]{2,1,0:T(8,128)}, f32[64,64,128]{2,1,0:T(8,128)S(1)}, u32[]{:S(2)}) copy-start(f32[64,64,128]{2,1,0:T(8,128)S(1)} %get-tuple-element.14.base_ref) | copy-start | bytes 6291460

commit v6 on v5

--- a/solution.py
+++ b/solution.py
@@ -6,7 +6,7 @@
 from jax.sharding import PartitionSpec as P
 
 CAP = 2
-META = 8
+META = 2
 FIELDS = 4 * CAP
 VMEM_LIMIT = 20 * 2**20
 CHUNKS = 4
@@ -51,6 +51,8 @@
             loads.append(pltpu.make_async_copy(amp_ref.at[piece], amp.at[piece], load_sem.at[j]))
             loads[j].start()
 
+        message = out_ref.reshape(owners, rows + META, domain)
+
         def clear(o, carry):
             count[o] = 0
             return carry
@@ -62,7 +64,7 @@
             rank = count[owner]
             count[owner] = rank + 1
             pos_ref[t] = owner * CAP + rank
-            slot = out_ref.at[owner, pl.ds(pl.multiple_of(rank * width, width), width)]
+            slot = message.at[owner, pl.ds(pl.multiple_of(rank * width, width), width)]
             pltpu.make_async_copy(amp.at[t], slot, tile_sem).start()
             return carry
 
@@ -95,15 +97,15 @@
                 (((1,), (1,)), ((), ())),
                 preferred_element_type=jnp.float32,
             )
-        meta[...] = total.reshape(owners, META, domain).astype(jnp.bfloat16)
-        meta_copy = pltpu.make_async_copy(meta, out_ref.at[:, pl.ds(rows, META)], meta_sem)
+        meta.reshape(owners * META, domain)[...] = total.astype(jnp.bfloat16)
+        meta_copy = pltpu.make_async_copy(meta, out_ref.at[:, pl.ds(rows // META, 1)], meta_sem)
         meta_copy.start()
         meta_copy.wait()
         pltpu.make_async_copy(amp, amp_ref, tile_sem).wait()
 
     return pl.pallas_call(
         kernel,
-        out_shape=(pltpu.HBM((owners, rows + META, domain), jnp.bfloat16), sds((tiles,), jnp.int32)),
+        out_shape=(pltpu.HBM((owners, rows // META + 1, META, domain), jnp.bfloat16), sds((tiles,), jnp.int32)),
         in_specs=[spec(pltpu.HBM), spec(pltpu.HBM)],
         out_specs=(spec(pltpu.HBM), spec(SMEM)),
         scratch_shapes=[
@@ -111,7 +113,7 @@
             SMEM(tile_list.shape, jnp.int32),
             VMEM(tile_list.shape, jnp.int32),
             VMEM((tiles, width, domain), jnp.bfloat16),
-            VMEM((owners, META, domain), jnp.bfloat16),
+            VMEM((owners, 1, META, domain), jnp.bfloat16),
             pltpu.SemaphoreType.DMA((2,)),
             pltpu.SemaphoreType.DMA((CHUNKS,)),
             pltpu.SemaphoreType.DMA,
@@ -123,7 +125,7 @@
 
 
 def owner_core(received, cycle_virtual, cycle_occupied, cycle_core, width, groups):
-    sources, message, domain = received.shape
+    sources, _, _, domain = received.shape
     rank = cycle_core.shape[0]
     rows = CAP * width
 
@@ -132,15 +134,16 @@
     def kernel(
         got_ref, cv_ref, co_ref, core_ref, out_ref, got, meta_b, meta, ids_v, ids, sums, cores, sem, part_sem, out_sem
     ):
-        meta_copy = pltpu.make_async_copy(got_ref.at[:, pl.ds(rows, META)], meta_b, sem)
+        message = got_ref.reshape(sources, rows + META, domain)
+        meta_copy = pltpu.make_async_copy(got_ref.at[:, pl.ds(rows // META, 1)], meta_b, sem)
         meta_copy.start()
         copies = []
         for j in range(PARTS):
             piece = pl.ds(j * part, part)
-            copies.append(pltpu.make_async_copy(got_ref.at[piece, pl.ds(0, rows)], got.at[piece], part_sem.at[j]))
+            copies.append(pltpu.make_async_copy(message.at[piece, pl.ds(0, rows)], got.at[piece], part_sem.at[j]))
             copies[j].start()
         meta_copy.wait()
-        meta[...] = meta_b[...].astype(jnp.float32).reshape(meta.shape)
+        meta[...] = meta_b.reshape(sources * META, domain)[...].astype(jnp.float32)
         turned = meta[pl.ds(0, sources, stride=META), :].T
         ids_v[...] = turned[0:FIELDS].astype(jnp.int32)
         ids_copy = pltpu.make_async_copy(ids_v, ids, sem)
@@ -181,7 +184,7 @@
         out_specs=spec(pltpu.HBM),
         scratch_shapes=[
             VMEM((sources, rows, domain), jnp.bfloat16),
-            VMEM((sources, META, domain), jnp.bfloat16),
+            VMEM((sources, 1, META, domain), jnp.bfloat16),
             VMEM((sources * META, domain), jnp.float32),
             VMEM((FIELDS, sources), jnp.int32),
             SMEM((FIELDS, sources), jnp.int32),

time: 134 us -> 132 us (0.985)
  waiting for transfers between devices: 48.1 us -> 46 us
    all_to_all x1, waiting for transfers between devices: 28.5 us -> 26.4 us  [body(): lax.all_to_all(send, 'occ', split_axis=0, concat_axis=0, tiled=True)]
where the time goes in v6:
time: 132 us; the launch traced here: 131 us
  blocking collectives  50.9 us (39%)
  waiting for transfers between devices  46 us (35%)
  starting transfers between devices  16.7 us (13%)
  Pallas kernels  15.6 us (12%)
  local copies, waits for them, and re-layouts  1.65 us (1%)
    all_to_all x1, waiting for transfers between devices, body(): lax.all_to_all(send, 'occ', split_axis=0, concat_axis=0, tiled=True)  26.4 us
    all_gather x1, blocking collectives, body(): virtual_all = lax.all_gather(cycle_virtual, 'vir', axis=0, tiled=True)  25.5 us
    all_gather x1, blocking collectives, body(): domain_all = lax.all_gather(domain_own, 'vir', axis=0, tiled=True)  25.5 us
    all_to_all x1, waiting for transfers between devices, body(): lax.all_to_all(answers, 'occ', split_axis=0, concat_axis=0, tiled=True)  19.6 us
    all_to_all x1, starting transfers between devices, body(): lax.all_to_all(send, 'occ', split_axis=0, concat_axis=0, tiled=True)  10.9 us
    all_to_all x1, starting transfers between devices, body(): lax.all_to_all(answers, 'occ', split_axis=0, concat_axis=0, tiled=True)  5.74 us
    pallas_call x1, Pallas kernels, owner_core(): pl.pallas_call(kernel, out_shape=pltpu.HBM((sources, rows, rank), jnp.bfl...  4.58 us
    pallas_call x1, Pallas kernels, ladder_part(): pl.pallas_call(kernel, out_shape=(sds(amplitudes.shape, jnp.float32), sds...  4.5 us
  transfers between devices with their start and end apart: 2, of which 2 were waited for; matrix products, arithmetic and copies ran while one was open for 0% of the time, Pallas kernels for 3%

profile of v6, /device:TPU:448, one launch (start us, length us, event | category | flops | bytes accessed | tf_op | source)
XLA Modules:
  0.0 131.0 jit_solution(15428333074960916477)
XLA Ops:
  0.0 2.8 %pack.1 = (bf16[64,65,2,128]{3,2,1,0:T(2,128)(2,1)}, s32[64]{0:T(128)S(1)}) custom-call(s32[4,64]{1,0:T(4,128)} %bitcast.4, bf16[64,64,128]{2,1,0:T(8,128)(2,1)} %amp_ref.3), custom_call_target="tpu_custom_call" | custom-call | tf_op jit(solution)/shard_map/pack/pallas_call | solution.py:106
  2.8 0.0 copy-start.7
  2.8 0.0 copy-start.8
  2.9 0.0 copy-start.4
  2.9 10.9 %all-to-all-start = ((bf16[64,65,2,128]{3,2,1,0:T(2,128)(2,1)}), bf16[64,65,2,128]{3,2,1,0:T(2,128)(2,1)}, u32[]{:S(2)}, u32[]{:S(2)}) async-start(bf16[64,65,2,128]{3,2,1,0:T(2,128)(2,1)} %get-tuple-element.11), calls=%async_computation | async-start | bytes 4259840 | tf_op jit(solution)/shard_map/all_to_all | solution.py:343
  13.8 0.0 copy-done.7
  13.9 0.0 copy-done.8
  13.9 25.5 %all_gather.6.cv_ref = bf16[16,128,128]{2,1,0:T(8,128)(2,1)S(1)} all-gather(bf16[2,128,128]{2,1,0:T(8,128)(2,1)S(1)} %copy-done.8), channel_id=1, replica_groups=mesh['occ'=64,'vir'=8] {'vir'}, dimensions={0}, use_global_device_ids=true | all-gather | bytes 589824 | tf_op jit(solution)/shard_map/all_gather | solution.py:344
  39.3 26.4 %all-to-all-done.got_ref = bf16[64,65,2,128]{3,2,1,0:T(2,128)(2,1)} async-done(((bf16[64,65,2,128]{3,2,1,0:T(2,128)(2,1)}), bf16[64,65,2,128]{3,2,1,0:T(2,128)(2,1)}, u32[]{:S(2)}, u32[]{:S(2)}) %all-to-all-start) | async-done | bytes 2129952 | tf_op jit(solution)/shard_map/all_to_all | solution.py:343
  65.8 0.0 copy-done.4
  65.8 4.6 %owner_core.1 = bf16[64,128,128]{2,1,0:T(8,128)(2,1)} custom-call(bf16[64,65,2,128]{3,2,1,0:T(2,128)(2,1)} %all-to-all-done.got_ref, bf16[16,128,128]{2,1,0:T(8,128)(2,1)S(1)} %all_gather.6.cv_ref, f32[400,128]{1,0:T(8,128)S(1)} %convert_element_type.3.co_ref, bf16[128,128]{1,0:T(8,128)(2,1)S(1)} %copy-done.4), custom_call_target="tpu_custom_call" | custom-call | tf_op jit(solution)/shard_map/owner_core/pallas_call | solution.py:180
  70.3 0.0 copy-start.3
  70.4 0.0 copy-start.9
  70.4 0.0 copy-start
  70.4 0.0 copy-start.2
  70.4 0.0 copy-start.5
  70.4 0.0 copy-start.6
  70.4 5.7 %all-to-all-start.1 = ((bf16[64,128,128]{2,1,0:T(8,128)(2,1)}), bf16[64,128,128]{2,1,0:T(8,128)(2,1)}, u32[]{:S(2)}, u32[]{:S(2)}) async-start(bf16[64,128,128]{2,1,0:T(8,128)(2,1)} %owner_core.1), calls=%async_computation.1 | async-start | bytes 4194304 | tf_op jit(solution)/shard_map/all_to_all | solution.py:347
  76.2 0.0 copy-done.3
  76.2 0.1 dynamic_slice.3
  76.3 0.1 broadcast_in_dim.7
  76.3 0.0 copy-done.9
  76.3 25.5 %all_gather.7.ld_ref = bf16[16,128,128]{2,1,0:T(8,128)(2,1)S(1)} all-gather(bf16[2,128,128]{2,1,0:T(8,128)(2,1)S(1)} %copy-done.9), channel_id=1, replica_groups=mesh['occ'=64,'vir'=8] {'vir'}, dimensions={0}, use_global_device_ids=true | all-gather | bytes 589824 | tf_op jit(solution)/shard_map/all_gather | solution.py:349
  101.8 0.1 broadcast_in_dim.8.row_ref
  101.9 0.0 copy-done
  101.9 0.0 copy-done.2
  101.9 0.0 copy-done.5
  101.9 0.0 copy-done.6
  101.9 4.5 %ladder.1 = (f32[64,64,128]{2,1,0:T(8,128)S(1)}, bf16[16,128,128]{2,1,0:T(8,128)(2,1)S(1)}) custom-call(s32[4,64]{1,0:T(4,128)S(1)} %bitcast.5, f32[400]{0:T(512)S(1)} %copy-done.6, bf16[64,64,128]{2,1,0:T(8,128)(2,1)S(1)} %copy-done, bf16[4,64,64]{2,1,0:T(8,128)(2,1)S(1)} %copy-done.2, bf16[16,128,128]{2,1,0:T(8,128)(2,1)S(1)} %all_gather.7.ld_ref, ...), custom_call_target="tpu_custom_call" | custom-call | tf_op jit(solution)/shard_map/ladder/pallas_call | solution.py:236
  106.4 1.3 %copy-done.1 = f32[64,64,128]{2,1,0:T(8,128)} copy-done((f32[64,64,128]{2,1,0:T(8,128)}, f32[64,64,128]{2,1,0:T(8,128)S(1)}, u32[]{:S(2)}) %copy-start.1) | copy-done | bytes 2097176
  107.8 19.6 %all-to-all-done.1.ret_ref = bf16[64,128,128]{2,1,0:T(8,128)(2,1)} async-done(((bf16[64,128,128]{2,1,0:T(8,128)(2,1)}), bf16[64,128,128]{2,1,0:T(8,128)(2,1)}, u32[]{:S(2)}, u32[]{:S(2)}) %all-to-all-start.1) | async-done | bytes 2097184 | tf_op jit(solution)/shard_map/all_to_all | solution.py:347
  127.4 3.7 %finish.1 = bf16[64,64,128]{2,1,0:T(8,128)(2,1)} custom-call(s32[4,64]{1,0:T(4,128)S(1)} %bitcast.6, s32[64]{0:T(128)S(1)} %get-tuple-element.10.pos_ref, f32[400]{0:T(512)S(1)} %copy-done.6, f32[4,64,128]{2,1,0:T(8,128)S(1)} %broadcast_in_dim.8.row_ref, f32[16,128]{1,0:T(8,128)S(1)} %bitcast.3, bf16[64,128,128]{2,1,0:T(8,128)(2,1)} %all-to-all-done.1.ret_ref, ...), custom_call_target="tpu_custom_call" | custom-call | tf_op jit(solution)/shard_map/finish/pallas_call | solution.py:303
  (2 shorter events, 0.0 us)
Async XLA Ops:
  2.8 11.0 %copy-start.7 = (bf16[400,128]{1,0:T(8,128)(2,1)S(1)}, bf16[400,128]{1,0:T(8,128)(2,1)}, u32[]{:S(2)}) copy-start(bf16[400,128]{1,0:T(8,128)(2,1)} %param.14) | copy-start | bytes 307204
  2.8 11.0 %copy-start.8 = (bf16[2,128,128]{2,1,0:T(8,128)(2,1)S(1)}, bf16[2,128,128]{2,1,0:T(8,128)(2,1)}, u32[]{:S(2)}) copy-start(bf16[2,128,128]{2,1,0:T(8,128)(2,1)} %param.13) | copy-start | bytes 196612
  2.9 62.9 %copy-start.4 = (bf16[128,128]{1,0:T(8,128)(2,1)S(1)}, bf16[128,128]{1,0:T(8,128)(2,1)}, u32[]{:S(2)}) copy-start(bf16[128,128]{1,0:T(8,128)(2,1)} %core_ref.1) | copy-start | bytes 98308
  2.9 62.9 %all-to-all-start = ((bf16[64,65,2,128]{3,2,1,0:T(2,128)(2,1)}), bf16[64,65,2,128]{3,2,1,0:T(2,128)(2,1)}, u32[]{:S(2)}, u32[]{:S(2)}) async-start(bf16[64,65,2,128]{3,2,1,0:T(2,128)(2,1)} %get-tuple-element.11), calls=%async_computation | async-start | bytes 4259840 | tf_op jit(solution)/shard_map/all_to_all | solution.py:343
  70.3 5.8 %copy-start.3 = (f32[2048]{0:T(1024)S(1)}, f32[2048]{0:T(1024)}, u32[]{:S(2)}) copy-start(f32[2048]{0:T(1024)} %param.17) | copy-start | bytes 24580
  70.4 6.0 %copy-start.9 = (bf16[2,128,128]{2,1,0:T(8,128)(2,1)S(1)}, bf16[2,128,128]{2,1,0:T(8,128)(2,1)}, u32[]{:S(2)}) copy-start(bf16[2,128,128]{2,1,0:T(8,128)(2,1)} %param.12) | copy-start | bytes 196612
  70.4 31.5 %copy-start = (bf16[64,64,128]{2,1,0:T(8,128)(2,1)S(1)}, bf16[64,64,128]{2,1,0:T(8,128)(2,1)}, u32[]{:S(2)}) copy-start(bf16[64,64,128]{2,1,0:T(8,128)(2,1)} %amp_ref.3) | copy-start | bytes 3145732
  70.4 31.5 %copy-start.2 = (bf16[4,64,64]{2,1,0:T(8,128)(2,1)S(1)}, bf16[4,64,64]{2,1,0:T(8,128)(2,1)}, u32[]{:S(2)}) copy-start(bf16[4,64,64]{2,1,0:T(8,128)(2,1)} %lv_ref.1) | copy-start | bytes 98308
  70.4 31.5 %copy-start.5 = (s32[64,4]{0,1:T(4,128)S(1)}, s32[64,4]{0,1:T(4,128)}, u32[]{:S(2)}) copy-start(s32[64,4]{0,1:T(4,128)} %param.10) | copy-start | bytes 3076
  70.4 31.5 %copy-start.6 = (f32[400]{0:T(512)S(1)}, f32[400]{0:T(512)}, u32[]{:S(2)}) copy-start(f32[400]{0:T(512)} %occ_ref.3) | copy-start | bytes 4804
  70.4 57.0 %all-to-all-start.1 = ((bf16[64,128,128]{2,1,0:T(8,128)(2,1)}), bf16[64,128,128]{2,1,0:T(8,128)(2,1)}, u32[]{:S(2)}, u32[]{:S(2)}) async-start(bf16[64,128,128]{2,1,0:T(8,128)(2,1)} %owner_core.1), calls=%async_computation.1 | async-start | bytes 4194304 | tf_op jit(solution)/shard_map/all_to_all | solution.py:347
  106.4 1.4 %copy-start.1 = (f32[64,64,128]{2,1,0:T(8,128)}, f32[64,64,128]{2,1,0:T(8,128)S(1)}, u32[]{:S(2)}) copy-start(f32[64,64,128]{2,1,0:T(8,128)S(1)} %get-tuple-element.14.base_ref) | copy-start | bytes 6291460

commit v7 on v6

--- a/solution.py
+++ b/solution.py
@@ -10,7 +10,6 @@
 FIELDS = 4 * CAP
 VMEM_LIMIT = 20 * 2**20
 CHUNKS = 4
-PARTS = 1
 SMEM = pltpu.SMEM
 VMEM = pltpu.VMEM
 
@@ -129,23 +128,10 @@
     rank = cycle_core.shape[0]
     rows = CAP * width
 
-    part = sources // PARTS
-
-    def kernel(
-        got_ref, cv_ref, co_ref, core_ref, out_ref, got, meta_b, meta, ids_v, ids, sums, cores, sem, part_sem, out_sem
-    ):
-        message = got_ref.reshape(sources, rows + META, domain)
-        meta_copy = pltpu.make_async_copy(got_ref.at[:, pl.ds(rows // META, 1)], meta_b, sem)
-        meta_copy.start()
-        copies = []
-        for j in range(PARTS):
-            piece = pl.ds(j * part, part)
-            copies.append(pltpu.make_async_copy(message.at[piece, pl.ds(0, rows)], got.at[piece], part_sem.at[j]))
-            copies[j].start()
-        meta_copy.wait()
-        meta[...] = meta_b.reshape(sources * META, domain)[...].astype(jnp.float32)
-        turned = meta[pl.ds(0, sources, stride=META), :].T
-        ids_v[...] = turned[0:FIELDS].astype(jnp.int32)
+    def kernel(got_ref, cv_ref, co_ref, core_ref, out_ref, meta, ids_v, ids, sums, cores, sem, out_sem):
+        got = got_ref.reshape(sources, rows + META, domain)
+        meta[...] = got_ref[:, rows // META, 0, :].astype(jnp.float32)
+        ids_v[...] = meta[...].T[0:FIELDS].astype(jnp.int32)
         ids_copy = pltpu.make_async_copy(ids_v, ids, sem)
         ids_copy.start()
         sums[...] = jnp.zeros_like(sums)
@@ -161,9 +147,7 @@
                 sums[key] += one * co_ref[pl.ds(k, 1), :]
             return carry
 
-        for j, copy in enumerate(copies):
-            copy.wait()
-            lax.fori_loop(j * part, (j + 1) * part, add, 0, unroll=64)
+        lax.fori_loop(0, sources, add, 0, unroll=64)
         grouped = sums[...].astype(jnp.bfloat16).reshape((groups + 1) * width, rank)
         core = jnp.dot(grouped, core_ref[...], preferred_element_type=jnp.float32)
         cores[...] = core.astype(jnp.bfloat16).reshape(cores.shape)
@@ -180,23 +164,20 @@
     return pl.pallas_call(
         kernel,
         out_shape=pltpu.HBM((sources, rows, rank), jnp.bfloat16),
-        in_specs=[spec(pltpu.HBM)] + [spec()] * 3,
+        in_specs=[spec()] * 4,
         out_specs=spec(pltpu.HBM),
         scratch_shapes=[
-            VMEM((sources, rows, domain), jnp.bfloat16),
-            VMEM((sources, 1, META, domain), jnp.bfloat16),
-            VMEM((sources * META, domain), jnp.float32),
+            VMEM((sources, domain), jnp.float32),
             VMEM((FIELDS, sources), jnp.int32),
             SMEM((FIELDS, sources), jnp.int32),
             VMEM((groups + 1, width, rank), jnp.float32),
             VMEM((groups + 1, width, rank), jnp.bfloat16),
             pltpu.SemaphoreType.DMA,
-            pltpu.SemaphoreType.DMA((PARTS,)),
             pltpu.SemaphoreType.DMA,
         ],
         compiler_params=params(),
         name="owner_core",
-    )(far(received), near(cycle_virtual), near(cycle_occupied), near(cycle_core))
+    )(near(received), near(cycle_virtual), near(cycle_occupied), near(cycle_core))
 
 
 def inverse_at(t, list_ref, occ_ref, row_ref, column_ref):

time: 132 us -> 131 us (level)
  no operation moved by 1% of the time
where the time goes in v7:
time: 131 us; the launch traced here: 130 us
  blocking collectives  50.9 us (39%)
  waiting for transfers between devices  46.1 us (35%)
  starting transfers between devices  16.5 us (13%)
  Pallas kernels  14.9 us (11%)
  local copies, waits for them, and re-layouts  1.64 us (1%)
    all_to_all x1, waiting for transfers between devices, body(): lax.all_to_all(send, 'occ', split_axis=0, concat_axis=0, tiled=True)  26.6 us
    all_gather x1, blocking collectives, body(): virtual_all = lax.all_gather(cycle_virtual, 'vir', axis=0, tiled=True)  25.5 us
    all_gather x1, blocking collectives, body(): domain_all = lax.all_gather(domain_own, 'vir', axis=0, tiled=True)  25.5 us
    all_to_all x1, waiting for transfers between devices, body(): lax.all_to_all(answers, 'occ', split_axis=0, concat_axis=0, tiled=True)  19.6 us
    all_to_all x1, starting transfers between devices, body(): lax.all_to_all(send, 'occ', split_axis=0, concat_axis=0, tiled=True)  10.7 us
    all_to_all x1, starting transfers between devices, body(): lax.all_to_all(answers, 'occ', split_axis=0, concat_axis=0, tiled=True)  5.74 us
    pallas_call x1, Pallas kernels, ladder_part(): pl.pallas_call(kernel, out_shape=(sds(amplitudes.shape, jnp.float32), sds...  4.5 us
    pallas_call x1, Pallas kernels, owner_core(): pl.pallas_call(kernel, out_shape=pltpu.HBM((sources, rows, rank), jnp.bfl...  3.94 us
  transfers between devices with their start and end apart: 2, of which 2 were waited for; matrix products, arithmetic and copies ran while one was open for 0% of the time, Pallas kernels for 3%

profile of v7, /device:TPU:448, one launch (start us, length us, event | category | flops | bytes accessed | tf_op | source)
XLA Modules:
  0.0 130.3 jit_solution(6601269731889295075)
XLA Ops:
  0.0 2.8 %pack.1 = (bf16[64,65,2,128]{3,2,1,0:T(2,128)(2,1)}, s32[64]{0:T(128)S(1)}) custom-call(s32[4,64]{1,0:T(4,128)} %bitcast.4, bf16[64,64,128]{2,1,0:T(8,128)(2,1)} %amp_ref.3), custom_call_target="tpu_custom_call" | custom-call | tf_op jit(solution)/shard_map/pack/pallas_call | solution.py:105
  2.8 0.0 copy-start.7
  2.8 0.0 copy-start.8
  2.8 0.0 copy-start.4
  2.8 10.7 %all-to-all-start = ((bf16[64,65,2,128]{3,2,1,0:T(2,128)(2,1)}), bf16[64,65,2,128]{3,2,1,0:T(2,128)(2,1)S(1)}, u32[]{:S(2)}, u32[]{:S(2)}) async-start(bf16[64,65,2,128]{3,2,1,0:T(2,128)(2,1)} %get-tuple-element.11), calls=%async_computation | async-start | bytes 4259840 | tf_op jit(solution)/shard_map/all_to_all | solution.py:324
  13.6 0.0 copy-done.7
  13.6 0.0 copy-done.8
  13.6 25.5 %all_gather.6.cv_ref = bf16[16,128,128]{2,1,0:T(8,128)(2,1)S(1)} all-gather(bf16[2,128,128]{2,1,0:T(8,128)(2,1)S(1)} %copy-done.8), channel_id=1, replica_groups=mesh['occ'=64,'vir'=8] {'vir'}, dimensions={0}, use_global_device_ids=true | all-gather | bytes 589824 | tf_op jit(solution)/shard_map/all_gather | solution.py:325
  39.1 26.6 %all-to-all-done.got_ref = bf16[64,65,2,128]{3,2,1,0:T(2,128)(2,1)S(1)} async-done(((bf16[64,65,2,128]{3,2,1,0:T(2,128)(2,1)}), bf16[64,65,2,128]{3,2,1,0:T(2,128)(2,1)S(1)}, u32[]{:S(2)}, u32[]{:S(2)}) %all-to-all-start) | async-done | bytes 2129952 | tf_op jit(solution)/shard_map/all_to_all | solution.py:324
  65.6 0.0 copy-done.4
  65.6 3.9 %owner_core.1 = bf16[64,128,128]{2,1,0:T(8,128)(2,1)} custom-call(bf16[64,65,2,128]{3,2,1,0:T(2,128)(2,1)S(1)} %all-to-all-done.got_ref, bf16[16,128,128]{2,1,0:T(8,128)(2,1)S(1)} %all_gather.6.cv_ref, f32[400,128]{1,0:T(8,128)S(1)} %convert_element_type.3.co_ref, bf16[128,128]{1,0:T(8,128)(2,1)S(1)} %copy-done.4), custom_call_target="tpu_custom_call" | custom-call | tf_op jit(solution)/shard_map/owner_core/pallas_call | solution.py:164
  69.6 0.0 copy-start.3
  69.6 0.0 copy-start.9
  69.6 0.0 copy-start
  69.6 0.0 copy-start.2
  69.6 0.0 copy-start.5
  69.6 0.0 copy-start.6
  69.7 5.7 %all-to-all-start.1 = ((bf16[64,128,128]{2,1,0:T(8,128)(2,1)}), bf16[64,128,128]{2,1,0:T(8,128)(2,1)}, u32[]{:S(2)}, u32[]{:S(2)}) async-start(bf16[64,128,128]{2,1,0:T(8,128)(2,1)} %owner_core.1), calls=%async_computation.1 | async-start | bytes 4194304 | tf_op jit(solution)/shard_map/all_to_all | solution.py:328
  75.4 0.0 copy-done.3
  75.4 0.1 dynamic_slice.3
  75.5 0.1 broadcast_in_dim.7
  75.6 0.0 copy-done.9
  75.6 25.5 %all_gather.7.ld_ref = bf16[16,128,128]{2,1,0:T(8,128)(2,1)S(1)} all-gather(bf16[2,128,128]{2,1,0:T(8,128)(2,1)S(1)} %copy-done.9), channel_id=1, replica_groups=mesh['occ'=64,'vir'=8] {'vir'}, dimensions={0}, use_global_device_ids=true | all-gather | bytes 589824 | tf_op jit(solution)/shard_map/all_gather | solution.py:330
  101.0 0.1 broadcast_in_dim.8.row_ref
  101.1 0.0 copy-done
  101.1 0.0 copy-done.2
  101.2 0.0 copy-done.5
  101.2 0.0 copy-done.6
  101.2 4.5 %ladder.1 = (f32[64,64,128]{2,1,0:T(8,128)S(1)}, bf16[16,128,128]{2,1,0:T(8,128)(2,1)S(1)}) custom-call(s32[4,64]{1,0:T(4,128)S(1)} %bitcast.5, f32[400]{0:T(512)S(1)} %copy-done.6, bf16[64,64,128]{2,1,0:T(8,128)(2,1)S(1)} %copy-done, bf16[4,64,64]{2,1,0:T(8,128)(2,1)S(1)} %copy-done.2, bf16[16,128,128]{2,1,0:T(8,128)(2,1)S(1)} %all_gather.7.ld_ref, ...), custom_call_target="tpu_custom_call" | custom-call | tf_op jit(solution)/shard_map/ladder/pallas_call | solution.py:217
  105.7 1.3 %copy-done.1 = f32[64,64,128]{2,1,0:T(8,128)} copy-done((f32[64,64,128]{2,1,0:T(8,128)}, f32[64,64,128]{2,1,0:T(8,128)S(1)}, u32[]{:S(2)}) %copy-start.1) | copy-done | bytes 2097176
  107.0 19.6 %all-to-all-done.1.ret_ref = bf16[64,128,128]{2,1,0:T(8,128)(2,1)} async-done(((bf16[64,128,128]{2,1,0:T(8,128)(2,1)}), bf16[64,128,128]{2,1,0:T(8,128)(2,1)}, u32[]{:S(2)}, u32[]{:S(2)}) %all-to-all-start.1) | async-done | bytes 2097184 | tf_op jit(solution)/shard_map/all_to_all | solution.py:328
  126.6 3.7 %finish.1 = bf16[64,64,128]{2,1,0:T(8,128)(2,1)} custom-call(s32[4,64]{1,0:T(4,128)S(1)} %bitcast.6, s32[64]{0:T(128)S(1)} %get-tuple-element.10.pos_ref, f32[400]{0:T(512)S(1)} %copy-done.6, f32[4,64,128]{2,1,0:T(8,128)S(1)} %broadcast_in_dim.8.row_ref, f32[16,128]{1,0:T(8,128)S(1)} %bitcast.3, bf16[64,128,128]{2,1,0:T(8,128)(2,1)} %all-to-all-done.1.ret_ref, ...), custom_call_target="tpu_custom_call" | custom-call | tf_op jit(solution)/shard_map/finish/pallas_call | solution.py:284
  (2 shorter events, 0.0 us)
Async XLA Ops:
  2.8 10.8 %copy-start.7 = (bf16[400,128]{1,0:T(8,128)(2,1)S(1)}, bf16[400,128]{1,0:T(8,128)(2,1)}, u32[]{:S(2)}) copy-start(bf16[400,128]{1,0:T(8,128)(2,1)} %param.14) | copy-start | bytes 307204
  2.8 10.8 %copy-start.8 = (bf16[2,128,128]{2,1,0:T(8,128)(2,1)S(1)}, bf16[2,128,128]{2,1,0:T(8,128)(2,1)}, u32[]{:S(2)}) copy-start(bf16[2,128,128]{2,1,0:T(8,128)(2,1)} %param.13) | copy-start | bytes 196612
  2.8 62.8 %copy-start.4 = (bf16[128,128]{1,0:T(8,128)(2,1)S(1)}, bf16[128,128]{1,0:T(8,128)(2,1)}, u32[]{:S(2)}) copy-start(bf16[128,128]{1,0:T(8,128)(2,1)} %core_ref.1) | copy-start | bytes 98308
  2.8 62.8 %all-to-all-start = ((bf16[64,65,2,128]{3,2,1,0:T(2,128)(2,1)}), bf16[64,65,2,128]{3,2,1,0:T(2,128)(2,1)S(1)}, u32[]{:S(2)}, u32[]{:S(2)}) async-start(bf16[64,65,2,128]{3,2,1,0:T(2,128)(2,1)} %get-tuple-element.11), calls=%async_computation | async-start | bytes 4259840 | tf_op jit(solution)/shard_map/all_to_all | solution.py:324
  69.6 5.8 %copy-start.3 = (f32[2048]{0:T(1024)S(1)}, f32[2048]{0:T(1024)}, u32[]{:S(2)}) copy-start(f32[2048]{0:T(1024)} %param.17) | copy-start | bytes 24580
  69.6 6.0 %copy-start.9 = (bf16[2,128,128]{2,1,0:T(8,128)(2,1)S(1)}, bf16[2,128,128]{2,1,0:T(8,128)(2,1)}, u32[]{:S(2)}) copy-start(bf16[2,128,128]{2,1,0:T(8,128)(2,1)} %param.12) | copy-start | bytes 196612
  69.6 31.5 %copy-start = (bf16[64,64,128]{2,1,0:T(8,128)(2,1)S(1)}, bf16[64,64,128]{2,1,0:T(8,128)(2,1)}, u32[]{:S(2)}) copy-start(bf16[64,64,128]{2,1,0:T(8,128)(2,1)} %amp_ref.3) | copy-start | bytes 3145732
  69.6 31.5 %copy-start.2 = (bf16[4,64,64]{2,1,0:T(8,128)(2,1)S(1)}, bf16[4,64,64]{2,1,0:T(8,128)(2,1)}, u32[]{:S(2)}) copy-start(bf16[4,64,64]{2,1,0:T(8,128)(2,1)} %lv_ref.1) | copy-start | bytes 98308
  69.6 31.5 %copy-start.5 = (s32[64,4]{0,1:T(4,128)S(1)}, s32[64,4]{0,1:T(4,128)}, u32[]{:S(2)}) copy-start(s32[64,4]{0,1:T(4,128)} %param.10) | copy-start | bytes 3076
  69.6 31.5 %copy-start.6 = (f32[400]{0:T(512)S(1)}, f32[400]{0:T(512)}, u32[]{:S(2)}) copy-start(f32[400]{0:T(512)} %occ_ref.3) | copy-start | bytes 4804
  69.7 56.9 %all-to-all-start.1 = ((bf16[64,128,128]{2,1,0:T(8,128)(2,1)}), bf16[64,128,128]{2,1,0:T(8,128)(2,1)}, u32[]{:S(2)}, u32[]{:S(2)}) async-start(bf16[64,128,128]{2,1,0:T(8,128)(2,1)} %owner_core.1), calls=%async_computation.1 | async-start | bytes 4194304 | tf_op jit(solution)/shard_map/all_to_all | solution.py:328
  105.7 1.3 %copy-start.1 = (f32[64,64,128]{2,1,0:T(8,128)}, f32[64,64,128]{2,1,0:T(8,128)S(1)}, u32[]{:S(2)}) copy-start(f32[64,64,128]{2,1,0:T(8,128)S(1)} %get-tuple-element.14.base_ref) | copy-start | bytes 6291460

commit v8 on v7

--- a/solution.py
+++ b/solution.py
@@ -241,7 +241,6 @@
         co_ref,
         base_ref,
         out_ref,
-        core,
         base,
         out,
         sem,
@@ -253,28 +252,19 @@
             loads.append(pltpu.make_async_copy(base_ref.at[piece], base.at[piece], sem.at[j, 0]))
             stores.append(pltpu.make_async_copy(out.at[piece], out_ref.at[piece], out_sem.at[j]))
 
-        for j, (low, high) in enumerate(pieces):
-
-            def fetch(t, carry):
-                slot = pos_ref[t]
-                row = pl.multiple_of(lax.rem(slot, CAP) * width, width)
-                tile = ret_ref.at[lax.div(slot, CAP), pl.ds(row, width)]
-                pltpu.make_async_copy(tile, core.at[t], sem.at[j, 1]).start()
-                return carry
-
-            loads[j].start()
-            lax.fori_loop(low, high, fetch, 0, unroll=8)
+        for load in loads:
+            load.start()
 
         def one(t, carry):
-            scaled = core[t].astype(jnp.float32) * co_ref[pl.ds(list_ref[1, t], 1), :]
+            slot = pos_ref[t]
+            row = pl.multiple_of(lax.rem(slot, CAP) * width, width)
+            scaled = ret_ref[lax.div(slot, CAP), pl.ds(row, width), :].astype(jnp.float32) * co_ref[pl.ds(list_ref[1, t], 1), :]
             term = jnp.dot(scaled.astype(jnp.bfloat16), cv_ref[list_ref[3, t]], preferred_element_type=jnp.float32)
             inverse = inverse_at(t, list_ref, occ_ref, row_ref, column_ref)
             out[t] = (base[t] + term * inverse).astype(jnp.bfloat16)
             return carry
 
         for j, (low, high) in enumerate(pieces):
-            piece = pl.ds(low, high - low)
-            pltpu.make_async_copy(core.at[piece], core.at[piece], sem.at[j, 1]).wait()
             loads[j].wait()
             lax.fori_loop(low, high, one, 0, unroll=high - low)
             stores[j].start()
@@ -284,10 +274,9 @@
     return pl.pallas_call(
         kernel,
         out_shape=sds(base.shape, jnp.bfloat16),
-        in_specs=[spec(SMEM)] * 3 + [spec()] * 2 + [spec(pltpu.HBM)] + [spec()] * 2 + [spec(pltpu.HBM)],
+        in_specs=[spec(SMEM)] * 3 + [spec()] * 5 + [spec(pltpu.HBM)],
         out_specs=spec(pltpu.HBM),
         scratch_shapes=[
-            VMEM((tiles, width, domain), jnp.bfloat16),
             VMEM((tiles, width, domain), jnp.float32),
             VMEM((tiles, width, domain), jnp.bfloat16),
             pltpu.SemaphoreType.DMA((len(pieces), 2)),
@@ -295,7 +284,7 @@
         ],
         compiler_params=params(),
         name="finish",
-    )(tile_list, position, *energies, far(returned), cycle_turned, cycle_occupied, far(base))
+    )(tile_list, position, *energies, near(returned), cycle_turned, cycle_occupied, far(base))
 
 
 def body(

time: 131 us -> 131 us (level)
  local copies, waits for them, and re-layouts: 1.64 us -> 3.66 us
  waiting for transfers between devices: 46.1 us -> 44.3 us
    unnamed x20, local copies, waits for them, and re-layouts: 1.39 us -> 3.41 us
    all_to_all x1, waiting for transfers between devices: 19.6 us -> 17.7 us  [body(): lax.all_to_all(answers, 'occ', split_axis=0, concat_axis=0, tiled=True)]
where the time goes in v8:
time: 131 us; the launch traced here: 130 us
  blocking collectives  50.9 us (39%)
  waiting for transfers between devices  44.3 us (34%)
  starting transfers between devices  16.2 us (12%)
  Pallas kernels  14.8 us (11%)
  local copies, waits for them, and re-layouts  3.66 us (3%)
    all_to_all x1, waiting for transfers between devices, body(): lax.all_to_all(send, 'occ', split_axis=0, concat_axis=0, tiled=True)  26.6 us
    all_gather x1, blocking collectives, body(): virtual_all = lax.all_gather(cycle_virtual, 'vir', axis=0, tiled=True)  25.5 us
    all_gather x1, blocking collectives, body(): domain_all = lax.all_gather(domain_own, 'vir', axis=0, tiled=True)  25.5 us
    all_to_all x1, waiting for transfers between devices, body(): lax.all_to_all(answers, 'occ', split_axis=0, concat_axis=0, tiled=True)  17.7 us
    all_to_all x1, starting transfers between devices, body(): lax.all_to_all(send, 'occ', split_axis=0, concat_axis=0, tiled=True)  10.7 us
    all_to_all x1, starting transfers between devices, body(): lax.all_to_all(answers, 'occ', split_axis=0, concat_axis=0, tiled=True)  5.5 us
    pallas_call x1, Pallas kernels, ladder_part(): pl.pallas_call(kernel, out_shape=(sds(amplitudes.shape, jnp.float32), sds...  4.5 us
    pallas_call x1, Pallas kernels, owner_core(): pl.pallas_call(kernel, out_shape=pltpu.HBM((sources, rows, rank), jnp.bfl...  3.94 us
  transfers between devices with their start and end apart: 2, of which 2 were waited for; matrix products, arithmetic and copies ran while one was open for 0% of the time, Pallas kernels for 3%

profile of v8, /device:TPU:448, one launch (start us, length us, event | category | flops | bytes accessed | tf_op | source)
XLA Modules:
  0.0 130.1 jit_solution(2695329439269761173)
XLA Ops:
  0.0 2.8 %pack.1 = (bf16[64,65,2,128]{3,2,1,0:T(2,128)(2,1)}, s32[64]{0:T(128)S(1)}) custom-call(s32[4,64]{1,0:T(4,128)} %bitcast.4, bf16[64,64,128]{2,1,0:T(8,128)(2,1)} %amp_ref.3), custom_call_target="tpu_custom_call" | custom-call | tf_op jit(solution)/shard_map/pack/pallas_call | solution.py:105
  2.8 0.0 copy-start.7
  2.8 0.0 copy-start.8
  2.8 0.0 copy-start.4
  2.8 10.7 %all-to-all-start = ((bf16[64,65,2,128]{3,2,1,0:T(2,128)(2,1)}), bf16[64,65,2,128]{3,2,1,0:T(2,128)(2,1)S(1)}, u32[]{:S(2)}, u32[]{:S(2)}) async-start(bf16[64,65,2,128]{3,2,1,0:T(2,128)(2,1)} %get-tuple-element.11), calls=%async_computation | async-start | bytes 4259840 | tf_op jit(solution)/shard_map/all_to_all | solution.py:313
  13.6 0.0 copy-done.7
  13.6 0.0 copy-done.8
  13.6 25.5 %all_gather.6.cv_ref = bf16[16,128,128]{2,1,0:T(8,128)(2,1)S(1)} all-gather(bf16[2,128,128]{2,1,0:T(8,128)(2,1)S(1)} %copy-done.8), channel_id=1, replica_groups=mesh['occ'=64,'vir'=8] {'vir'}, dimensions={0}, use_global_device_ids=true | all-gather | bytes 589824 | tf_op jit(solution)/shard_map/all_gather | solution.py:314
  39.1 26.6 %all-to-all-done.got_ref = bf16[64,65,2,128]{3,2,1,0:T(2,128)(2,1)S(1)} async-done(((bf16[64,65,2,128]{3,2,1,0:T(2,128)(2,1)}), bf16[64,65,2,128]{3,2,1,0:T(2,128)(2,1)S(1)}, u32[]{:S(2)}, u32[]{:S(2)}) %all-to-all-start) | async-done | bytes 2129952 | tf_op jit(solution)/shard_map/all_to_all | solution.py:313
  65.6 0.0 copy-done.4
  65.6 3.9 %owner_core.1 = bf16[64,128,128]{2,1,0:T(8,128)(2,1)} custom-call(bf16[64,65,2,128]{3,2,1,0:T(2,128)(2,1)S(1)} %all-to-all-done.got_ref, bf16[16,128,128]{2,1,0:T(8,128)(2,1)S(1)} %all_gather.6.cv_ref, f32[400,128]{1,0:T(8,128)S(1)} %convert_element_type.3.co_ref, bf16[128,128]{1,0:T(8,128)(2,1)S(1)} %copy-done.4), custom_call_target="tpu_custom_call" | custom-call | tf_op jit(solution)/shard_map/owner_core/pallas_call | solution.py:164
  69.6 0.0 copy-start.3
  69.6 0.0 copy-start.9
  69.6 0.0 copy-start.5
  69.6 0.0 copy-start.6
  69.6 5.5 %all-to-all-start.1 = ((bf16[64,128,128]{2,1,0:T(8,128)(2,1)}), bf16[64,128,128]{2,1,0:T(8,128)(2,1)S(1)}, u32[]{:S(2)}, u32[]{:S(2)}) async-start(bf16[64,128,128]{2,1,0:T(8,128)(2,1)} %owner_core.1), calls=%async_computation.1 | async-start | bytes 4194304 | tf_op jit(solution)/shard_map/all_to_all | solution.py:317
  75.1 0.0 copy-done.3
  75.1 0.1 dynamic_slice.3
  75.2 0.1 broadcast_in_dim.7
  75.3 0.0 copy-done.9
  75.3 25.5 %all_gather.7.ld_ref = bf16[16,128,128]{2,1,0:T(8,128)(2,1)S(1)} all-gather(bf16[2,128,128]{2,1,0:T(8,128)(2,1)S(1)} %copy-done.9), channel_id=1, replica_groups=mesh['occ'=64,'vir'=8] {'vir'}, dimensions={0}, use_global_device_ids=true | all-gather | bytes 589824 | tf_op jit(solution)/shard_map/all_gather | solution.py:319
  100.8 0.1 broadcast_in_dim.8.row_ref
  100.9 0.0 copy-done.5
  100.9 0.0 copy-done.6
  100.9 0.0 copy-start
  100.9 1.2 copy-done
  102.1 0.8 copy-done.2
  102.9 4.5 %ladder.1 = (f32[64,64,128]{2,1,0:T(8,128)S(1)}, bf16[16,128,128]{2,1,0:T(8,128)(2,1)S(1)}) custom-call(s32[4,64]{1,0:T(4,128)S(1)} %bitcast.5, f32[400]{0:T(512)S(1)} %copy-done.6, bf16[64,64,128]{2,1,0:T(8,128)(2,1)S(1)} %copy-done, bf16[4,64,64]{2,1,0:T(8,128)(2,1)S(1)} %copy-done.2, bf16[16,128,128]{2,1,0:T(8,128)(2,1)S(1)} %all_gather.7.ld_ref, ...), custom_call_target="tpu_custom_call" | custom-call | tf_op jit(solution)/shard_map/ladder/pallas_call | solution.py:217
  107.5 0.0 copy-start.1
  107.5 1.3 %copy-done.1 = f32[64,64,128]{2,1,0:T(8,128)} copy-done((f32[64,64,128]{2,1,0:T(8,128)}, f32[64,64,128]{2,1,0:T(8,128)S(1)}, u32[]{:S(2)}) %copy-start.1) | copy-done | bytes 2097176
  108.8 17.7 %all-to-all-done.1.ret_ref = bf16[64,128,128]{2,1,0:T(8,128)(2,1)S(1)} async-done(((bf16[64,128,128]{2,1,0:T(8,128)(2,1)}), bf16[64,128,128]{2,1,0:T(8,128)(2,1)S(1)}, u32[]{:S(2)}, u32[]{:S(2)}) %all-to-all-start.1) | async-done | bytes 2097184 | tf_op jit(solution)/shard_map/all_to_all | solution.py:317
  126.5 3.6 %finish.1 = bf16[64,64,128]{2,1,0:T(8,128)(2,1)} custom-call(s32[4,64]{1,0:T(4,128)S(1)} %bitcast.6, s32[64]{0:T(128)S(1)} %get-tuple-element.10.pos_ref, f32[400]{0:T(512)S(1)} %copy-done.6, f32[4,64,128]{2,1,0:T(8,128)S(1)} %broadcast_in_dim.8.row_ref, f32[16,128]{1,0:T(8,128)S(1)} %bitcast.3, bf16[64,128,128]{2,1,0:T(8,128)(2,1)S(1)} %all-to-all-done.1.ret_ref, ...), custom_call_target="tpu_custom_call" | custom-call | tf_op jit(solution)/shard_map/finish/pallas_call | solution.py:274
  (2 shorter events, 0.0 us)
Async XLA Ops:
  2.8 10.8 %copy-start.7 = (bf16[400,128]{1,0:T(8,128)(2,1)S(1)}, bf16[400,128]{1,0:T(8,128)(2,1)}, u32[]{:S(2)}) copy-start(bf16[400,128]{1,0:T(8,128)(2,1)} %param.14) | copy-start | bytes 307204
  2.8 10.8 %copy-start.8 = (bf16[2,128,128]{2,1,0:T(8,128)(2,1)S(1)}, bf16[2,128,128]{2,1,0:T(8,128)(2,1)}, u32[]{:S(2)}) copy-start(bf16[2,128,128]{2,1,0:T(8,128)(2,1)} %param.13) | copy-start | bytes 196612
  2.8 62.8 %copy-start.4 = (bf16[128,128]{1,0:T(8,128)(2,1)S(1)}, bf16[128,128]{1,0:T(8,128)(2,1)}, u32[]{:S(2)}) copy-start(bf16[128,128]{1,0:T(8,128)(2,1)} %core_ref.1) | copy-start | bytes 98308
  2.8 62.8 %all-to-all-start = ((bf16[64,65,2,128]{3,2,1,0:T(2,128)(2,1)}), bf16[64,65,2,128]{3,2,1,0:T(2,128)(2,1)S(1)}, u32[]{:S(2)}, u32[]{:S(2)}) async-start(bf16[64,65,2,128]{3,2,1,0:T(2,128)(2,1)} %get-tuple-element.11), calls=%async_computation | async-start | bytes 4259840 | tf_op jit(solution)/shard_map/all_to_all | solution.py:313
  69.6 5.6 %copy-start.3 = (f32[2048]{0:T(1024)S(1)}, f32[2048]{0:T(1024)}, u32[]{:S(2)}) copy-start(f32[2048]{0:T(1024)} %param.17) | copy-start | bytes 24580
  69.6 5.7 %copy-start.9 = (bf16[2,128,128]{2,1,0:T(8,128)(2,1)S(1)}, bf16[2,128,128]{2,1,0:T(8,128)(2,1)}, u32[]{:S(2)}) copy-start(bf16[2,128,128]{2,1,0:T(8,128)(2,1)} %param.12) | copy-start | bytes 196612
  69.6 31.3 %copy-start.5 = (s32[64,4]{0,1:T(4,128)S(1)}, s32[64,4]{0,1:T(4,128)}, u32[]{:S(2)}) copy-start(s32[64,4]{0,1:T(4,128)} %param.10) | copy-start | bytes 3076
  69.6 31.3 %copy-start.6 = (f32[400]{0:T(512)S(1)}, f32[400]{0:T(512)}, u32[]{:S(2)}) copy-start(f32[400]{0:T(512)} %occ_ref.3) | copy-start | bytes 4804
  69.6 56.9 %all-to-all-start.1 = ((bf16[64,128,128]{2,1,0:T(8,128)(2,1)}), bf16[64,128,128]{2,1,0:T(8,128)(2,1)S(1)}, u32[]{:S(2)}, u32[]{:S(2)}) async-start(bf16[64,128,128]{2,1,0:T(8,128)(2,1)} %owner_core.1), calls=%async_computation.1 | async-start | bytes 4194304 | tf_op jit(solution)/shard_map/all_to_all | solution.py:317
  100.9 1.2 copy-start
  102.1 0.8 copy-start.2
  107.5 1.3 %copy-start.1 = (f32[64,64,128]{2,1,0:T(8,128)}, f32[64,64,128]{2,1,0:T(8,128)S(1)}, u32[]{:S(2)}) copy-start(f32[64,64,128]{2,1,0:T(8,128)S(1)} %get-tuple-element.14.base_ref) | copy-start | bytes 6291460

commit v9 on v8

--- a/solution.py
+++ b/solution.py
@@ -227,7 +227,7 @@
 
 def finish(tile_list, position, returned, cycle_turned, cycle_occupied, base, energies):
     tiles, width, domain = base.shape
-    bounds = [tiles * j // CHUNKS for j in range(CHUNKS + 1)]
+    bounds = [0, tiles // 2, tiles]
     pieces = list(zip(bounds[:-1], bounds[1:]))
 
     def kernel(

time: 131 us -> 131 us (level)
  no operation moved by 1% of the time
where the time goes in v9:
time: 131 us; the launch traced here: 130 us
  blocking collectives  50.9 us (39%)
  waiting for transfers between devices  44.3 us (34%)
  starting transfers between devices  16.2 us (12%)
  Pallas kernels  14.9 us (11%)
  local copies, waits for them, and re-layouts  3.66 us (3%)
    all_to_all x1, waiting for transfers between devices, body(): lax.all_to_all(send, 'occ', split_axis=0, concat_axis=0, tiled=True)  26.6 us
    all_gather x1, blocking collectives, body(): virtual_all = lax.all_gather(cycle_virtual, 'vir', axis=0, tiled=True)  25.5 us
    all_gather x1, blocking collectives, body(): domain_all = lax.all_gather(domain_own, 'vir', axis=0, tiled=True)  25.5 us
    all_to_all x1, waiting for transfers between devices, body(): lax.all_to_all(answers, 'occ', split_axis=0, concat_axis=0, tiled=True)  17.7 us
    all_to_all x1, starting transfers between devices, body(): lax.all_to_all(send, 'occ', split_axis=0, concat_axis=0, tiled=True)  10.7 us
    all_to_all x1, starting transfers between devices, body(): lax.all_to_all(answers, 'occ', split_axis=0, concat_axis=0, tiled=True)  5.47 us
    pallas_call x1, Pallas kernels, ladder_part(): pl.pallas_call(kernel, out_shape=(sds(amplitudes.shape, jnp.float32), sds...  4.5 us
    pallas_call x1, Pallas kernels, owner_core(): pl.pallas_call(kernel, out_shape=pltpu.HBM((sources, rows, rank), jnp.bfl...  3.96 us
  transfers between devices with their start and end apart: 2, of which 2 were waited for; matrix products, arithmetic and copies ran while one was open for 0% of the time, Pallas kernels for 3%

profile of v9, /device:TPU:448, one launch (start us, length us, event | category | flops | bytes accessed | tf_op | source)
XLA Modules:
  0.0 130.1 jit_solution(11578194846593935272)
XLA Ops:
  0.0 2.8 %pack.1 = (bf16[64,65,2,128]{3,2,1,0:T(2,128)(2,1)}, s32[64]{0:T(128)S(1)}) custom-call(s32[4,64]{1,0:T(4,128)} %bitcast.4, bf16[64,64,128]{2,1,0:T(8,128)(2,1)} %amp_ref.3), custom_call_target="tpu_custom_call" | custom-call | tf_op jit(solution)/shard_map/pack/pallas_call | solution.py:105
  2.8 0.0 copy-start.7
  2.8 0.0 copy-start.8
  2.8 0.0 copy-start.4
  2.8 10.7 %all-to-all-start = ((bf16[64,65,2,128]{3,2,1,0:T(2,128)(2,1)}), bf16[64,65,2,128]{3,2,1,0:T(2,128)(2,1)S(1)}, u32[]{:S(2)}, u32[]{:S(2)}) async-start(bf16[64,65,2,128]{3,2,1,0:T(2,128)(2,1)} %get-tuple-element.11), calls=%async_computation | async-start | bytes 4259840 | tf_op jit(solution)/shard_map/all_to_all | solution.py:313
  13.6 0.0 copy-done.7
  13.6 0.0 copy-done.8
  13.6 25.5 %all_gather.6.cv_ref = bf16[16,128,128]{2,1,0:T(8,128)(2,1)S(1)} all-gather(bf16[2,128,128]{2,1,0:T(8,128)(2,1)S(1)} %copy-done.8), channel_id=1, replica_groups=mesh['occ'=64,'vir'=8] {'vir'}, dimensions={0}, use_global_device_ids=true | all-gather | bytes 589824 | tf_op jit(solution)/shard_map/all_gather | solution.py:314
  39.1 26.6 %all-to-all-done.got_ref = bf16[64,65,2,128]{3,2,1,0:T(2,128)(2,1)S(1)} async-done(((bf16[64,65,2,128]{3,2,1,0:T(2,128)(2,1)}), bf16[64,65,2,128]{3,2,1,0:T(2,128)(2,1)S(1)}, u32[]{:S(2)}, u32[]{:S(2)}) %all-to-all-start) | async-done | bytes 2129952 | tf_op jit(solution)/shard_map/all_to_all | solution.py:313
  65.6 0.0 copy-done.4
  65.6 4.0 %owner_core.1 = bf16[64,128,128]{2,1,0:T(8,128)(2,1)} custom-call(bf16[64,65,2,128]{3,2,1,0:T(2,128)(2,1)S(1)} %all-to-all-done.got_ref, bf16[16,128,128]{2,1,0:T(8,128)(2,1)S(1)} %all_gather.6.cv_ref, f32[400,128]{1,0:T(8,128)S(1)} %convert_element_type.3.co_ref, bf16[128,128]{1,0:T(8,128)(2,1)S(1)} %copy-done.4), custom_call_target="tpu_custom_call" | custom-call | tf_op jit(solution)/shard_map/owner_core/pallas_call | solution.py:164
  69.6 0.0 copy-start.3
  69.6 0.0 copy-start.9
  69.6 0.0 copy-start.5
  69.6 0.0 copy-start.6
  69.6 5.5 %all-to-all-start.1 = ((bf16[64,128,128]{2,1,0:T(8,128)(2,1)}), bf16[64,128,128]{2,1,0:T(8,128)(2,1)S(1)}, u32[]{:S(2)}, u32[]{:S(2)}) async-start(bf16[64,128,128]{2,1,0:T(8,128)(2,1)} %owner_core.1), calls=%async_computation.1 | async-start | bytes 4194304 | tf_op jit(solution)/shard_map/all_to_all | solution.py:317
  75.1 0.0 copy-done.3
  75.1 0.1 dynamic_slice.3
  75.2 0.1 broadcast_in_dim.7
  75.3 0.0 copy-done.9
  75.3 25.5 %all_gather.7.ld_ref = bf16[16,128,128]{2,1,0:T(8,128)(2,1)S(1)} all-gather(bf16[2,128,128]{2,1,0:T(8,128)(2,1)S(1)} %copy-done.9), channel_id=1, replica_groups=mesh['occ'=64,'vir'=8] {'vir'}, dimensions={0}, use_global_device_ids=true | all-gather | bytes 589824 | tf_op jit(solution)/shard_map/all_gather | solution.py:319
  100.8 0.1 broadcast_in_dim.8.row_ref
  100.9 0.0 copy-done.5
  100.9 0.0 copy-done.6
  100.9 0.0 copy-start
  100.9 1.2 copy-done
  102.1 0.8 copy-done.2
  102.9 4.5 %ladder.1 = (f32[64,64,128]{2,1,0:T(8,128)S(1)}, bf16[16,128,128]{2,1,0:T(8,128)(2,1)S(1)}) custom-call(s32[4,64]{1,0:T(4,128)S(1)} %bitcast.5, f32[400]{0:T(512)S(1)} %copy-done.6, bf16[64,64,128]{2,1,0:T(8,128)(2,1)S(1)} %copy-done, bf16[4,64,64]{2,1,0:T(8,128)(2,1)S(1)} %copy-done.2, bf16[16,128,128]{2,1,0:T(8,128)(2,1)S(1)} %all_gather.7.ld_ref, ...), custom_call_target="tpu_custom_call" | custom-call | tf_op jit(solution)/shard_map/ladder/pallas_call | solution.py:217
  107.4 0.0 copy-start.1
  107.5 1.3 %copy-done.1 = f32[64,64,128]{2,1,0:T(8,128)} copy-done((f32[64,64,128]{2,1,0:T(8,128)}, f32[64,64,128]{2,1,0:T(8,128)S(1)}, u32[]{:S(2)}) %copy-start.1) | copy-done | bytes 2097176
  108.8 17.7 %all-to-all-done.1.ret_ref = bf16[64,128,128]{2,1,0:T(8,128)(2,1)S(1)} async-done(((bf16[64,128,128]{2,1,0:T(8,128)(2,1)}), bf16[64,128,128]{2,1,0:T(8,128)(2,1)S(1)}, u32[]{:S(2)}, u32[]{:S(2)}) %all-to-all-start.1) | async-done | bytes 2097184 | tf_op jit(solution)/shard_map/all_to_all | solution.py:317
  126.5 3.6 %finish.1 = bf16[64,64,128]{2,1,0:T(8,128)(2,1)} custom-call(s32[4,64]{1,0:T(4,128)S(1)} %bitcast.6, s32[64]{0:T(128)S(1)} %get-tuple-element.10.pos_ref, f32[400]{0:T(512)S(1)} %copy-done.6, f32[4,64,128]{2,1,0:T(8,128)S(1)} %broadcast_in_dim.8.row_ref, f32[16,128]{1,0:T(8,128)S(1)} %bitcast.3, bf16[64,128,128]{2,1,0:T(8,128)(2,1)S(1)} %all-to-all-done.1.ret_ref, ...), custom_call_target="tpu_custom_call" | custom-call | tf_op jit(solution)/shard_map/finish/pallas_call | solution.py:274
  (2 shorter events, 0.0 us)
Async XLA Ops:
  2.8 10.8 %copy-start.7 = (bf16[400,128]{1,0:T(8,128)(2,1)S(1)}, bf16[400,128]{1,0:T(8,128)(2,1)}, u32[]{:S(2)}) copy-start(bf16[400,128]{1,0:T(8,128)(2,1)} %param.14) | copy-start | bytes 307204
  2.8 10.8 %copy-start.8 = (bf16[2,128,128]{2,1,0:T(8,128)(2,1)S(1)}, bf16[2,128,128]{2,1,0:T(8,128)(2,1)}, u32[]{:S(2)}) copy-start(bf16[2,128,128]{2,1,0:T(8,128)(2,1)} %param.13) | copy-start | bytes 196612
  2.8 62.8 %copy-start.4 = (bf16[128,128]{1,0:T(8,128)(2,1)S(1)}, bf16[128,128]{1,0:T(8,128)(2,1)}, u32[]{:S(2)}) copy-start(bf16[128,128]{1,0:T(8,128)(2,1)} %core_ref.1) | copy-start | bytes 98308
  2.8 62.8 %all-to-all-start = ((bf16[64,65,2,128]{3,2,1,0:T(2,128)(2,1)}), bf16[64,65,2,128]{3,2,1,0:T(2,128)(2,1)S(1)}, u32[]{:S(2)}, u32[]{:S(2)}) async-start(bf16[64,65,2,128]{3,2,1,0:T(2,128)(2,1)} %get-tuple-element.11), calls=%async_computation | async-start | bytes 4259840 | tf_op jit(solution)/shard_map/all_to_all | solution.py:313
  69.6 5.5 %copy-start.3 = (f32[2048]{0:T(1024)S(1)}, f32[2048]{0:T(1024)}, u32[]{:S(2)}) copy-start(f32[2048]{0:T(1024)} %param.17) | copy-start | bytes 24580
  69.6 5.7 %copy-start.9 = (bf16[2,128,128]{2,1,0:T(8,128)(2,1)S(1)}, bf16[2,128,128]{2,1,0:T(8,128)(2,1)}, u32[]{:S(2)}) copy-start(bf16[2,128,128]{2,1,0:T(8,128)(2,1)} %param.12) | copy-start | bytes 196612
  69.6 31.2 %copy-start.5 = (s32[64,4]{0,1:T(4,128)S(1)}, s32[64,4]{0,1:T(4,128)}, u32[]{:S(2)}) copy-start(s32[64,4]{0,1:T(4,128)} %param.10) | copy-start | bytes 3076
  69.6 31.2 %copy-start.6 = (f32[400]{0:T(512)S(1)}, f32[400]{0:T(512)}, u32[]{:S(2)}) copy-start(f32[400]{0:T(512)} %occ_ref.3) | copy-start | bytes 4804
  69.6 56.8 %all-to-all-start.1 = ((bf16[64,128,128]{2,1,0:T(8,128)(2,1)}), bf16[64,128,128]{2,1,0:T(8,128)(2,1)S(1)}, u32[]{:S(2)}, u32[]{:S(2)}) async-start(bf16[64,128,128]{2,1,0:T(8,128)(2,1)} %owner_core.1), calls=%async_computation.1 | async-start | bytes 4194304 | tf_op jit(solution)/shard_map/all_to_all | solution.py:317
  100.9 1.2 copy-start
  102.1 0.8 copy-start.2
  107.4 1.3 %copy-start.1 = (f32[64,64,128]{2,1,0:T(8,128)}, f32[64,64,128]{2,1,0:T(8,128)S(1)}, u32[]{:S(2)}) copy-start(f32[64,64,128]{2,1,0:T(8,128)S(1)} %get-tuple-element.14.base_ref) | copy-start | bytes 6291460
